TPU v7x, 32 devices: a whole 2x2x4 slice. The times are simulated.
32 devices in a mesh: ctx: 8 (over z, y), grp: 4 (over x, core).
Axes of the slice: x: 2, y: 2, z: 4, core: 2. Of those that a mesh axis runs over, the one named last changes fastest.
Arguments:
- query_gate: bfloat16 [1024, 4096], P('ctx', 'grp'), may hold values from -6 to 6
- key_gate: bfloat16 [1024, 4096], P('ctx', 'grp'), may hold values from -6 to 6
- values: bfloat16 [1024, 4096], P('ctx', 'grp'), may hold values from -6 to 6
- upstream: bfloat16 [1024, 4096], P('ctx', 'grp'), may hold values from -6 to 6
- skip_weight: float32 [4096], P('grp'), may hold values from -3 to 3
- residues: float32 [256, 16], replicated, may hold values from -3 to 3
- log_rates: float32 [256, 16], replicated, as said below
Outputs:
- query_grad: bfloat16 [1024, 4096], P('ctx', 'grp')
- key_grad: bfloat16 [1024, 4096], P('ctx', 'grp')
- value_grad: bfloat16 [1024, 4096], P('ctx', 'grp')
- skip_grad: float32 [4096], P('grp')
- residue_grad: float32 [256, 16], replicated
- log_rate_grad: float32 [256, 16], replicated
Inputs may be any that keep to these rules, and one draw needn't show every extreme that they name: `log_rates`: each entry is the natural logarithm of a rate between 1/4 and 1024/30.
All inputs are finite; a program needn't handle non-finite values.
Results may differ from a plain program's by a relative error of at most 0.0013.
Values sent between devices are 32-bit elements; how exact they have to be, the bound alone decides.
No kernel may reach another device: no remote copies, remote signals or barrier semaphores. Data moves between devices by JAX's collectives and lax.ppermute only.
A program may use at most 64 MiB of HBM per device.

v0:
```python
import functools

import jax
import jax.numpy as jnp
from jax import lax
from jax.experimental import pallas as pl
from jax.experimental.pallas import tpu as pltpu
from jax.sharding import PartitionSpec as P

GROUP_CH = 16
LANES = 128
SUB = 8
TILE_FILTERS = LANES // GROUP_CH
HIGHEST = lax.Precision.HIGHEST
F32 = jnp.float32
BF16 = jnp.bfloat16


def own_columns(table, filters):
    total = table.shape[1]
    start = lax.axis_index("grp") * filters
    return pltpu.roll(table, lax.rem(total - start, total), 1)[:, :filters]


def group_mask(filters, channels):
    row = lax.broadcasted_iota(jnp.int32, (filters, channels), 0)
    col = lax.broadcasted_iota(jnp.int32, (filters, channels), 1)
    return jnp.where(row == lax.div(col, GROUP_CH), 1.0, 0.0).astype(F32)


def per_channel(table, mask):
    return jnp.dot(table, mask, precision=HIGHEST, preferred_element_type=F32)


def split(x):
    high = x.astype(BF16)
    return high, (x - high.astype(F32)).astype(BF16)


def wide_dot(a_high, a_low, b_high, b_low):
    dot = functools.partial(jnp.dot, preferred_element_type=F32)
    return dot(a_high, b_high) + (dot(a_high, b_low) + dot(a_low, b_high))


def spread(row):
    return jnp.broadcast_to(row, (SUB, LANES))


def states_kernel(
    full,
    log_rates_h,
    key_h,
    values_h,
    upstream_h,
    query_h,
    states,
    decays,
    rate_out,
    mixed_out,
    carried_out,
    rates_s,
    key,
    values,
    upstream,
    query,
    weight_s,
    sems,
):
    rows, channels = key.shape
    tiles = channels // LANES
    filters = channels // GROUP_CH
    modes = log_rates_h.shape[0]
    copies = [
        pltpu.make_async_copy(src, dst, sems.at[n])
        for n, (src, dst) in enumerate(
            (
                (log_rates_h, rates_s),
                (key_h, key),
                (values_h, values),
                (upstream_h, upstream),
                (query_h, query),
            )
        )
    ]
    for copy in copies:
        copy.start()
    copies[0].wait()
    step_rates = own_columns(jnp.exp(rates_s[...]), filters) * (1.0 / full)
    channel_rates = per_channel(step_rates, group_mask(filters, channels))
    time = lax.broadcasted_iota(jnp.int32, (modes, rows), 1).astype(F32)
    back_time = float(rows - 1) - time
    for f in range(filters):
        rate = jnp.broadcast_to(step_rates[:, f : f + 1], (modes, rows))
        ct, place = f // TILE_FILTERS, pl.ds((f % TILE_FILTERS) * modes, modes)
        for n, high_low in enumerate((split(jnp.exp(-rate * back_time)), split(jnp.exp(-rate * time)))):
            weight_s[ct, 2 * n, place, :] = high_low[0]
            weight_s[ct, 2 * n + 1, place, :] = high_low[1]
    for ct in range(tiles):
        rate = channel_rates[:, ct * LANES : (ct + 1) * LANES]
        rate_out[ct] = rate
        decay = jnp.exp(-rate * float(rows))
        decays[ct * modes : (ct + 1) * modes, :] = decay
        decays[(tiles + ct) * modes : (tiles + ct + 1) * modes, :] = decay
    decays[2 * tiles * modes :, :] = jnp.ones((tiles, LANES), F32)
    lane_filter = lax.div(lax.broadcasted_iota(jnp.int32, (modes, LANES), 1), GROUP_CH)

    def fold(products):
        parts = [
            jnp.where(lane_filter == f, products[f * modes : (f + 1) * modes, :], 0.0)
            for f in range(TILE_FILTERS)
        ]
        while len(parts) > 1:
            parts = [a + b for a, b in zip(parts[::2], parts[1::2])]
        return parts[0]

    for copy in copies[1:]:
        copy.wait()
    for ct in range(tiles):
        lanes = slice(ct * LANES, (ct + 1) * LANES)
        mixed = key[:, lanes].astype(F32) * values[:, lanes].astype(F32)
        carried = upstream[:, lanes].astype(F32) * query[:, lanes].astype(F32)
        mixed_out[ct] = mixed
        carried_out[ct] = carried
        ahead = wide_dot(weight_s[ct, 0], weight_s[ct, 1], *split(mixed))
        behind = wide_dot(weight_s[ct, 2], weight_s[ct, 3], *split(carried))
        states[ct * modes : (ct + 1) * modes, :] = fold(ahead)
        states[(tiles + ct) * modes : (tiles + ct + 1) * modes, :] = fold(behind)
        states[2 * tiles * modes + ct : 2 * tiles * modes + ct + 1, :] = jnp.sum(
            mixed * carried, axis=0, keepdims=True
        )


def sub_ends(x_ref, ct, decay, steps, reverse):
    order = range(steps - 1, -1, -1) if reverse else range(steps)
    state = None
    for i in order:
        x = x_ref[ct, pl.ds(i, SUB, stride=steps), :]
        state = [x] * len(decay) if state is None else [d * s + x for d, s in zip(decay, state)]
    return state


def sub_starts(first, ends, jumps, reverse):
    index = lax.broadcasted_iota(jnp.int32, (SUB, LANES), 0)
    if reverse:
        index = SUB - 1 - index
    shift = lambda v, n: pltpu.roll(v, SUB - n if reverse else n, 0)
    out = []
    for m, (end, jump) in enumerate(zip(ends, jumps)):
        x = jnp.where(index == 0, 0.0 if first is None else spread(first[m : m + 1, :]), shift(end, 1))
        for n in (1, 2, 4):
            x = x + jnp.where(index >= n, jump, 0.0) * shift(x, n)
            jump = jump * jump
        out.append(x)
    return out


def local_kernel(begin, rate_ref, mixed_ref, carried_ref, sums, after_s):
    rows = mixed_ref.shape[1]
    modes = rate_ref.shape[1]
    steps = rows // SUB
    half = modes // 2
    index = lax.broadcasted_iota(jnp.int32, (SUB, LANES), 0).astype(F32)

    def tile(n, _):
        ct = begin + n
        rate = rate_ref[ct]
        for lo in range(0, modes, half):
            rate_rows = [spread(rate[m : m + 1, :]) for m in range(lo, lo + half)]
            decay = [jnp.exp(-r) for r in rate_rows]
            jumps = [jnp.exp(-r * float(steps)) for r in rate_rows]
            state = sub_starts(None, sub_ends(carried_ref, ct, decay, steps, True), jumps, True)
            tally = None
            for i in range(steps - 1, -1, -1):
                c = carried_ref[ct, pl.ds(i, SUB, stride=steps), :]
                after = [d * s for d, s in zip(decay, state)]
                for m in range(half):
                    after_s[i, m] = after[m]
                tally = after if tally is None else [d * t + a for d, t, a in zip(decay, tally, after)]
                state = [a + c for a in after]
            sums[n, 2 * modes + lo : 2 * modes + lo + half, :] = jnp.concatenate(
                [
                    jnp.sum(t * (d * jnp.exp(-r * (index * float(steps)))), axis=0, keepdims=True)
                    for t, d, r in zip(tally, decay, rate_rows)
                ],
                axis=0,
            )
            state = sub_starts(None, sub_ends(mixed_ref, ct, decay, steps, False), jumps, False)
            first = [jnp.zeros((SUB, LANES), F32)] * half
            second = [jnp.zeros((SUB, LANES), F32)] * half
            tally = None
            for i in range(steps):
                x = mixed_ref[ct, pl.ds(i, SUB, stride=steps), :]
                c = carried_ref[ct, pl.ds(i, SUB, stride=steps), :]
                state = [d * s + x for d, s in zip(decay, state)]
                first = [f + c * s for f, s in zip(first, state)]
                second = [f + after_s[i, m] * state[m] for m, f in enumerate(second)]
                tally = state if tally is None else [d * t + s for d, t, s in zip(decay, tally, state)]
            left = [jnp.exp(-r * ((SUB - 1 - index) * float(steps))) for r in rate_rows]
            for place, values in (
                (0, first),
                (modes, second),
                (3 * modes, [t * (d * e) for t, d, e in zip(tally, decay, left)]),
            ):
                sums[n, place + lo : place + lo + half, :] = jnp.concatenate(
                    [jnp.sum(v, axis=0, keepdims=True) for v in values], axis=0
                )
        return 0

    lax.fori_loop(0, sums.shape[0], tile, 0)


def cross_kernel(full, rows, skip_rows, rate_ref, own, edges, skip_total, *refs):
    *locals_, sums, skip_grad = refs
    tiles, modes, _ = rate_ref.shape
    half = tiles * modes
    filters = tiles * TILE_FILTERS
    skip_grad[...] = skip_total[pl.ds(skip_rows, tiles), :] / jnp.sqrt(jnp.float32(full))
    firsts, seconds = [], []
    done = 0
    for ref in locals_:
        for n in range(ref.shape[0]):
            ct = done + n
            rate = rate_ref[ct]
            at = slice(ct * modes, (ct + 1) * modes)
            far = slice(half + ct * modes, half + (ct + 1) * modes)
            incoming, outgoing = edges[at, :], edges[far, :]
            firsts.append(ref[n, 0:modes, :] + jnp.exp(-rate) * own[far, :] * incoming)
            seconds.append(
                ref[n, modes : 2 * modes, :]
                + incoming * ref[n, 2 * modes : 3 * modes, :]
                + outgoing * ref[n, 3 * modes : 4 * modes, :]
                + (float(rows) * jnp.exp(-rate * float(rows + 1))) * (incoming * outgoing)
            )
        done += ref.shape[0]
    mask = group_mask(filters, tiles * LANES)
    both = jnp.concatenate([jnp.concatenate(v, axis=1) for v in (firsts, seconds)], axis=0)
    summed = lax.dot_general(
        both, mask, (((1,), (1,)), ((), ())), precision=HIGHEST, preferred_element_type=F32
    )
    packed = jnp.concatenate([summed[:modes], summed[modes:] * (1.0 / full)], axis=1)

    def place(p, _):
        sums[p] = packed
        return 0

    lax.fori_loop(0, sums.shape[0], place, 0)


def grads_kernel(
    full,
    log_rates,
    residues,
    skip_weight,
    rate_ref,
    edges,
    mixed_ref,
    carried_ref,
    key,
    values,
    upstream,
    query_grad,
    key_grad,
    value_grad,
    conv_s,
    back_s,
    scale_s,
):
    tiles, rows, _ = mixed_ref.shape
    modes = rate_ref.shape[1]
    channels = tiles * LANES
    filters = channels // GROUP_CH
    steps = rows // SUB
    half = modes // 2
    rates = jnp.exp(own_columns(log_rates[...], filters))
    scaled = own_columns(residues[...], filters) * jnp.sqrt(rates / full)
    scaled = per_channel(scaled, group_mask(filters, channels))
    for ct in range(tiles):
        scale_s[ct] = scaled[:, ct * LANES : (ct + 1) * LANES]

    def tile(ct, _):
        rate = rate_ref[ct]
        scale = scale_s[ct]
        base = pl.multiple_of(ct * modes, modes)
        incoming = edges[pl.ds(base, modes), :]
        outgoing = edges[pl.ds(tiles * modes + base, modes), :]
        for lo in range(0, modes, half):
            rate_rows = [spread(rate[m : m + 1, :]) for m in range(lo, lo + half)]
            decay = [jnp.exp(-r) for r in rate_rows]
            jumps = [jnp.exp(-r * float(steps)) for r in rate_rows]
            scales = [spread(scale[m : m + 1, :]) for m in range(lo, lo + half)]
            for x_ref, edge, result, reverse in (
                (mixed_ref, incoming, conv_s, False),
                (carried_ref, outgoing, back_s, True),
            ):
                ends = sub_ends(x_ref, ct, decay, steps, reverse)
                state = sub_starts(edge[lo : lo + half, :], ends, jumps, reverse)
                for i in range(steps - 1, -1, -1) if reverse else range(steps):
                    x = x_ref[ct, pl.ds(i, SUB, stride=steps), :]
                    state = [d * s + x for d, s in zip(decay, state)]
                    terms = [g * s for g, s in zip(scales, state)]
                    if lo > 0:
                        terms.append(result[pl.ds(i, SUB, stride=steps), :])
                    result[pl.ds(i, SUB, stride=steps), :] = functools.reduce(jnp.add, terms)
        lanes = pl.ds(pl.multiple_of(ct * LANES, LANES), LANES)
        weight = skip_weight[pl.ds(ct, 1), :]
        query_grad[:, lanes] = (
            upstream[:, lanes].astype(F32) * (conv_s[...] + weight * mixed_ref[ct])
        ).astype(query_grad.dtype)
        mixed_grad = back_s[...] + weight * carried_ref[ct]
        key_grad[:, lanes] = (mixed_grad * values[:, lanes].astype(F32)).astype(key_grad.dtype)
        value_grad[:, lanes] = (mixed_grad * key[:, lanes].astype(F32)).astype(value_grad.dtype)
        return 0

    lax.fori_loop(0, tiles, tile, 0)


def final_kernel(full, groups, log_rates, residues, sums, residue_grad, log_rate_grad):
    modes = log_rates.shape[0]
    filters = sums.shape[2] // 2
    totals = []
    for g in range(groups):
        parts = [sums[p] for p in range(g, sums.shape[0], groups)]
        totals.append(functools.reduce(jnp.add, parts))
    first_sum = jnp.concatenate([t[:, :filters] for t in totals], axis=1)
    second_sum = jnp.concatenate([t[:, filters:] for t in totals], axis=1)
    rates = jnp.exp(log_rates[...])
    root = jnp.sqrt(rates / full)
    scale_root = jnp.sqrt(jnp.float32(full))
    residue_grad[...] = root * first_sum / scale_root
    log_rate_grad[...] = residues[...] * root * (0.5 * first_sum - rates * second_sum) / scale_root


def exchange(states, decays, rows_state):
    context = lax.axis_size("ctx")
    position = lax.axis_index("ctx")
    is_forward = lax.broadcasted_iota(jnp.int32, states.shape, 0) < rows_state
    edge_rows = 2 * rows_state
    edges = reach = None
    step = 1
    while step < context:
        upper = (position & step) != 0
        pairs = [(i, i ^ step) for i in range(context)]
        takes = (is_forward == upper)[:edge_rows]
        if 2 * step < context:
            other = lax.ppermute(states, "ctx", pairs)
            summed = jnp.where(is_forward == upper, states + decays * other, decays * states + other)
            skip = summed[edge_rows:]
        else:
            half = jnp.where(upper, states[rows_state:edge_rows], states[:rows_state])
            other = lax.ppermute(
                jnp.concatenate([half, states[edge_rows:]], axis=0), "ctx", pairs
            )
            skip = states[edge_rows:] + other[rows_state:]
            other = jnp.concatenate([other[:rows_state]] * 2, axis=0)
            summed = None
        other = other[:edge_rows]
        if edges is None:
            edges = jnp.where(takes, other, 0.0)
            reach = jnp.where(takes, decays[:edge_rows], 1.0)
        else:
            edges = edges + jnp.where(takes, reach * other, 0.0)
            reach = jnp.where(takes, reach * decays[:edge_rows], reach)
        decays = decays * decays
        states = summed
        step *= 2
    return edges, skip


def local(query_gate, key_gate, values, upstream, skip_weight, residues, log_rates):
    context = lax.axis_size("ctx")
    groups = lax.axis_size("grp")
    rows, channels = query_gate.shape
    total_filters, modes = residues.shape
    filters = channels // GROUP_CH
    tiles = channels // LANES
    full = rows * context
    rows_state = tiles * modes
    chunk = 2 * rows_state + tiles
    vmem = pl.BlockSpec(memory_space=pltpu.VMEM)
    anywhere = pl.BlockSpec(memory_space=pltpu.HBM)
    shape = jax.ShapeDtypeStruct
    params = pltpu.CompilerParams(vmem_limit_bytes=16 * 1024 * 1024)
    log_rates_t, residues_t = log_rates.T, residues.T

    states, decays, rate, mixed, carried = pl.pallas_call(
        functools.partial(states_kernel, full),
        out_shape=(
            shape((chunk, LANES), F32),
            shape((chunk, LANES), F32),
            shape((tiles, modes, LANES), F32),
            shape((tiles, rows, LANES), F32),
            shape((tiles, rows, LANES), F32),
        ),
        in_specs=[anywhere] * 5,
        out_specs=(vmem,) * 5,
        scratch_shapes=[
            pltpu.VMEM((modes, total_filters), F32),
            pltpu.VMEM((rows, channels), BF16),
            pltpu.VMEM((rows, channels), BF16),
            pltpu.VMEM((rows, channels), BF16),
            pltpu.VMEM((rows, channels), BF16),
            pltpu.VMEM((tiles, 4, TILE_FILTERS * modes, rows), BF16),
            pltpu.SemaphoreType.DMA((5,)),
        ],
        compiler_params=params,
        name="states",
    )(*(pltpu.with_memory_space_constraint(x, pltpu.HBM) for x in (log_rates_t, key_gate, values, upstream, query_gate)))

    edges, skip_total = exchange(states, decays, rows_state)

    pieces = 2
    share = tiles // pieces
    work = rows * channels * modes // pieces
    local_sums = [
        pl.pallas_call(
            functools.partial(local_kernel, n * share),
            out_shape=shape((share, 4 * modes, LANES), F32),
            in_specs=[vmem] * 3,
            out_specs=vmem,
            scratch_shapes=[pltpu.VMEM((rows // SUB, modes // 2, SUB, LANES), F32)],
            compiler_params=params,
            cost_estimate=pl.CostEstimate(
                flops=16 * work, transcendentals=0, bytes_accessed=8 * rows * channels // pieces
            ),
            name="within",
        )(rate, mixed, carried)
        for n in range(pieces)
    ]

    sums, skip_grad = pl.pallas_call(
        functools.partial(cross_kernel, full, rows, 0),
        out_shape=(shape((context * groups, modes, 2 * filters), F32), shape((tiles, LANES), F32)),
        in_specs=[vmem] * (4 + pieces),
        out_specs=(vmem,) * 2,
        compiler_params=params,
        name="across",
    )(rate, states, edges, skip_total, *local_sums)

    everyone = lax.all_to_all(sums, ("ctx", "grp"), split_axis=0, concat_axis=0, tiled=True)

    query_grad, key_grad, value_grad = pl.pallas_call(
        functools.partial(grads_kernel, full),
        out_shape=(shape((rows, channels), BF16),) * 3,
        in_specs=[vmem] * 10,
        out_specs=(vmem,) * 3,
        scratch_shapes=[
            pltpu.VMEM((rows, LANES), F32),
            pltpu.VMEM((rows, LANES), F32),
            pltpu.VMEM((tiles, modes, LANES), F32),
        ],
        compiler_params=params,
        cost_estimate=pl.CostEstimate(
            flops=12 * rows * channels * modes, transcendentals=0, bytes_accessed=20 * rows * channels
        ),
        name="grads",
    )(
        log_rates_t,
        residues_t,
        skip_weight.reshape(tiles, LANES),
        rate,
        edges,
        mixed,
        carried,
        key_gate,
        values,
        upstream,
    )

    residue_grad, log_rate_grad = pl.pallas_call(
        functools.partial(final_kernel, full, groups),
        out_shape=(shape((modes, total_filters), F32),) * 2,
        in_specs=[vmem] * 3,
        out_specs=(vmem,) * 2,
        compiler_params=params,
        name="final",
    )(log_rates_t, residues_t, everyone)
    return (
        query_grad,
        key_grad,
        value_grad,
        skip_grad.reshape(channels),
        residue_grad.T,
        log_rate_grad.T,
    )


def solution(mesh):
    placed = (
        P("ctx", "grp"),
        P("ctx", "grp"),
        P("ctx", "grp"),
        P("ctx", "grp"),
        P("grp"),
        P(),
        P(),
    )
    return jax.shard_map(
        local,
        mesh=mesh,
        in_specs=placed,
        out_specs=(P("ctx", "grp"), P("ctx", "grp"), P("ctx", "grp"), P("grp"), P(), P()),
        check_vma=False,
    )
```

profile of v0, /device:TPU:0, one launch (start us, length us, event | category | flops | bytes accessed | tf_op | source)
XLA Modules:
  0.0 40.2 jit_solution(8027341444329530561)
XLA Ops:
  0.6 1.9 %states.1 = (f32[264,128]{1,0:T(8,128)S(1)}, f32[264,128]{1,0:T(8,128)S(1)}, f32[8,16,128]{2,1,0:T(8,128)S(1)}, f32[8,128,128]{2,1,0:T(8,128)S(1)}, f32[8,128,128]{2,1,0:T(8,128)S(1)}) custom-call(f32[16,256]{1,0:T(8,128)} %bitcast.9, bf16[128,1024]{1,0:T(8,128)(2,1)} %key.1, bf16[128,1024]{1,0:T(8,128)(2,1)} %values.1, bf16[128,1024]{1,0:T(8,128)(2,1)} %upstream.1, ...), custom_call_target="tpu_custom_call" | custom-call | tf_op jit(solution)/shard_map/states/pallas_call | solution.py:385
  2.5 3.0 %collective-permute-start = (f32[264,128]{1,0:T(8,128)S(1)}, f32[264,128]{1,0:T(8,128)S(1)}, u32[]{:S(2)}, u32[]{:S(2)}) collective-permute-start(f32[264,128]{1,0:T(8,128)S(1)} %get-tuple-element.19.own), channel_id=1, source_target_pairs={{0,4},{4,0},{8,12},{12,8},{16,20},{20,16},{24,28},{28,24},{1,5},{5... | collective-permute-start | bytes 405512 | tf_op jit(solution)/shard_map/ppermute | solution.py:345
  5.6 3.6 %collective-permute-done = f32[264,128]{1,0:T(8,128)S(1)} collective-permute-done((f32[264,128]{1,0:T(8,128)S(1)}, f32[264,128]{1,0:T(8,128)S(1)}, u32[]{:S(2)}, u32[]{:S(2)}) %collective-permute-start) | collective-permute-done | bytes 135200 | tf_op jit(solution)/shard_map/ppermute | solution.py:345
  9.2 0.1 add_select_fusion.1
  9.3 1.9 %collective-permute-start.1 = (f32[264,128]{1,0:T(8,128)S(1)}, f32[264,128]{1,0:T(8,128)S(1)}, u32[]{:S(2)}, u32[]{:S(2)}) collective-permute-start(f32[264,128]{1,0:T(8,128)S(1)} %add_select_fusion.1), channel_id=1, source_target_pairs={{0,8},{4,12},{8,0},{12,4},{16,24},{20,28},{24,16},{28,20},{1,9},{5... | collective-permute-start | bytes 405512 | tf_op jit(solution)/shard_map/ppermute | solution.py:345
  11.1 3.0 %within.3.refs_1_ = f32[4,64,128]{2,1,0:T(8,128)S(1)} custom-call(f32[8,16,128]{2,1,0:T(8,128)S(1)} %get-tuple-element.18.rate_ref, f32[8,128,128]{2,1,0:T(8,128)S(1)} %get-tuple-element.21.mixed_ref, f32[8,128,128]{2,1,0:T(8,128)S(1)} %get-tuple-element.22.carried_ref), custom_call_target="tpu_custom_call" | custom-call | flops 16777216 | bytes 524288 | tf_op jit(solution)/shard_map/within/pallas_call | solution.py:415
  14.2 3.0 %within.2.refs_0_ = f32[4,64,128]{2,1,0:T(8,128)S(1)} custom-call(f32[8,16,128]{2,1,0:T(8,128)S(1)} %get-tuple-element.18.rate_ref, f32[8,128,128]{2,1,0:T(8,128)S(1)} %get-tuple-element.21.mixed_ref, f32[8,128,128]{2,1,0:T(8,128)S(1)} %get-tuple-element.22.carried_ref), custom_call_target="tpu_custom_call" | custom-call | flops 16777216 | bytes 524288 | tf_op jit(solution)/shard_map/within/pallas_call | solution.py:415
  17.2 0.0 collective-permute-done.1
  17.2 0.1 add_select_fusion
  17.4 2.7 %collective-permute-start.2 = (f32[136,128]{1,0:T(8,128)S(1)}, f32[136,128]{1,0:T(8,128)S(1)}, u32[]{:S(2)}, u32[]{:S(2)}) collective-permute-start(f32[136,128]{1,0:T(8,128)S(1)} %pad_maximum_fusion), channel_id=1, source_target_pairs={{0,16},{4,20},{8,24},{12,28},{16,0},{20,4},{24,8},{28,12},{1,17},{... | collective-permute-start | bytes 208904 | tf_op jit(solution)/shard_map/ppermute | solution.py:350
  20.1 3.0 %collective-permute-done.2 = f32[136,128]{1,0:T(8,128)S(1)} collective-permute-done((f32[136,128]{1,0:T(8,128)S(1)}, f32[136,128]{1,0:T(8,128)S(1)}, u32[]{:S(2)}, u32[]{:S(2)}) %collective-permute-start.2) | collective-permute-done | bytes 69664 | tf_op jit(solution)/shard_map/ppermute | solution.py:350
  23.1 0.2 fusion.2.edges
  23.3 0.0 copy-start.2
  23.3 0.0 copy-start.3
  23.3 0.0 copy-start.4
  23.3 0.0 copy-start.5
  23.3 1.2 %across.1 = (f32[32,16,128]{2,1,0:T(8,128)}, f32[8,128]{1,0:T(8,128)}) custom-call(f32[8,16,128]{2,1,0:T(8,128)S(1)} %get-tuple-element.18.rate_ref, f32[264,128]{1,0:T(8,128)S(1)} %get-tuple-element.19.own, f32[256,128]{1,0:T(8,128)S(1)} %fusion.2.edges, f32[8,128]{1,0:T(8,128)S(1)} %slice_add_fusion.skip_total, f32[4,64,128]{2,1,0:T(8,128)S(1)} %within.2.refs_0_, ...), custom_call_target="tpu_custom_call" | custom-call | tf_op jit(solution)/shard_map/across/pallas_call | solution.py:430
  24.5 4.4 %all-to-all-start = ((f32[32,16,128]{2,1,0:T(8,128)}), f32[32,16,128]{2,1,0:T(8,128)S(1)}, u32[]{:S(2)}, u32[]{:S(2)}) async-start(f32[32,16,128]{2,1,0:T(8,128)} %get-tuple-element.27), calls=%async_computation | async-start | bytes 524288 | tf_op jit(solution)/shard_map/all_to_all | solution.py:439
  28.9 0.0 copy-done.2
  29.0 0.0 copy-done.3
  29.0 0.0 copy-done.4
  29.0 6.0 %grads.1 = (bf16[128,1024]{1,0:T(8,128)(2,1)}, bf16[128,1024]{1,0:T(8,128)(2,1)}, bf16[128,1024]{1,0:T(8,128)(2,1)}) custom-call(f32[16,256]{1,0:T(8,128)S(1)} %bitcast.10, f32[16,256]{1,0:T(8,128)S(1)} %bitcast.12, f32[8,128]{1,0:T(8,128)S(1)} %bitcast.14, f32[8,16,128]{2,1,0:T(8,128)S(1)} %get-tuple-element.18.rate_ref, f32[256,128]{1,0:T(8,128)S(1)} %fusion.2.edges, ...), custom_call_target="tpu_custom_call" | custom-call | flops 25165824 | bytes 2621440 | tf_op jit(solution)/shard_map/grads/pallas_call | solution.py:441
  35.0 4.5 %all-to-all-done.sums = f32[32,16,128]{2,1,0:T(8,128)S(1)} async-done(((f32[32,16,128]{2,1,0:T(8,128)}), f32[32,16,128]{2,1,0:T(8,128)S(1)}, u32[]{:S(2)}, u32[]{:S(2)}) %all-to-all-start) | async-done | bytes 262176 | tf_op jit(solution)/shard_map/all_to_all | solution.py:439
  39.5 0.7 %final.1 = (f32[16,256]{1,0:T(8,128)}, f32[16,256]{1,0:T(8,128)}) custom-call(f32[16,256]{1,0:T(8,128)S(1)} %bitcast.11, f32[16,256]{1,0:T(8,128)S(1)} %bitcast.13, f32[32,16,128]{2,1,0:T(8,128)S(1)} %all-to-all-done.sums), custom_call_target="tpu_custom_call" | custom-call | tf_op jit(solution)/shard_map/final/pallas_call | solution.py:469
  (13 shorter events, 0.1 us)
Async XLA Ops:
  2.5 6.6 %collective-permute-start = (f32[264,128]{1,0:T(8,128)S(1)}, f32[264,128]{1,0:T(8,128)S(1)}, u32[]{:S(2)}, u32[]{:S(2)}) collective-permute-start(f32[264,128]{1,0:T(8,128)S(1)} %get-tuple-element.19.own), channel_id=1, source_target_pairs={{0,4},{4,0},{8,12},{12,8},{16,20},{20,16},{24,28},{28,24},{1,5},{5... | collective-permute-start | bytes 405512 | tf_op jit(solution)/shard_map/ppermute | solution.py:345
  9.3 8.0 %collective-permute-start.1 = (f32[264,128]{1,0:T(8,128)S(1)}, f32[264,128]{1,0:T(8,128)S(1)}, u32[]{:S(2)}, u32[]{:S(2)}) collective-permute-start(f32[264,128]{1,0:T(8,128)S(1)} %add_select_fusion.1), channel_id=1, source_target_pairs={{0,8},{4,12},{8,0},{12,4},{16,24},{20,28},{24,16},{28,20},{1,9},{5... | collective-permute-start | bytes 405512 | tf_op jit(solution)/shard_map/ppermute | solution.py:345
  17.4 5.7 %collective-permute-start.2 = (f32[136,128]{1,0:T(8,128)S(1)}, f32[136,128]{1,0:T(8,128)S(1)}, u32[]{:S(2)}, u32[]{:S(2)}) collective-permute-start(f32[136,128]{1,0:T(8,128)S(1)} %pad_maximum_fusion), channel_id=1, source_target_pairs={{0,16},{4,20},{8,24},{12,28},{16,0},{20,4},{24,8},{28,12},{1,17},{... | collective-permute-start | bytes 208904 | tf_op jit(solution)/shard_map/ppermute | solution.py:350
  23.3 5.7 %copy-start.2 = (bf16[128,1024]{1,0:T(8,128)(2,1)S(1)}, bf16[128,1024]{1,0:T(8,128)(2,1)}, u32[]{:S(2)}) copy-start(bf16[128,1024]{1,0:T(8,128)(2,1)} %upstream.1) | copy-start | bytes 786436
  23.3 5.7 %copy-start.3 = (f32[256,16]{0,1:T(8,128)S(1)}, f32[256,16]{0,1:T(8,128)}, u32[]{:S(2)}) copy-start(f32[256,16]{0,1:T(8,128)} %param.13) | copy-start | bytes 49156
  23.3 5.7 %copy-start.4 = (f32[256,16]{0,1:T(8,128)S(1)}, f32[256,16]{0,1:T(8,128)}, u32[]{:S(2)}) copy-start(f32[256,16]{0,1:T(8,128)} %param.12) | copy-start | bytes 49156
  23.3 5.7 %copy-start.5 = (f32[1024]{0:T(1024)S(1)}, f32[1024]{0:T(1024)}, u32[]{:S(2)}) copy-start(f32[1024]{0:T(1024)} %param.11) | copy-start | bytes 12292
  24.5 4.5 %copy-start = (bf16[128,1024]{1,0:T(8,128)(2,1)S(1)}, bf16[128,1024]{1,0:T(8,128)(2,1)}, u32[]{:S(2)}) copy-start(bf16[128,1024]{1,0:T(8,128)(2,1)} %key.1) | copy-start | bytes 786436
  24.5 4.5 %copy-start.1 = (bf16[128,1024]{1,0:T(8,128)(2,1)S(1)}, bf16[128,1024]{1,0:T(8,128)(2,1)}, u32[]{:S(2)}) copy-start(bf16[128,1024]{1,0:T(8,128)(2,1)} %values.1) | copy-start | bytes 786436
  24.5 15.0 %all-to-all-start = ((f32[32,16,128]{2,1,0:T(8,128)}), f32[32,16,128]{2,1,0:T(8,128)S(1)}, u32[]{:S(2)}, u32[]{:S(2)}) async-start(f32[32,16,128]{2,1,0:T(8,128)} %get-tuple-element.27), calls=%async_computation | async-start | bytes 524288 | tf_op jit(solution)/shard_map/all_to_all | solution.py:439
where the time goes:
time: 40.5 us; the launch traced here: 40.2 us
  Pallas kernels  15.9 us (39%)
  starting transfers between devices  12 us (30%)
  waiting for transfers between devices  11.1 us (27%)
  between operations  0.81 us (2%)
  other arithmetic  0.44 us (1%)
    pallas_call x2, Pallas kernels, local(): pl.pallas_call(functools.partial(local_kernel, n * share), out_shape=shap...  6.07 us
    pallas_call x1, Pallas kernels, local(): pl.pallas_call(functools.partial(grads_kernel, full), out_shape=(shape((r...  6.02 us
    ppermute x2, starting transfers between devices, exchange(): other = lax.ppermute(states, 'ctx', pairs)  4.89 us
    all_to_all x1, waiting for transfers between devices, local(): lax.all_to_all(sums, ('ctx', 'grp'), split_axis=0, concat_axis=0, tiled=T...  4.52 us
    all_to_all x1, starting transfers between devices, local(): lax.all_to_all(sums, ('ctx', 'grp'), split_axis=0, concat_axis=0, tiled=T...  4.42 us
    ppermute x2, waiting for transfers between devices, exchange(): other = lax.ppermute(states, 'ctx', pairs)  3.58 us
    ppermute x1, waiting for transfers between devices, exchange(): lax.ppermute(jnp.concatenate([half, states[edge_rows:]], axis=0), 'ctx',...  3.02 us
    ppermute x1, starting transfers between devices, exchange(): lax.ppermute(jnp.concatenate([half, states[edge_rows:]], axis=0), 'ctx',...  2.65 us
  transfers between devices with their start and end apart: 4, of which 3 were waited for; matrix products, arithmetic and copies ran while one was open for 0% of the time, Pallas kernels for 30%

commit v1 on v0

--- a/solution.py
+++ b/solution.py
@@ -139,14 +139,14 @@
     return state
 
 
-def sub_starts(first, ends, jumps, reverse):
+def sub_starts(ends, jumps, reverse):
     index = lax.broadcasted_iota(jnp.int32, (SUB, LANES), 0)
     if reverse:
         index = SUB - 1 - index
     shift = lambda v, n: pltpu.roll(v, SUB - n if reverse else n, 0)
     out = []
-    for m, (end, jump) in enumerate(zip(ends, jumps)):
-        x = jnp.where(index == 0, 0.0 if first is None else spread(first[m : m + 1, :]), shift(end, 1))
+    for end, jump in zip(ends, jumps):
+        x = jnp.where(index == 0, 0.0, shift(end, 1))
         for n in (1, 2, 4):
             x = x + jnp.where(index >= n, jump, 0.0) * shift(x, n)
             jump = jump * jump
@@ -154,8 +154,8 @@
     return out
 
 
-def local_kernel(begin, rate_ref, mixed_ref, carried_ref, sums, after_s):
-    rows = mixed_ref.shape[1]
+def local_kernel(begin, rate_ref, states, mixed_ref, carried_ref, sums, starts, after_s):
+    tiles, rows, _ = mixed_ref.shape
     modes = rate_ref.shape[1]
     steps = rows // SUB
     half = modes // 2
@@ -164,11 +164,16 @@
     def tile(n, _):
         ct = begin + n
         rate = rate_ref[ct]
+        behind = states[pl.ds(pl.multiple_of((tiles + ct) * modes, modes), modes), :]
+        sums[n, 4 * modes : 5 * modes, :] = jnp.exp(-rate) * behind
+        sums[n, 5 * modes : 6 * modes, :] = float(rows) * jnp.exp(-rate * float(rows + 1))
         for lo in range(0, modes, half):
             rate_rows = [spread(rate[m : m + 1, :]) for m in range(lo, lo + half)]
             decay = [jnp.exp(-r) for r in rate_rows]
             jumps = [jnp.exp(-r * float(steps)) for r in rate_rows]
-            state = sub_starts(None, sub_ends(carried_ref, ct, decay, steps, True), jumps, True)
+            state = sub_starts(sub_ends(carried_ref, ct, decay, steps, True), jumps, True)
+            for m in range(half):
+                starts[n, 1, lo + m] = state[m]
             tally = None
             for i in range(steps - 1, -1, -1):
                 c = carried_ref[ct, pl.ds(i, SUB, stride=steps), :]
@@ -184,7 +189,9 @@
                 ],
                 axis=0,
             )
-            state = sub_starts(None, sub_ends(mixed_ref, ct, decay, steps, False), jumps, False)
+            state = sub_starts(sub_ends(mixed_ref, ct, decay, steps, False), jumps, False)
+            for m in range(half):
+                starts[n, 0, lo + m] = state[m]
             first = [jnp.zeros((SUB, LANES), F32)] * half
             second = [jnp.zeros((SUB, LANES), F32)] * half
             tally = None
@@ -209,45 +216,62 @@
     lax.fori_loop(0, sums.shape[0], tile, 0)
 
 
-def cross_kernel(full, rows, skip_rows, rate_ref, own, edges, skip_total, *refs):
-    *locals_, sums, skip_grad = refs
-    tiles, modes, _ = rate_ref.shape
-    half = tiles * modes
-    filters = tiles * TILE_FILTERS
-    skip_grad[...] = skip_total[pl.ds(skip_rows, tiles), :] / jnp.sqrt(jnp.float32(full))
-    firsts, seconds = [], []
-    done = 0
+def across_kernel(full, unit, decays, states, edges_in, reach, near, middle, far, *refs):
+    *locals_, edges, skip_grad, packed = refs
+    tiles = skip_grad.shape[0]
+    half = (states.shape[0] - tiles) // 2
+    modes = half // tiles
+    place = lax.axis_index("ctx") // unit
+    skip = states[2 * half :, :]
+    for ref in (near, middle, far):
+        skip = skip + ref[half:, :]
+    skip_grad[...] = skip / jnp.sqrt(jnp.float32(full))
+    sums = []
+    ct = 0
     for ref in locals_:
+        firsts, seconds = [], []
         for n in range(ref.shape[0]):
-            ct = done + n
-            rate = rate_ref[ct]
             at = slice(ct * modes, (ct + 1) * modes)
-            far = slice(half + ct * modes, half + (ct + 1) * modes)
-            incoming, outgoing = edges[at, :], edges[far, :]
-            firsts.append(ref[n, 0:modes, :] + jnp.exp(-rate) * own[far, :] * incoming)
-            seconds.append(
-                ref[n, modes : 2 * modes, :]
-                + incoming * ref[n, 2 * modes : 3 * modes, :]
-                + outgoing * ref[n, 3 * modes : 4 * modes, :]
-                + (float(rows) * jnp.exp(-rate * float(rows + 1))) * (incoming * outgoing)
-            )
-        done += ref.shape[0]
-    mask = group_mask(filters, tiles * LANES)
-    both = jnp.concatenate([jnp.concatenate(v, axis=1) for v in (firsts, seconds)], axis=0)
-    summed = lax.dot_general(
-        both, mask, (((1,), (1,)), ((), ())), precision=HIGHEST, preferred_element_type=F32
+            up = slice(half + ct * modes, half + (ct + 1) * modes)
+            decay = decays[at, :]
+            incoming = outgoing = jnp.zeros((modes, LANES), F32)
+            for k, other in ((1, near), (2, middle), (3, far)):
+                partner = place ^ k
+                apart = jnp.abs(place - partner)
+                term = other[at, :]
+                term = jnp.where(apart >= 2, term * decay, term)
+                term = jnp.where(apart >= 3, term * decay, term)
+                incoming = incoming + jnp.where(partner < place, term, 0.0)
+                outgoing = outgoing + jnp.where(partner > place, term, 0.0)
+            incoming = edges_in[at, :] + reach[at, :] * incoming
+            outgoing = edges_in[up, :] + reach[up, :] * outgoing
+            edges[at, :] = incoming
+            edges[up, :] = outgoing
+            part = [ref[n, p * modes : (p + 1) * modes, :] for p in range(6)]
+            firsts.append(part[0] + part[4] * incoming)
+            seconds.append(part[1] + incoming * (part[2] + part[5] * outgoing) + outgoing * part[3])
+            ct += 1
+        both = jnp.concatenate([jnp.concatenate(v, axis=1) for v in (firsts, seconds)], axis=0)
+        channels = both.shape[1]
+        high, rest = split(both)
+        middle_part, low = split(both - high.astype(F32))
+        stacked = jnp.concatenate([high, middle_part, low], axis=0)
+        summed = lax.dot_general(
+            stacked,
+            group_mask(channels // GROUP_CH, channels).astype(BF16),
+            (((1,), (1,)), ((), ())),
+            preferred_element_type=F32,
+        )
+        sums.append(summed[: 2 * modes] + summed[2 * modes : 4 * modes] + summed[4 * modes :])
+    packed[...] = jnp.concatenate(
+        [v[:modes] for v in sums] + [v[modes:] * (1.0 / full) for v in sums], axis=1
     )
-    packed = jnp.concatenate([summed[:modes], summed[modes:] * (1.0 / full)], axis=1)
-
-    def place(p, _):
-        sums[p] = packed
-        return 0
-
-    lax.fori_loop(0, sums.shape[0], place, 0)
 
 
 def grads_kernel(
     full,
+    begin,
+    aliased,
     log_rates,
     residues,
     skip_weight,
@@ -255,16 +279,13 @@
     edges,
     mixed_ref,
     carried_ref,
+    starts,
     key,
     values,
     upstream,
-    query_grad,
-    key_grad,
-    value_grad,
-    conv_s,
-    back_s,
-    scale_s,
+    *refs,
 ):
+    query_grad, key_grad, value_grad, conv_s, back_s, scale_s = refs[aliased:]
     tiles, rows, _ = mixed_ref.shape
     modes = rate_ref.shape[1]
     channels = tiles * LANES
@@ -276,8 +297,11 @@
     scaled = per_channel(scaled, group_mask(filters, channels))
     for ct in range(tiles):
         scale_s[ct] = scaled[:, ct * LANES : (ct + 1) * LANES]
-
-    def tile(ct, _):
+    index = lax.broadcasted_iota(jnp.int32, (SUB, LANES), 0).astype(F32) * float(steps)
+    back_index = float(rows - steps) - index
+
+    def tile(n, _):
+        ct = begin + n
         rate = rate_ref[ct]
         scale = scale_s[ct]
         base = pl.multiple_of(ct * modes, modes)
@@ -286,22 +310,22 @@
         for lo in range(0, modes, half):
             rate_rows = [spread(rate[m : m + 1, :]) for m in range(lo, lo + half)]
             decay = [jnp.exp(-r) for r in rate_rows]
-            jumps = [jnp.exp(-r * float(steps)) for r in rate_rows]
             scales = [spread(scale[m : m + 1, :]) for m in range(lo, lo + half)]
-            for x_ref, edge, result, reverse in (
-                (mixed_ref, incoming, conv_s, False),
-                (carried_ref, outgoing, back_s, True),
+            for way, (x_ref, edge, result, away) in enumerate(
+                ((mixed_ref, incoming, conv_s, index), (carried_ref, outgoing, back_s, back_index))
             ):
-                ends = sub_ends(x_ref, ct, decay, steps, reverse)
-                state = sub_starts(edge[lo : lo + half, :], ends, jumps, reverse)
-                for i in range(steps - 1, -1, -1) if reverse else range(steps):
+                state = [
+                    starts[n, way, lo + m] + jnp.exp(-r * away) * edge[lo + m : lo + m + 1, :]
+                    for m, r in enumerate(rate_rows)
+                ]
+                for i in range(steps - 1, -1, -1) if way else range(steps):
                     x = x_ref[ct, pl.ds(i, SUB, stride=steps), :]
                     state = [d * s + x for d, s in zip(decay, state)]
                     terms = [g * s for g, s in zip(scales, state)]
                     if lo > 0:
                         terms.append(result[pl.ds(i, SUB, stride=steps), :])
                     result[pl.ds(i, SUB, stride=steps), :] = functools.reduce(jnp.add, terms)
-        lanes = pl.ds(pl.multiple_of(ct * LANES, LANES), LANES)
+        lanes = pl.ds(pl.multiple_of(n * LANES, LANES), LANES)
         weight = skip_weight[pl.ds(ct, 1), :]
         query_grad[:, lanes] = (
             upstream[:, lanes].astype(F32) * (conv_s[...] + weight * mixed_ref[ct])
@@ -311,16 +335,20 @@
         value_grad[:, lanes] = (mixed_grad * key[:, lanes].astype(F32)).astype(value_grad.dtype)
         return 0
 
-    lax.fori_loop(0, tiles, tile, 0)
-
-
-def final_kernel(full, groups, log_rates, residues, sums, residue_grad, log_rate_grad):
-    modes = log_rates.shape[0]
-    filters = sums.shape[2] // 2
+    lax.fori_loop(0, starts.shape[0], tile, 0)
+
+
+def final_kernel(full, log_rates, residues, mine, theirs, residue_grad, log_rate_grad):
+    modes, total_filters = log_rates.shape
+    filters = mine.shape[1] // 2
+    group = lax.axis_index("grp")
+    by_distance = [mine[:modes, :], theirs[:modes, :], mine[modes:, :], theirs[modes:, :]]
     totals = []
-    for g in range(groups):
-        parts = [sums[p] for p in range(g, sums.shape[0], groups)]
-        totals.append(functools.reduce(jnp.add, parts))
+    for g in range(total_filters // filters):
+        total = by_distance[0]
+        for k in range(1, 4):
+            total = jnp.where((group ^ k) == g, by_distance[k], total)
+        totals.append(total)
     first_sum = jnp.concatenate([t[:, :filters] for t in totals], axis=1)
     second_sum = jnp.concatenate([t[:, filters:] for t in totals], axis=1)
     rates = jnp.exp(log_rates[...])
@@ -330,58 +358,33 @@
     log_rate_grad[...] = residues[...] * root * (0.5 * first_sum - rates * second_sum) / scale_root
 
 
-def exchange(states, decays, rows_state):
-    context = lax.axis_size("ctx")
-    position = lax.axis_index("ctx")
-    is_forward = lax.broadcasted_iota(jnp.int32, states.shape, 0) < rows_state
-    edge_rows = 2 * rows_state
-    edges = reach = None
-    step = 1
-    while step < context:
-        upper = (position & step) != 0
-        pairs = [(i, i ^ step) for i in range(context)]
-        takes = (is_forward == upper)[:edge_rows]
-        if 2 * step < context:
-            other = lax.ppermute(states, "ctx", pairs)
-            summed = jnp.where(is_forward == upper, states + decays * other, decays * states + other)
-            skip = summed[edge_rows:]
-        else:
-            half = jnp.where(upper, states[rows_state:edge_rows], states[:rows_state])
-            other = lax.ppermute(
-                jnp.concatenate([half, states[edge_rows:]], axis=0), "ctx", pairs
-            )
-            skip = states[edge_rows:] + other[rows_state:]
-            other = jnp.concatenate([other[:rows_state]] * 2, axis=0)
-            summed = None
-        other = other[:edge_rows]
-        if edges is None:
-            edges = jnp.where(takes, other, 0.0)
-            reach = jnp.where(takes, decays[:edge_rows], 1.0)
-        else:
-            edges = edges + jnp.where(takes, reach * other, 0.0)
-            reach = jnp.where(takes, reach * decays[:edge_rows], reach)
-        decays = decays * decays
-        states = summed
-        step *= 2
-    return edges, skip
+def flip(x, step, axes="ctx"):
+    return lax.ppermute(x, axes, [(i, i ^ step) for i in range(lax.axis_size(axes))])
+
+
+def after(x, *others):
+    return lax.optimization_barrier((x, *others))[0]
 
 
 def local(query_gate, key_gate, values, upstream, skip_weight, residues, log_rates):
     context = lax.axis_size("ctx")
     groups = lax.axis_size("grp")
+    position = lax.axis_index("ctx")
     rows, channels = query_gate.shape
     total_filters, modes = residues.shape
     filters = channels // GROUP_CH
     tiles = channels // LANES
     full = rows * context
-    rows_state = tiles * modes
-    chunk = 2 * rows_state + tiles
+    half = tiles * modes
+    chunk = 2 * half + tiles
     vmem = pl.BlockSpec(memory_space=pltpu.VMEM)
     anywhere = pl.BlockSpec(memory_space=pltpu.HBM)
     shape = jax.ShapeDtypeStruct
     params = pltpu.CompilerParams(vmem_limit_bytes=16 * 1024 * 1024)
     log_rates_t, residues_t = log_rates.T, residues.T
-
+    assert groups == 4 and context >= 4 and context & (context - 1) == 0
+
+    inputs = (log_rates_t, key_gate, values, upstream, query_gate)
     states, decays, rate, mixed, carried = pl.pallas_call(
         functools.partial(states_kernel, full),
         out_shape=(
@@ -404,76 +407,127 @@
         ],
         compiler_params=params,
         name="states",
-    )(*(pltpu.with_memory_space_constraint(x, pltpu.HBM) for x in (log_rates_t, key_gate, values, upstream, query_gate)))
-
-    edges, skip_total = exchange(states, decays, rows_state)
+    )(*(pltpu.with_memory_space_constraint(x, pltpu.HBM) for x in inputs))
+    own_states = states
 
     pieces = 2
     share = tiles // pieces
     work = rows * channels * modes // pieces
-    local_sums = [
-        pl.pallas_call(
+
+    def within(n, rate):
+        return pl.pallas_call(
             functools.partial(local_kernel, n * share),
-            out_shape=shape((share, 4 * modes, LANES), F32),
-            in_specs=[vmem] * 3,
-            out_specs=vmem,
+            out_shape=(shape((share, 6 * modes, LANES), F32), shape((share, 2, modes, SUB, LANES), F32)),
+            in_specs=[vmem] * 4,
+            out_specs=(vmem,) * 2,
             scratch_shapes=[pltpu.VMEM((rows // SUB, modes // 2, SUB, LANES), F32)],
             compiler_params=params,
             cost_estimate=pl.CostEstimate(
                 flops=16 * work, transcendentals=0, bytes_accessed=8 * rows * channels // pieces
             ),
             name="within",
-        )(rate, mixed, carried)
-        for n in range(pieces)
+        )(rate, own_states, mixed, carried)
+
+    is_forward = lax.broadcasted_iota(jnp.int32, states.shape, 0) < half
+    edges = jnp.zeros((2 * half, LANES), F32)
+    reach = jnp.ones((2 * half, LANES), F32)
+    inside = []
+    step = 1
+    while 4 * step < context:
+        upper = (position & step) != 0
+        other = flip(states, step)
+        if step == 1:
+            inside.append(within(0, rate))
+            other = after(other, *inside[0])
+        takes = (is_forward == upper)[: 2 * half]
+        edges = edges + jnp.where(takes, reach * other[: 2 * half], 0.0)
+        reach = jnp.where(takes, reach * decays[: 2 * half], reach)
+        states = jnp.where(is_forward == upper, states + decays * other, decays * states + other)
+        decays = decays * decays
+        step *= 2
+    sends = [
+        jnp.concatenate(
+            [jnp.where((position & bit) == 0, states[:half], states[half : 2 * half]), states[2 * half :]],
+            axis=0,
+        )
+        for bit in (step, 2 * step)
     ]
-
-    sums, skip_grad = pl.pallas_call(
-        functools.partial(cross_kernel, full, rows, 0),
-        out_shape=(shape((context * groups, modes, 2 * filters), F32), shape((tiles, LANES), F32)),
-        in_specs=[vmem] * (4 + pieces),
-        out_specs=(vmem,) * 2,
+    others = [flip(sends[1], 3 * step), flip(sends[1], 2 * step), flip(sends[0], step)]
+    for n in range(len(inside), pieces):
+        inside.append(within(n, after(rate, states)))
+
+    edges, skip_grad, packed = pl.pallas_call(
+        functools.partial(across_kernel, full, step),
+        out_shape=(
+            shape((2 * half, LANES), F32),
+            shape((tiles, LANES), F32),
+            shape((modes, 2 * filters), F32),
+        ),
+        in_specs=[vmem] * (7 + pieces),
+        out_specs=(vmem,) * 3,
         compiler_params=params,
         name="across",
-    )(rate, states, edges, skip_total, *local_sums)
-
-    everyone = lax.all_to_all(sums, ("ctx", "grp"), split_axis=0, concat_axis=0, tiled=True)
-
-    query_grad, key_grad, value_grad = pl.pallas_call(
-        functools.partial(grads_kernel, full),
-        out_shape=(shape((rows, channels), BF16),) * 3,
-        in_specs=[vmem] * 10,
-        out_specs=(vmem,) * 3,
-        scratch_shapes=[
-            pltpu.VMEM((rows, LANES), F32),
-            pltpu.VMEM((rows, LANES), F32),
-            pltpu.VMEM((tiles, modes, LANES), F32),
-        ],
-        compiler_params=params,
-        cost_estimate=pl.CostEstimate(
-            flops=12 * rows * channels * modes, transcendentals=0, bytes_accessed=20 * rows * channels
-        ),
-        name="grads",
-    )(
-        log_rates_t,
-        residues_t,
-        skip_weight.reshape(tiles, LANES),
-        rate,
-        edges,
-        mixed,
-        carried,
-        key_gate,
-        values,
-        upstream,
-    )
+    )(decays, states, edges, reach, others[2], others[1], others[0], *(v[0] for v in inside))
+
+    def grads(n, rate, before):
+        part = pl.BlockSpec((rows, share * LANES), lambda i: (0, n))
+        whole = lambda x: pl.BlockSpec(x.shape, lambda i: (0,) * x.ndim)
+        operands = (
+            log_rates_t,
+            residues_t,
+            skip_weight.reshape(tiles, LANES),
+            rate,
+            edges,
+            mixed,
+            carried,
+            inside[n][1],
+        )
+        return pl.pallas_call(
+            functools.partial(grads_kernel, full, n * share, len(before)),
+            grid=(1,),
+            out_shape=(shape((rows, channels), BF16),) * 3,
+            in_specs=[whole(x) for x in operands] + [part] * 3 + [anywhere] * len(before),
+            out_specs=(part,) * 3,
+            scratch_shapes=[
+                pltpu.VMEM((rows, LANES), F32),
+                pltpu.VMEM((rows, LANES), F32),
+                pltpu.VMEM((tiles, modes, LANES), F32),
+            ],
+            input_output_aliases={len(operands) + 3 + k: k for k in range(len(before))},
+            compiler_params=params,
+            cost_estimate=pl.CostEstimate(
+                flops=8 * work, transcendentals=0, bytes_accessed=20 * rows * channels // pieces
+            ),
+            name="grads",
+        )(*operands, key_gate, values, upstream, *before)
+
+    outputs = grads(0, rate, ())
+    bit = context // 4
+    waits = outputs
+    while bit >= 2:
+        parts = [flip(packed, k * bit) for k in (3, 2, 1)]
+        parts[0] = after(parts[0], *waits)
+        waits = ()
+        packed = packed + (parts[0] + parts[1] + parts[2])
+        bit //= 4
+    if bit == 1:
+        packed = packed + flip(packed, 2)
+    everyone = ("ctx", "grp")
+    both = flip(packed, groups + 2, everyone), flip(packed, groups, everyone), flip(packed, 2, everyone)
+    outputs = grads(1, after(rate, packed), outputs)
+    both = (after(both[0], *outputs), *both[1:])
+    mine = jnp.concatenate([packed + both[1], both[2] + both[0]], axis=0)
+    theirs = flip(mine, 1, "grp")
+    query_grad, key_grad, value_grad = outputs
 
     residue_grad, log_rate_grad = pl.pallas_call(
-        functools.partial(final_kernel, full, groups),
+        functools.partial(final_kernel, full),
         out_shape=(shape((modes, total_filters), F32),) * 2,
-        in_specs=[vmem] * 3,
+        in_specs=[vmem] * 4,
         out_specs=(vmem,) * 2,
         compiler_params=params,
         name="final",
-    )(log_rates_t, residues_t, everyone)
+    )(log_rates_t, residues_t, mine, theirs)
     return (
         query_grad,
         key_grad,

time: 40.5 us -> 35.4 us (0.87)
  waiting for transfers between devices: 11.1 us -> 3.76 us
  starting transfers between devices: 12 us -> 15.5 us
  Pallas kernels: 15.9 us -> 14.8 us
    ppermute x3 -> x11, starting transfers between devices: 7.55 us -> 15.5 us  [flip(): lax.ppermute(x, axes, [(i, i ^ step) for i in range(lax.axis_size(axes))])]
    all_to_all x1 -> x0, waiting for transfers between devices: 4.52 us -> none  [local(): lax.all_to_all(sums, ('ctx', 'grp'), split_axis=0, concat_axis=0, tiled=T...]
    all_to_all x1 -> x0, starting transfers between devices: 4.42 us -> none  [local(): lax.all_to_all(sums, ('ctx', 'grp'), split_axis=0, concat_axis=0, tiled=T...]
    ppermute x3 -> x11, waiting for transfers between devices: 6.6 us -> 3.76 us  [flip(): lax.ppermute(x, axes, [(i, i ^ step) for i in range(lax.axis_size(axes))])]
    pallas_call x5 -> x6, Pallas kernels: 14 us -> 12.9 us  [the longest x2 6.08 us: within(): pl.pallas_call(functools.partial(local_kernel, n * share), out_shape=(sha...]
  transfers between devices with their start and end apart: 4 -> 11, of which waited for: 3 -> 5; matrix products, arithmetic and copies ran while one was open for 0% -> 0% of each run, Pallas kernels for 30% -> 33%
where the time goes in v1:
time: 35.4 us; the launch traced here: 35.1 us
  starting transfers between devices  15.5 us (44%)
  Pallas kernels  14.8 us (42%)
  waiting for transfers between devices  3.76 us (11%)
  between operations  0.76 us (2%)
    ppermute x11, starting transfers between devices, flip(): lax.ppermute(x, axes, [(i, i ^ step) for i in range(lax.axis_size(axes))])  15.5 us
    pallas_call x2, Pallas kernels, within(): pl.pallas_call(functools.partial(local_kernel, n * share), out_shape=(sha...  6.08 us
    pallas_call x2, Pallas kernels, grads(): pl.pallas_call(functools.partial(grads_kernel, full, n * share, len(befor...  5.41 us
    ppermute x11, waiting for transfers between devices, flip(): lax.ppermute(x, axes, [(i, i ^ step) for i in range(lax.axis_size(axes))])  3.76 us
    pallas_call x1, Pallas kernels, local(): pl.pallas_call(functools.partial(states_kernel, full), out_shape=(shape((...  1.9 us
    pallas_call x1, Pallas kernels, local(): pl.pallas_call(functools.partial(across_kernel, full, step), out_shape=(s...  0.73 us
  transfers between devices with their start and end apart: 11, of which 5 were waited for; matrix products, arithmetic and copies ran while one was open for 0% of the time, Pallas kernels for 33%

profile of v1, /device:TPU:0, one launch (start us, length us, event | category | flops | bytes accessed | tf_op | source)
XLA Modules:
  0.0 35.1 jit_solution(14490173429279823133)
XLA Ops:
  0.6 1.9 %states.1 = (f32[264,128]{1,0:T(8,128)S(1)}, f32[264,128]{1,0:T(8,128)S(1)}, f32[8,16,128]{2,1,0:T(8,128)S(1)}, f32[8,128,128]{2,1,0:T(8,128)S(1)}, f32[8,128,128]{2,1,0:T(8,128)S(1)}) custom-call(f32[16,256]{1,0:T(8,128)} %bitcast.7, bf16[128,1024]{1,0:T(8,128)(2,1)} %key.3, bf16[128,1024]{1,0:T(8,128)(2,1)} %values.3, bf16[128,1024]{1,0:T(8,128)(2,1)} %upstream.3, ...), custom_call_target="tpu_custom_call" | custom-call | tf_op jit(solution)/shard_map/states/pallas_call | solution.py:388
  2.5 3.0 %collective-permute-start = (f32[264,128]{1,0:T(8,128)S(1)}, f32[264,128]{1,0:T(8,128)S(1)}, u32[]{:S(2)}, u32[]{:S(2)}) collective-permute-start(f32[264,128]{1,0:T(8,128)S(1)} %get-tuple-element.33.states), channel_id=1, source_target_pairs={{0,4},{4,0},{8,12},{12,8},{16,20},{20,16},{24,28},{28,24},{1,5},{5... | collective-permute-start | bytes 405512 | tf_op jit(solution)/shard_map/ppermute | solution.py:362
  5.6 3.0 %within.2 = (f32[4,96,128]{2,1,0:T(8,128)S(1)}, f32[4,2,16,8,128]{4,3,2,1,0:T(8,128)S(1)}) custom-call(f32[8,16,128]{2,1,0:T(8,128)S(1)} %get-tuple-element.47.rate_ref, f32[264,128]{1,0:T(8,128)S(1)} %get-tuple-element.33.states, f32[8,128,128]{2,1,0:T(8,128)S(1)} %get-tuple-element.34.mixed_ref, f32[8,128,128]{2,1,0:T(8,128)S(1)} %get-tuple-element.35.carried_ref), custom_call_target="tpu_custom_call" | custom-call | flops 16777216 | bytes 524288 | tf_op jit(solution)/shard_map/within/pallas_call | solution.py:418
  8.6 0.5 %collective-permute-done = f32[264,128]{1,0:T(8,128)S(1)} collective-permute-done((f32[264,128]{1,0:T(8,128)S(1)}, f32[264,128]{1,0:T(8,128)S(1)}, u32[]{:S(2)}, u32[]{:S(2)}) %collective-permute-start) | collective-permute-done | bytes 135200 | tf_op jit(solution)/shard_map/ppermute | solution.py:362
  9.2 0.1 add_select_fusion
  9.3 3.9 %collective-permute-start.3 = (f32[136,128]{1,0:T(8,128)S(1)}, f32[136,128]{1,0:T(8,128)S(1)}, u32[]{:S(2)}, u32[]{:S(2)}) collective-permute-start(f32[136,128]{1,0:T(8,128)S(1)} %get-tuple-element.60), channel_id=1, source_target_pairs={{0,24},{4,28},{8,16},{12,20},{16,8},{20,12},{24,0},{28,4},{1,25},{... | collective-permute-start | bytes 208904 | tf_op jit(solution)/shard_map/ppermute | solution.py:362
  13.2 0.6 %collective-permute-start.1 = (f32[136,128]{1,0:T(8,128)S(1)}, f32[136,128]{1,0:T(8,128)S(1)}, u32[]{:S(2)}, u32[]{:S(2)}) collective-permute-start(f32[136,128]{1,0:T(8,128)S(1)} %get-tuple-element.61), channel_id=1, source_target_pairs={{0,8},{4,12},{8,0},{12,4},{16,24},{20,28},{24,16},{28,20},{1,9},{5... | collective-permute-start | bytes 208904 | tf_op jit(solution)/shard_map/ppermute | solution.py:362
  13.9 0.1 slice_select_fusion
  14.0 3.0 %within.3 = (f32[4,96,128]{2,1,0:T(8,128)S(1)}, f32[4,2,16,8,128]{4,3,2,1,0:T(8,128)S(1)}) custom-call(f32[8,16,128]{2,1,0:T(8,128)S(1)} %get-tuple-element.47.rate_ref, f32[264,128]{1,0:T(8,128)S(1)} %get-tuple-element.33.states, f32[8,128,128]{2,1,0:T(8,128)S(1)} %get-tuple-element.34.mixed_ref, f32[8,128,128]{2,1,0:T(8,128)S(1)} %get-tuple-element.35.carried_ref), custom_call_target="tpu_custom_call" | custom-call | flops 16777216 | bytes 524288 | tf_op jit(solution)/shard_map/within/pallas_call | solution.py:418
  17.0 1.1 %collective-permute-done.1.near = f32[136,128]{1,0:T(8,128)S(1)} collective-permute-done((f32[136,128]{1,0:T(8,128)S(1)}, f32[136,128]{1,0:T(8,128)S(1)}, u32[]{:S(2)}, u32[]{:S(2)}) %collective-permute-start.1) | collective-permute-done | bytes 69664 | tf_op jit(solution)/shard_map/ppermute | solution.py:362
  18.1 0.5 %collective-permute-done.2.middle = f32[136,128]{1,0:T(8,128)S(1)} collective-permute-done((f32[136,128]{1,0:T(8,128)S(1)}, f32[136,128]{1,0:T(8,128)S(1)}, u32[]{:S(2)}, u32[]{:S(2)}) %collective-permute-start.2) | collective-permute-done | bytes 69664 | tf_op jit(solution)/shard_map/ppermute | solution.py:362
  18.7 0.0 copy-start.4
  18.7 0.7 %across.1 = (f32[256,128]{1,0:T(8,128)S(1)}, f32[8,128]{1,0:T(8,128)}, f32[16,128]{1,0:T(8,128)S(1)}) custom-call(f32[264,128]{1,0:T(8,128)S(1)} %get-tuple-element.57.decays, f32[264,128]{1,0:T(8,128)S(1)} %get-tuple-element.56.states, f32[256,128]{1,0:T(8,128)S(1)} %get-tuple-element.63.edges_in, f32[256,128]{1,0:T(8,128)S(1)} %get-tuple-element.62.reach, ...), custom_call_target="tpu_custom_call" | custom-call | tf_op jit(solution)/shard_map/across/pallas_call | solution.py:459
  19.4 2.4 %collective-permute-start.4 = (f32[16,128]{1,0:T(8,128)S(1)}, f32[16,128]{1,0:T(8,128)S(1)}, u32[]{:S(2)}, u32[]{:S(2)}) collective-permute-start(f32[16,128]{1,0:T(8,128)S(1)} %get-tuple-element.41), channel_id=1, source_target_pairs={{0,24},{4,28},{8,16},{12,20},{16,8},{20,12},{24,0},{28,4},{1,25},{... | collective-permute-start | bytes 24584 | tf_op jit(solution)/shard_map/ppermute | solution.py:362
  21.8 0.0 collective-permute-start.6
  21.8 2.0 %collective-permute-start.5 = (f32[16,128]{1,0:T(8,128)S(1)}, f32[16,128]{1,0:T(8,128)S(1)}, u32[]{:S(2)}, u32[]{:S(2)}) collective-permute-start(f32[16,128]{1,0:T(8,128)S(1)} %get-tuple-element.41), channel_id=1, source_target_pairs={{0,16},{4,20},{8,24},{12,28},{16,0},{20,4},{24,8},{28,12},{1,17},{... | collective-permute-start | bytes 24584 | tf_op jit(solution)/shard_map/ppermute | solution.py:362
  23.8 2.7 %grads.2 = (bf16[128,1024]{1,0:T(8,128)(2,1)}, bf16[128,1024]{1,0:T(8,128)(2,1)}, bf16[128,1024]{1,0:T(8,128)(2,1)}) custom-call(f32[16,256]{1,0:T(8,128)S(1)} %bitcast.8, f32[16,256]{1,0:T(8,128)S(1)} %bitcast.11, f32[8,128]{1,0:T(8,128)S(1)} %bitcast.14, f32[8,16,128]{2,1,0:T(8,128)S(1)} %get-tuple-element.47.rate_ref, ...), custom_call_target="tpu_custom_call" | custom-call | flops 8388608 | bytes 1310720 | tf_op jit(solution)/shard_map/grads/pallas_call | solution.py:485
  26.6 2.5 %collective-permute-start.9 = (f32[16,128]{1,0:T(8,128)S(1)}, f32[16,128]{1,0:T(8,128)S(1)}, u32[]{:S(2)}, u32[]{:S(2)}) collective-permute-start(f32[16,128]{1,0:T(8,128)S(1)} %add_add_fusion), channel_id=1, source_target_pairs={{0,6},{1,7},{2,4},{3,5},{4,2},{5,3},{6,0},{7,1},{8,14},{9,15},{10,... | collective-permute-start | bytes 24584 | tf_op jit(solution)/shard_map/ppermute | solution.py:362
  29.1 0.5 %collective-permute-start.7 = (f32[16,128]{1,0:T(8,128)S(1)}, f32[16,128]{1,0:T(8,128)S(1)}, u32[]{:S(2)}, u32[]{:S(2)}) collective-permute-start(f32[16,128]{1,0:T(8,128)S(1)} %add_add_fusion), channel_id=1, source_target_pairs={{0,4},{1,5},{2,6},{3,7},{4,0},{5,1},{6,2},{7,3},{8,12},{9,13},{10,... | collective-permute-start | bytes 24584 | tf_op jit(solution)/shard_map/ppermute | solution.py:362
  29.6 0.5 %collective-permute-start.8 = (f32[16,128]{1,0:T(8,128)S(1)}, f32[16,128]{1,0:T(8,128)S(1)}, u32[]{:S(2)}, u32[]{:S(2)}) collective-permute-start(f32[16,128]{1,0:T(8,128)S(1)} %add_add_fusion), channel_id=1, source_target_pairs={{0,2},{1,3},{2,0},{3,1},{4,6},{5,7},{6,4},{7,5},{8,10},{9,11},{10,... | collective-permute-start | bytes 24584 | tf_op jit(solution)/shard_map/ppermute | solution.py:362
  30.1 2.7 %grads.3 = (bf16[128,1024]{1,0:T(8,128)(2,1)}, bf16[128,1024]{1,0:T(8,128)(2,1)}, bf16[128,1024]{1,0:T(8,128)(2,1)}) custom-call(f32[16,256]{1,0:T(8,128)S(1)} %bitcast.9, f32[16,256]{1,0:T(8,128)S(1)} %bitcast.12, f32[8,128]{1,0:T(8,128)S(1)} %bitcast.15, ...), custom_call_target="tpu_custom_call", output_to_operand_aliasing={{0}: (11, {}), {1}: (12, {}), {2}: (13, {})} | custom-call | flops 8388608 | bytes 1310720 | tf_op jit(solution)/shard_map/grads/pallas_call | solution.py:485
  32.8 0.4 %collective-permute-done.8 = f32[16,128]{1,0:T(8,128)S(1)} collective-permute-done((f32[16,128]{1,0:T(8,128)S(1)}, f32[16,128]{1,0:T(8,128)S(1)}, u32[]{:S(2)}, u32[]{:S(2)}) %collective-permute-start.8) | collective-permute-done | bytes 8224 | tf_op jit(solution)/shard_map/ppermute | solution.py:362
  33.3 1.2 %collective-permute-done.10.theirs = f32[32,128]{1,0:T(8,128)S(1)} collective-permute-done((f32[32,128]{1,0:T(8,128)S(1)}, f32[32,128]{1,0:T(8,128)S(1)}, u32[]{:S(2)}, u32[]{:S(2)}) %collective-permute-start.10) | collective-permute-done | bytes 16416 | tf_op jit(solution)/shard_map/ppermute | solution.py:362
  34.4 0.7 %final.1 = (f32[16,256]{1,0:T(8,128)}, f32[16,256]{1,0:T(8,128)}) custom-call(f32[16,256]{1,0:T(8,128)S(1)} %bitcast.10, f32[16,256]{1,0:T(8,128)S(1)} %bitcast.13, f32[32,128]{1,0:T(8,128)S(1)} %pad_maximum_fusion.2.mine, f32[32,128]{1,0:T(8,128)S(1)} %collective-permute-done.10.theirs), custom_call_target="tpu_custom_call" | custom-call | tf_op jit(solution)/shard_map/final/pallas_call | solution.py:523
  (27 shorter events, 0.1 us)
Async XLA Ops:
  2.5 6.6 %collective-permute-start = (f32[264,128]{1,0:T(8,128)S(1)}, f32[264,128]{1,0:T(8,128)S(1)}, u32[]{:S(2)}, u32[]{:S(2)}) collective-permute-start(f32[264,128]{1,0:T(8,128)S(1)} %get-tuple-element.33.states), channel_id=1, source_target_pairs={{0,4},{4,0},{8,12},{12,8},{16,20},{20,16},{24,28},{28,24},{1,5},{5... | collective-permute-start | bytes 405512 | tf_op jit(solution)/shard_map/ppermute | solution.py:362
  9.3 8.8 %collective-permute-start.3 = (f32[136,128]{1,0:T(8,128)S(1)}, f32[136,128]{1,0:T(8,128)S(1)}, u32[]{:S(2)}, u32[]{:S(2)}) collective-permute-start(f32[136,128]{1,0:T(8,128)S(1)} %get-tuple-element.60), channel_id=1, source_target_pairs={{0,24},{4,28},{8,16},{12,20},{16,8},{20,12},{24,0},{28,4},{1,25},{... | collective-permute-start | bytes 208904 | tf_op jit(solution)/shard_map/ppermute | solution.py:362
  13.2 5.5 %collective-permute-start.2 = (f32[136,128]{1,0:T(8,128)S(1)}, f32[136,128]{1,0:T(8,128)S(1)}, u32[]{:S(2)}, u32[]{:S(2)}) collective-permute-start(f32[136,128]{1,0:T(8,128)S(1)} %get-tuple-element.60), channel_id=1, source_target_pairs={{0,16},{4,20},{8,24},{12,28},{16,0},{20,4},{24,8},{28,12},{1,17},{... | collective-permute-start | bytes 208904 | tf_op jit(solution)/shard_map/ppermute | solution.py:362
  13.2 4.9 %collective-permute-start.1 = (f32[136,128]{1,0:T(8,128)S(1)}, f32[136,128]{1,0:T(8,128)S(1)}, u32[]{:S(2)}, u32[]{:S(2)}) collective-permute-start(f32[136,128]{1,0:T(8,128)S(1)} %get-tuple-element.61), channel_id=1, source_target_pairs={{0,8},{4,12},{8,0},{12,4},{16,24},{20,28},{24,16},{28,20},{1,9},{5... | collective-permute-start | bytes 208904 | tf_op jit(solution)/shard_map/ppermute | solution.py:362
  18.7 5.1 %copy-start = (bf16[128,1024]{1,0:T(8,128)(2,1)S(1)}, bf16[128,1024]{1,0:T(8,128)(2,1)}, u32[]{:S(2)}) copy-start(bf16[128,1024]{1,0:T(8,128)(2,1)} %key.3) | copy-start | bytes 786436
  18.7 5.1 %copy-start.1 = (bf16[128,1024]{1,0:T(8,128)(2,1)S(1)}, bf16[128,1024]{1,0:T(8,128)(2,1)}, u32[]{:S(2)}) copy-start(bf16[128,1024]{1,0:T(8,128)(2,1)} %values.3) | copy-start | bytes 786436
  18.7 5.1 %copy-start.2 = (bf16[128,1024]{1,0:T(8,128)(2,1)S(1)}, bf16[128,1024]{1,0:T(8,128)(2,1)}, u32[]{:S(2)}) copy-start(bf16[128,1024]{1,0:T(8,128)(2,1)} %upstream.3) | copy-start | bytes 786436
  18.7 5.2 %copy-start.3 = (f32[256,16]{0,1:T(8,128)S(1)}, f32[256,16]{0,1:T(8,128)}, u32[]{:S(2)}) copy-start(f32[256,16]{0,1:T(8,128)} %param.13) | copy-start | bytes 49156
  18.7 5.2 %copy-start.4 = (f32[256,16]{0,1:T(8,128)S(1)}, f32[256,16]{0,1:T(8,128)}, u32[]{:S(2)}) copy-start(f32[256,16]{0,1:T(8,128)} %param.12) | copy-start | bytes 49156
  19.4 4.4 %copy-start.5 = (f32[1024]{0:T(1024)S(1)}, f32[1024]{0:T(1024)}, u32[]{:S(2)}) copy-start(f32[1024]{0:T(1024)} %param.11) | copy-start | bytes 12292
  19.4 7.1 %collective-permute-start.4 = (f32[16,128]{1,0:T(8,128)S(1)}, f32[16,128]{1,0:T(8,128)S(1)}, u32[]{:S(2)}, u32[]{:S(2)}) collective-permute-start(f32[16,128]{1,0:T(8,128)S(1)} %get-tuple-element.41), channel_id=1, source_target_pairs={{0,24},{4,28},{8,16},{12,20},{16,8},{20,12},{24,0},{28,4},{1,25},{... | collective-permute-start | bytes 24584 | tf_op jit(solution)/shard_map/ppermute | solution.py:362
  21.8 4.8 %collective-permute-start.6 = (f32[16,128]{1,0:T(8,128)S(1)}, f32[16,128]{1,0:T(8,128)S(1)}, u32[]{:S(2)}, u32[]{:S(2)}) collective-permute-start(f32[16,128]{1,0:T(8,128)S(1)} %get-tuple-element.41), channel_id=1, source_target_pairs={{0,8},{4,12},{8,0},{12,4},{16,24},{20,28},{24,16},{28,20},{1,9},{5... | collective-permute-start | bytes 24584 | tf_op jit(solution)/shard_map/ppermute | solution.py:362
  21.8 4.8 %collective-permute-start.5 = (f32[16,128]{1,0:T(8,128)S(1)}, f32[16,128]{1,0:T(8,128)S(1)}, u32[]{:S(2)}, u32[]{:S(2)}) collective-permute-start(f32[16,128]{1,0:T(8,128)S(1)} %get-tuple-element.41), channel_id=1, source_target_pairs={{0,16},{4,20},{8,24},{12,28},{16,0},{20,4},{24,8},{28,12},{1,17},{... | collective-permute-start | bytes 24584 | tf_op jit(solution)/shard_map/ppermute | solution.py:362
  26.6 6.3 %collective-permute-start.9 = (f32[16,128]{1,0:T(8,128)S(1)}, f32[16,128]{1,0:T(8,128)S(1)}, u32[]{:S(2)}, u32[]{:S(2)}) collective-permute-start(f32[16,128]{1,0:T(8,128)S(1)} %add_add_fusion), channel_id=1, source_target_pairs={{0,6},{1,7},{2,4},{3,5},{4,2},{5,3},{6,0},{7,1},{8,14},{9,15},{10,... | collective-permute-start | bytes 24584 | tf_op jit(solution)/shard_map/ppermute | solution.py:362
  29.1 3.8 %collective-permute-start.7 = (f32[16,128]{1,0:T(8,128)S(1)}, f32[16,128]{1,0:T(8,128)S(1)}, u32[]{:S(2)}, u32[]{:S(2)}) collective-permute-start(f32[16,128]{1,0:T(8,128)S(1)} %add_add_fusion), channel_id=1, source_target_pairs={{0,4},{1,5},{2,6},{3,7},{4,0},{5,1},{6,2},{7,3},{8,12},{9,13},{10,... | collective-permute-start | bytes 24584 | tf_op jit(solution)/shard_map/ppermute | solution.py:362
  29.6 3.7 %collective-permute-start.8 = (f32[16,128]{1,0:T(8,128)S(1)}, f32[16,128]{1,0:T(8,128)S(1)}, u32[]{:S(2)}, u32[]{:S(2)}) collective-permute-start(f32[16,128]{1,0:T(8,128)S(1)} %add_add_fusion), channel_id=1, source_target_pairs={{0,2},{1,3},{2,0},{3,1},{4,6},{5,7},{6,4},{7,5},{8,10},{9,11},{10,... | collective-permute-start | bytes 24584 | tf_op jit(solution)/shard_map/ppermute | solution.py:362
  33.3 1.2 %collective-permute-start.10 = (f32[32,128]{1,0:T(8,128)S(1)}, f32[32,128]{1,0:T(8,128)S(1)}, u32[]{:S(2)}, u32[]{:S(2)}) collective-permute-start(f32[32,128]{1,0:T(8,128)S(1)} %pad_maximum_fusion.2.mine), channel_id=1, source_target_pairs={{0,1},{1,0},{2,3},{3,2},{4,5},{5,4},{6,7},{7,6},{8,9},{9,8},{10,11... | collective-permute-start | bytes 49160 | tf_op jit(solution)/shard_map/ppermute | solution.py:362

commit v2 on v0

v2 whole, which is shorter than its diff:
```python
import functools

import jax
import jax.numpy as jnp
from jax import lax
from jax.experimental import pallas as pl
from jax.experimental.pallas import tpu as pltpu
from jax.sharding import PartitionSpec as P

GROUP_CH = 16
LANES = 128
SUB = 8
TILE_FILTERS = LANES // GROUP_CH
HIGHEST = lax.Precision.HIGHEST
F32 = jnp.float32
BF16 = jnp.bfloat16


def own_columns(table, filters):
    total = table.shape[1]
    start = lax.axis_index("grp") * filters
    return pltpu.roll(table, lax.rem(total - start, total), 1)[:, :filters]


def group_mask(filters, channels):
    row = lax.broadcasted_iota(jnp.int32, (filters, channels), 0)
    col = lax.broadcasted_iota(jnp.int32, (filters, channels), 1)
    return jnp.where(row == lax.div(col, GROUP_CH), 1.0, 0.0).astype(F32)


def per_channel(table, mask):
    return jnp.dot(table, mask, precision=HIGHEST, preferred_element_type=F32)


def split(x):
    high = x.astype(BF16)
    return high, (x - high.astype(F32)).astype(BF16)


def wide_dot(a_high, a_low, b_high, b_low):
    dot = functools.partial(jnp.dot, preferred_element_type=F32)
    return dot(a_high, b_high) + (dot(a_high, b_low) + dot(a_low, b_high))


def spread(row):
    return jnp.broadcast_to(row, (SUB, LANES))


def sub_ends(x_ref, ct, decay, steps, reverse):
    order = range(steps - 1, -1, -1) if reverse else range(steps)
    state = None
    for i in order:
        x = x_ref[ct, pl.ds(i, SUB, stride=steps), :]
        state = [x] * len(decay) if state is None else [d * s + x for d, s in zip(decay, state)]
    return state


def sub_starts(ends, jumps, reverse):
    index = lax.broadcasted_iota(jnp.int32, (SUB, LANES), 0)
    if reverse:
        index = SUB - 1 - index
    shift = lambda v, n: pltpu.roll(v, SUB - n if reverse else n, 0)
    out = []
    for end, jump in zip(ends, jumps):
        x = jnp.where(index == 0, 0.0, shift(end, 1))
        for n in (1, 2, 4):
            x = x + jnp.where(index >= n, jump, 0.0) * shift(x, n)
            jump = jump * jump
        out.append(x)
    return out


def fold_modes(products, modes):
    lane_filter = lax.div(lax.broadcasted_iota(jnp.int32, (modes, LANES), 1), GROUP_CH)
    parts = [
        jnp.where(lane_filter == f, products[f * modes : (f + 1) * modes, :], 0.0)
        for f in range(TILE_FILTERS)
    ]
    while len(parts) > 1:
        parts = [a + b for a, b in zip(parts[::2], parts[1::2])]
    return parts[0]


def states_kernel(
    full,
    log_rates_h,
    key_h,
    values_h,
    upstream_h,
    query_h,
    states,
    rate_out,
    mixed_out,
    carried_out,
    skip_out,
    rates_s,
    key,
    values,
    upstream,
    query,
    weight_s,
    sems,
):
    rows, channels = key.shape
    tiles = channels // LANES
    filters = channels // GROUP_CH
    modes = log_rates_h.shape[0]
    part = tiles // 2 * modes
    wide = TILE_FILTERS * modes
    copies = [
        pltpu.make_async_copy(src, dst, sems.at[n])
        for n, (src, dst) in enumerate(
            (
                (log_rates_h, rates_s),
                (key_h, key),
                (values_h, values),
                (upstream_h, upstream),
                (query_h, query),
            )
        )
    ]
    for copy in copies:
        copy.start()
    copies[0].wait()
    step_rates = own_columns(jnp.exp(rates_s[...]), filters) * (1.0 / full)
    channel_rates = per_channel(step_rates, group_mask(filters, channels))
    time = lax.broadcasted_iota(jnp.int32, (modes, rows), 1).astype(F32)
    back_time = float(rows - 1) - time
    for f in range(filters):
        rate = jnp.broadcast_to(step_rates[:, f : f + 1], (modes, rows))
        ct, row = f // TILE_FILTERS, (f % TILE_FILTERS) * modes
        for way, away in enumerate((back_time, time)):
            weight = jnp.exp(-rate * away)
            for n, high_low in enumerate((split(weight), split(weight * away))):
                at = slice(n * wide + row, n * wide + row + modes)
                weight_s[ct, 2 * way, at, :] = high_low[0]
                weight_s[ct, 2 * way + 1, at, :] = high_low[1]
    for ct in range(tiles):
        rate_out[ct] = channel_rates[:, ct * LANES : (ct + 1) * LANES]
    for copy in copies[1:]:
        copy.wait()
    for ct in range(tiles):
        lanes = slice(ct * LANES, (ct + 1) * LANES)
        mixed = key[:, lanes].astype(F32) * values[:, lanes].astype(F32)
        carried = upstream[:, lanes].astype(F32) * query[:, lanes].astype(F32)
        mixed_out[ct] = mixed
        carried_out[ct] = carried
        base = ct // (tiles // 2) * 4 * part + ct % (tiles // 2) * modes
        for way, x in enumerate((mixed, carried)):
            products = wide_dot(weight_s[ct, 2 * way], weight_s[ct, 2 * way + 1], *split(x))
            for n in range(2):
                at = base + (2 * way + n) * part
                states[at : at + modes, :] = fold_modes(products[n * wide : (n + 1) * wide], modes)
        skip_out[ct : ct + 1, :] = jnp.sum(mixed * carried, axis=0, keepdims=True)


def by_filter(firsts, seconds, first_filter, filters):
    modes = firsts[0].shape[0]
    both = jnp.concatenate([jnp.concatenate(v, axis=1) for v in (firsts, seconds)], axis=0)
    channels = both.shape[1]
    row = lax.broadcasted_iota(jnp.int32, (filters, channels), 0)
    col = lax.broadcasted_iota(jnp.int32, (filters, channels), 1)
    mask = jnp.where(row == first_filter + lax.div(col, GROUP_CH), 1.0, 0.0).astype(BF16)
    high, rest = split(both)
    middle, low = split(both - high.astype(F32))
    summed = lax.dot_general(
        jnp.concatenate([high, middle, low], axis=0),
        mask,
        (((1,), (1,)), ((), ())),
        preferred_element_type=F32,
    )
    summed = summed[: 2 * modes] + summed[2 * modes : 4 * modes] + summed[4 * modes :]
    return jnp.concatenate([summed[:modes], summed[modes:]], axis=1)


def within_kernel(rate_ref, mixed_ref, carried_ref, skip, sums, starts, after_s, first_s, second_s):
    tiles, rows, _ = mixed_ref.shape
    modes = rate_ref.shape[1]
    steps = rows // SUB
    half = modes // 2

    def tile(ct, _):
        rate = rate_ref[ct]
        for lo in range(0, modes, half):
            rate_rows = [spread(rate[m : m + 1, :]) for m in range(lo, lo + half)]
            decay = [jnp.exp(-r) for r in rate_rows]
            jumps = [jnp.exp(-r * float(steps)) for r in rate_rows]
            state = sub_starts(sub_ends(carried_ref, ct, decay, steps, True), jumps, True)
            for m in range(half):
                starts[ct, 1, lo + m] = state[m]
            for i in range(steps - 1, -1, -1):
                c = carried_ref[ct, pl.ds(i, SUB, stride=steps), :]
                state = [d * s for d, s in zip(decay, state)]
                for m in range(half):
                    after_s[i, m] = state[m]
                state = [a + c for a in state]
            state = sub_starts(sub_ends(mixed_ref, ct, decay, steps, False), jumps, False)
            for m in range(half):
                starts[ct, 0, lo + m] = state[m]
            first = [jnp.zeros((SUB, LANES), F32)] * half
            second = [jnp.zeros((SUB, LANES), F32)] * half
            for i in range(steps):
                x = mixed_ref[ct, pl.ds(i, SUB, stride=steps), :]
                c = carried_ref[ct, pl.ds(i, SUB, stride=steps), :]
                state = [d * s + x for d, s in zip(decay, state)]
                first = [f + c * s for f, s in zip(first, state)]
                second = [f + after_s[i, m] * state[m] for m, f in enumerate(second)]
            for ref, values in ((first_s, first), (second_s, second)):
                ref[ct, lo : lo + half, :] = jnp.concatenate(
                    [jnp.sum(v, axis=0, keepdims=True) for v in values], axis=0
                )
        return 0

    lax.fori_loop(0, tiles, tile, 0)
    packet = by_filter(
        [first_s[ct] for ct in range(tiles)],
        [second_s[ct] for ct in range(tiles)],
        0,
        tiles * TILE_FILTERS,
    )
    sums[:modes, :] = packet
    sums[modes:, :] = skip[...]


def spans_join(own, other, rate, upper, span):
    low = [jnp.where(upper, o, w) for w, o in zip(own, other)]
    high = [jnp.where(upper, w, o) for w, o in zip(own, other)]
    decay = jnp.exp(-rate)
    first = decay * (low[0] * high[2])
    second = decay * (low[1] * high[2] + low[0] * (high[2] + high[3]))
    far = jnp.exp(-rate * float(span))
    joined = (
        far * low[0] + high[0],
        far * (low[1] + float(span) * low[0]) + high[1],
        low[2] + far * high[2],
        low[3] + far * (high[3] + float(span) * high[2]),
    )
    return joined, first, second


def border_sums(first, second, tiles, modes):
    cut = lambda v: [v[n * modes : (n + 1) * modes, :] for n in range(tiles // 2)]
    begin = (lax.axis_index("ctx") & 1) * (tiles // 2 * TILE_FILTERS)
    return by_filter(cut(first), cut(second), begin, tiles * TILE_FILTERS)


def half_rates(rate_ref):
    tiles, modes, _ = rate_ref.shape
    begin = (lax.axis_index("ctx") & 1) * (tiles // 2)
    return jnp.concatenate([rate_ref[begin + n] for n in range(tiles // 2)], axis=0)


def join_kernel(rows, step, is_last_next, rate_ref, own_ref, other_ref, *refs):
    tiles, modes, _ = rate_ref.shape
    part = tiles // 2 * modes
    if step == 1:
        sums_ref, joined_ref, borders_ref, *send = refs
        begin = (lax.axis_index("ctx") & 1) * (4 * part)
        own = [own_ref[pl.ds(pl.multiple_of(begin + q * part, part), part), :] for q in range(4)]
        sums = sums_ref[...]
    else:
        old_borders, joined_ref, borders_ref, *send = refs
        own = [own_ref[q * part : (q + 1) * part, :] for q in range(4)]
        sums = own_ref[4 * part :, :] + other_ref[4 * part :, :]
    other = [other_ref[q * part : (q + 1) * part, :] for q in range(4)]
    position = lax.axis_index("ctx")
    upper = (position & step) != 0
    rate = half_rates(rate_ref)
    joined, first, second = spans_join(own, other, rate, upper, rows * step)
    for q in range(4):
        joined_ref[q * part : (q + 1) * part, :] = joined[q]
    sums = jnp.concatenate([sums[:modes] + border_sums(first, second, tiles, modes), sums[modes:]], axis=0)
    joined_ref[4 * part :, :] = sums
    if step == 1:
        borders_ref[...] = jnp.zeros_like(borders_ref)
    else:
        borders_ref[...] = add_borders(
            rows, step, rate, [old_borders[:part, :], old_borders[part:, :]], other[0], other[2]
        )
    if is_last_next:
        next_upper = (position & (2 * step)) != 0
        for q in range(2):
            send[0][q * part : (q + 1) * part, :] = jnp.where(next_upper, joined[2 + q], joined[q])
        send[0][2 * part :, :] = sums


def add_borders(rows, step, rate, borders, forward, backward):
    position = lax.axis_index("ctx")
    upper = (position & step) != 0
    before = ((position & (step - 1)) >> 1).astype(F32) * float(2 * rows)
    behind = float(rows * (step - 2)) - before
    return jnp.concatenate(
        [
            borders[0] + jnp.where(upper, jnp.exp(-rate * before) * forward, 0.0),
            borders[1] + jnp.where(upper, 0.0, jnp.exp(-rate * behind) * backward),
        ],
        axis=0,
    )


def last_join_kernel(
    rows, step, rate_ref, own_ref, other_ref, borders_ref, states_ref, partner_ref, mine_ref, back_ref
):
    tiles, modes, _ = rate_ref.shape
    part = tiles // 2 * modes
    position = lax.axis_index("ctx")
    upper = (position & step) != 0
    rate = half_rates(rate_ref)
    own = [own_ref[q * part : (q + 1) * part, :] for q in range(4)]
    other = [other_ref[q * part : (q + 1) * part, :] for q in range(2)]
    _, first, second = spans_join(own, other + other, rate, upper, rows * step)
    packet = border_sums(first, second, tiles, modes)
    borders = add_borders(
        rows, step, rate, [borders_ref[:part, :], borders_ref[part:, :]], other[0], other[0]
    )
    incoming, outgoing = borders[:part], borders[part:]
    far = jnp.exp(-rate * float(rows))
    begin = (position & 1) * (4 * part)
    pick = lambda q: states_ref[pl.ds(pl.multiple_of(begin + q * part, part), part), :]
    second_block = (position & 1) != 0
    through = far * incoming
    across = far * outgoing
    for ref, is_second, forward, backward in (
        (mine_ref, second_block, partner_ref[:part, :], partner_ref[2 * part : 3 * part, :]),
        (back_ref, jnp.logical_not(second_block), pick(0), pick(2)),
    ):
        ref[:part, :] = jnp.where(is_second, through + forward, incoming)
        ref[part : 2 * part, :] = jnp.where(is_second, outgoing, across + backward)
        sums = own_ref[4 * part :, :] + other_ref[2 * part :, :]
        ref[2 * part : 2 * part + modes, :] = sums[:modes] + packet
        ref[2 * part + modes :, :] = sums[modes:]


def block_kernel(
    full, log_rates, residues, skip_weight, rate_ref, mixed_ref, carried_ref, starts, scales, results
):
    tiles, rows, _ = mixed_ref.shape
    modes = rate_ref.shape[1]
    filters = tiles * TILE_FILTERS
    steps = rows // SUB
    half = modes // 2
    scaled = own_columns(residues[...], filters) * jnp.sqrt(
        jnp.exp(own_columns(log_rates[...], filters)) / full
    )
    scaled = per_channel(scaled, group_mask(filters, tiles * LANES))
    for n in range(tiles):
        scales[n] = scaled[:, n * LANES : (n + 1) * LANES]

    def tile(ct, _):
        rate = rate_ref[ct]
        scale = scales[ct]
        weight = spread(skip_weight[pl.ds(ct, 1), :])
        for lo in range(0, modes, half):
            decay = [jnp.exp(-spread(rate[m : m + 1, :])) for m in range(lo, lo + half)]
            gains = [spread(scale[m : m + 1, :]) for m in range(lo, lo + half)]
            for way, x_ref in enumerate((mixed_ref, carried_ref)):
                state = [starts[ct, way, lo + m] for m in range(half)]
                for i in range(steps - 1, -1, -1) if way else range(steps):
                    at = pl.ds(i, SUB, stride=steps)
                    x = x_ref[ct, at, :]
                    state = [d * s + x for d, s in zip(decay, state)]
                    terms = [g * s for g, s in zip(gains, state)]
                    terms.append(results[ct, way, at, :] if lo > 0 else weight * x)
                    while len(terms) > 1:
                        odd = terms[len(terms) // 2 * 2 :]
                        terms = [a + b for a, b in zip(terms[::2], terms[1::2])] + odd
                    results[ct, way, at, :] = terms[0]
        return 0

    lax.fori_loop(0, tiles, tile, 0)


def grads_kernel(full, mine, theirs, rate_ref, scale_ref, results, key, values, upstream, *refs):
    query_grad, key_grad, value_grad, skip_grad = refs
    tiles, modes, _ = scale_ref.shape
    rows = key.shape[0]
    share = tiles // 2
    part = share * modes
    skip_rows = slice(2 * part + modes, 2 * part + modes + tiles)
    skip_grad[...] = (mine[skip_rows, :] + theirs[skip_rows, :]) / jnp.sqrt(jnp.float32(full))
    second_half = (lax.axis_index("ctx") & 1) != 0
    lane = lax.broadcasted_iota(jnp.int32, (modes, LANES), 1)
    own_mode = lax.broadcasted_iota(jnp.int32, (modes, LANES), 0) == lax.rem(lane, modes)
    lane_filter = lax.div(lane, GROUP_CH)
    time = lax.broadcasted_iota(jnp.int32, (rows, LANES), 0).astype(F32)

    def piece(p):
        is_mine = second_half if p else jnp.logical_not(second_half)
        for n in range(share):
            ct = p * share + n
            rate = rate_ref[ct]
            rate_row = jnp.sum(jnp.where(own_mode, rate, 0.0), axis=0, keepdims=True)
            parts = []
            for offset, away in ((0, time + 1.0), (part, float(rows) - time)):
                at = slice(offset + n * modes, offset + (n + 1) * modes)
                edge = scale_ref[ct] * jnp.where(is_mine, mine[at, :], theirs[at, :])
                spaced = jnp.concatenate(
                    [jnp.where(lane_filter == f, edge, 0.0) for f in range(TILE_FILTERS)], axis=0
                )
                parts.append(wide_dot(*split(jnp.exp(-rate_row * away)), *split(spaced)))
            lanes = slice(n * LANES, (n + 1) * LANES)
            query_grad[:, lanes] = (
                upstream[:, lanes].astype(F32) * (results[ct, 0] + parts[0])
            ).astype(query_grad.dtype)
            mixed_grad = results[ct, 1] + parts[1]
            key_grad[:, lanes] = (mixed_grad * values[:, lanes].astype(F32)).astype(key_grad.dtype)
            value_grad[:, lanes] = (mixed_grad * key[:, lanes].astype(F32)).astype(value_grad.dtype)

    for p in range(2):
        pl.when(pl.program_id(0) == p)(functools.partial(piece, p))


def final_kernel(full, log_rates, residues, *refs):
    *by_distance, residue_grad, log_rate_grad = refs
    total_filters = log_rates.shape[1]
    filters = by_distance[0].shape[1] // 2
    group = lax.axis_index("grp")
    by_distance = [ref[...] for ref in by_distance]
    totals = []
    for g in range(total_filters // filters):
        total = by_distance[0]
        for k in range(1, len(by_distance)):
            total = jnp.where((group ^ k) == g, by_distance[k], total)
        totals.append(total)
    first_sum = jnp.concatenate([t[:, :filters] for t in totals], axis=1)
    second_sum = jnp.concatenate([t[:, filters:] for t in totals], axis=1) * (1.0 / full)
    rates = jnp.exp(log_rates[...])
    root = jnp.sqrt(rates / full)
    scale_root = jnp.sqrt(jnp.float32(full))
    residue_grad[...] = root * first_sum / scale_root
    log_rate_grad[...] = residues[...] * root * (0.5 * first_sum - rates * second_sum) / scale_root


def flip(x, step, axis="ctx"):
    return lax.ppermute(x, axis, [(i, i ^ step) for i in range(lax.axis_size(axis))])


def after(x, *others):
    return lax.optimization_barrier((x, *others))[0]


def local(query_gate, key_gate, values, upstream, skip_weight, residues, log_rates):
    context = lax.axis_size("ctx")
    groups = lax.axis_size("grp")
    position = lax.axis_index("ctx")
    rows, channels = query_gate.shape
    total_filters, modes = residues.shape
    filters = channels // GROUP_CH
    tiles = channels // LANES
    full = rows * context
    part = tiles // 2 * modes
    tail = modes + tiles
    assert context >= 4 and context & (context - 1) == 0 and groups & (groups - 1) == 0
    vmem = pl.BlockSpec(memory_space=pltpu.VMEM)
    in_hbm = pl.BlockSpec(memory_space=pltpu.HBM)
    shape = lambda *dims: jax.ShapeDtypeStruct(dims, F32)
    params = pltpu.CompilerParams(vmem_limit_bytes=16 * 1024 * 1024)
    log_rates_t, residues_t = log_rates.T, residues.T

    def call(name, kernel, out_shape, operands, scratch=(), flops=0):
        return pl.pallas_call(
            kernel,
            out_shape=out_shape,
            in_specs=[vmem] * len(operands),
            out_specs=(vmem,) * len(out_shape),
            scratch_shapes=[pltpu.VMEM(dims, F32) for dims in scratch],
            compiler_params=params,
            cost_estimate=pl.CostEstimate(flops=flops, transcendentals=0, bytes_accessed=flops // 4),
            name=name,
        )(*operands)

    inputs = (log_rates_t, key_gate, values, upstream, query_gate)
    states, rate, mixed, carried, skip = pl.pallas_call(
        functools.partial(states_kernel, full),
        out_shape=(
            shape(8 * part, LANES),
            shape(tiles, modes, LANES),
            shape(tiles, rows, LANES),
            shape(tiles, rows, LANES),
            shape(tiles, LANES),
        ),
        in_specs=[in_hbm] * 5,
        out_specs=(vmem,) * 5,
        scratch_shapes=[
            pltpu.VMEM((modes, total_filters), F32),
            pltpu.VMEM((rows, channels), BF16),
            pltpu.VMEM((rows, channels), BF16),
            pltpu.VMEM((rows, channels), BF16),
            pltpu.VMEM((rows, channels), BF16),
            pltpu.VMEM((tiles, 4, 2 * TILE_FILTERS * modes, rows), BF16),
            pltpu.SemaphoreType.DMA((5,)),
        ],
        compiler_params=params,
        name="states",
    )(*(pltpu.with_memory_space_constraint(x, pltpu.HBM) for x in inputs))
    work = rows * channels * modes

    other_half = lax.dynamic_slice_in_dim(states, (1 - (position & 1)) * (4 * part), 4 * part, 0)
    partner = flip(other_half, 1)
    sums, starts = call(
        "within",
        within_kernel,
        (shape(tail, LANES), shape(tiles, 2, modes, SUB, LANES)),
        (rate, mixed, carried, skip),
        ((rows // SUB, modes // 2, SUB, LANES), (tiles, modes, LANES), (tiles, modes, LANES)),
        12 * work,
    )
    scale = results = None
    step = 1
    own, other, extra = states, after(partner, sums), (sums,)
    while 2 * step < context:
        is_last_next = 4 * step >= context
        own, borders, *send = call(
            "join",
            functools.partial(join_kernel, rows, step, is_last_next),
            (shape(4 * part + tail, LANES), shape(2 * part, LANES))
            + ((shape(2 * part + tail, LANES),) if is_last_next else ()),
            (rate, own, other, *extra),
        )
        other = flip(send[0] if send else own, 2 * step)
        if step == 1:
            scale, results = call(
                "block",
                functools.partial(block_kernel, full),
                (shape(tiles, modes, LANES), shape(tiles, 2, rows, LANES)),
                (
                    log_rates_t,
                    residues_t,
                    skip_weight.reshape(tiles, LANES),
                    after(rate, own),
                    mixed,
                    carried,
                    starts,
                ),
                (),
                8 * work,
            )
            other = after(other, results)
        extra = (borders,)
        step *= 2
    mine, back = call(
        "last_join",
        functools.partial(last_join_kernel, rows, step),
        (shape(2 * part + tail, LANES),) * 2,
        (rate, own, other, borders, states, partner),
    )
    theirs = flip(back, 1)

    packed = mine[2 * part : 2 * part + modes] + theirs[2 * part : 2 * part + modes]
    gathered = [flip(packed, k, "grp") for k in range(1, groups)]
    columns = pl.BlockSpec((rows, channels // 2), lambda i: (0, i))
    outputs = pl.pallas_call(
        functools.partial(grads_kernel, full),
        grid=(2,),
        out_shape=(jax.ShapeDtypeStruct((rows, channels), BF16),) * 3 + (shape(tiles, LANES),),
        in_specs=[vmem] * 5 + [columns] * 3,
        out_specs=(columns,) * 3 + (pl.BlockSpec((tiles, LANES), lambda i: (0, 0)),),
        compiler_params=params,
        cost_estimate=pl.CostEstimate(
            flops=4 * work, transcendentals=0, bytes_accessed=20 * rows * channels
        ),
        name="grads",
    )(mine, theirs, rate, scale, results, key_gate, values, upstream)
    query_grad, key_grad, value_grad, skip_grad = outputs
    gathered[0] = after(gathered[0], *outputs)
    residue_grad, log_rate_grad = call(
        "final",
        functools.partial(final_kernel, full),
        (shape(modes, total_filters),) * 2,
        (log_rates_t, residues_t, packed, *gathered),
    )
    return (
        query_grad,
        key_grad,
        value_grad,
        skip_grad.reshape(channels),
        residue_grad.T,
        log_rate_grad.T,
    )


def solution(mesh):
    placed = (
        P("ctx", "grp"),
        P("ctx", "grp"),
        P("ctx", "grp"),
        P("ctx", "grp"),
        P("grp"),
        P(),
        P(),
    )
    return jax.shard_map(
        local,
        mesh=mesh,
        in_specs=placed,
        out_specs=(P("ctx", "grp"), P("ctx", "grp"), P("ctx", "grp"), P("grp"), P(), P()),
        check_vma=False,
    )
```

time: 40.5 us -> 33.1 us (0.82)
  waiting for transfers between devices: 11.1 us -> 8.58 us
  starting transfers between devices: 12 us -> 9.74 us
  Pallas kernels: 15.9 us -> 13.7 us
  other arithmetic: 0.44 us -> 0.01 us
    all_to_all x1 -> x0, waiting for transfers between devices: 4.52 us -> none  [local(): lax.all_to_all(sums, ('ctx', 'grp'), split_axis=0, concat_axis=0, tiled=T...]
    all_to_all x1 -> x0, starting transfers between devices: 4.42 us -> none  [local(): lax.all_to_all(sums, ('ctx', 'grp'), split_axis=0, concat_axis=0, tiled=T...]
    ppermute x3 -> x7, starting transfers between devices: 7.55 us -> 9.74 us  [flip(): lax.ppermute(x, axis, [(i, i ^ step) for i in range(lax.axis_size(axis))])]
    pallas_call x6 -> x8, Pallas kernels: 15.9 us -> 13.7 us  [the longest x6 9.59 us: call(): pl.pallas_call(kernel, out_shape=out_shape, in_specs=[vmem] * len(operand...]
    ppermute x3 -> x7, waiting for transfers between devices: 6.6 us -> 8.58 us  [flip(): lax.ppermute(x, axis, [(i, i ^ step) for i in range(lax.axis_size(axis))])]
  transfers between devices with their start and end apart: 4 -> 7, of which waited for: 3 -> 4; matrix products, arithmetic and copies ran while one was open for 0% -> 0% of each run, Pallas kernels for 30% -> 30%
where the time goes in v2:
time: 33.1 us; the launch traced here: 32.8 us
  Pallas kernels  13.7 us (41%)
  starting transfers between devices  9.74 us (29%)
  waiting for transfers between devices  8.58 us (26%)
  between operations  0.69 us (2%)
    ppermute x7, starting transfers between devices, flip(): lax.ppermute(x, axis, [(i, i ^ step) for i in range(lax.axis_size(axis))])  9.74 us
    pallas_call x6, Pallas kernels, call(): pl.pallas_call(kernel, out_shape=out_shape, in_specs=[vmem] * len(operand...  9.59 us
    ppermute x7, waiting for transfers between devices, flip(): lax.ppermute(x, axis, [(i, i ^ step) for i in range(lax.axis_size(axis))])  8.58 us
    pallas_call x1, Pallas kernels, local(): pl.pallas_call(functools.partial(states_kernel, full), out_shape=(shape(8...  2.32 us
    pallas_call x1, Pallas kernels, local(): pl.pallas_call(functools.partial(grads_kernel, full), grid=(2,), out_shap...  1.76 us
  transfers between devices with their start and end apart: 7, of which 4 were waited for; matrix products, arithmetic and copies ran while one was open for 0% of the time, Pallas kernels for 30%

profile of v2, /device:TPU:0, one launch (start us, length us, event | category | flops | bytes accessed | tf_op | source)
XLA Modules:
  0.0 32.8 jit_solution(15103622633467888717)
XLA Ops:
  0.6 2.3 %states.1 = (f32[512,128]{1,0:T(8,128)S(1)}, f32[8,16,128]{2,1,0:T(8,128)S(1)}, f32[8,128,128]{2,1,0:T(8,128)S(1)}, f32[8,128,128]{2,1,0:T(8,128)S(1)}, f32[8,128]{1,0:T(8,128)S(1)}) custom-call(f32[16,256]{1,0:T(8,128)} %bitcast.6, bf16[128,1024]{1,0:T(8,128)(2,1)} %key.1, bf16[128,1024]{1,0:T(8,128)(2,1)} %values.1, bf16[128,1024]{1,0:T(8,128)(2,1)} %upstream.1, ...), custom_call_target="tpu_custom_call" | custom-call | tf_op jit(solution)/shard_map/states/pallas_call | solution.py:473
  3.0 3.0 %collective-permute-start = (f32[256,128]{1,0:T(8,128)S(1)}, f32[256,128]{1,0:T(8,128)S(1)}, u32[]{:S(2)}, u32[]{:S(2)}) collective-permute-start(f32[256,128]{1,0:T(8,128)S(1)} %constant_dynamic-slice_fusion), channel_id=1, source_target_pairs={{0,4},{4,0},{8,12},{12,8},{16,20},{20,16},{24,28},{28,24},{1,5},{5... | collective-permute-start | bytes 393224 | tf_op jit(solution)/shard_map/ppermute | solution.py:435
  6.0 5.0 %within.1 = (f32[24,128]{1,0:T(8,128)S(1)}, f32[8,2,16,8,128]{4,3,2,1,0:T(8,128)S(1)}) custom-call(f32[8,16,128]{2,1,0:T(8,128)S(1)} %get-tuple-element.40.rate_ref, f32[8,128,128]{2,1,0:T(8,128)S(1)} %get-tuple-element.34.mixed_ref, f32[8,128,128]{2,1,0:T(8,128)S(1)} %get-tuple-element.35.carried_ref, f32[8,128]{1,0:T(8,128)S(1)} %get-tuple-element.36.skip), custom_call_target="tpu_custom_call" | custom-call | flops 25165824 | bytes 6291456 | tf_op jit(solution)/shard_map/within/pallas_call | solution.py:461
  11.0 0.0 collective-permute-done.other_ref.partner_ref
  11.0 0.0 copy-start.4
  11.0 0.2 join.2
  11.3 1.6 %collective-permute-start.1 = (f32[280,128]{1,0:T(8,128)S(1)}, f32[280,128]{1,0:T(8,128)S(1)}, u32[]{:S(2)}, u32[]{:S(2)}) collective-permute-start(f32[280,128]{1,0:T(8,128)S(1)} %get-tuple-element.39.own_ref), channel_id=1, source_target_pairs={{0,8},{4,12},{8,0},{12,4},{16,24},{20,28},{24,16},{28,20},{1,9},{5... | collective-permute-start | bytes 430088 | tf_op jit(solution)/shard_map/ppermute | solution.py:435
  12.9 0.0 copy-done.3
  12.9 3.1 %block.1 = (f32[8,16,128]{2,1,0:T(8,128)S(1)}, f32[8,2,128,128]{3,2,1,0:T(8,128)S(1)}) custom-call(f32[16,256]{1,0:T(8,128)S(1)} %bitcast.7, f32[16,256]{1,0:T(8,128)S(1)} %bitcast.9, f32[8,128]{1,0:T(8,128)S(1)} %bitcast.11, f32[8,16,128]{2,1,0:T(8,128)S(1)} %get-tuple-element.40.rate_ref, f32[8,128,128]{2,1,0:T(8,128)S(1)} %get-tuple-element.34.mixed_ref, ...), custom_call_target="tpu_custom_call" | custom-call | flops 16777216 | bytes 4194304 | tf_op jit(solution)/shard_map/block/pallas_call | solution.py:461
  16.1 0.5 %collective-permute-done.1.other_ref = f32[280,128]{1,0:T(8,128)S(1)} collective-permute-done((f32[280,128]{1,0:T(8,128)S(1)}, f32[280,128]{1,0:T(8,128)S(1)}, u32[]{:S(2)}, u32[]{:S(2)}) %collective-permute-start.1) | collective-permute-done | bytes 143392 | tf_op jit(solution)/shard_map/ppermute | solution.py:435
  16.5 0.3 join.3
  16.8 2.6 %collective-permute-start.2 = (f32[152,128]{1,0:T(8,128)S(1)}, f32[152,128]{1,0:T(8,128)S(1)}, u32[]{:S(2)}, u32[]{:S(2)}) collective-permute-start(f32[152,128]{1,0:T(8,128)S(1)} %get-tuple-element.46), channel_id=1, source_target_pairs={{0,16},{4,20},{8,24},{12,28},{16,0},{20,4},{24,8},{28,12},{1,17},{... | collective-permute-start | bytes 233480 | tf_op jit(solution)/shard_map/ppermute | solution.py:435
  19.4 2.7 %collective-permute-done.2.other_ref = f32[152,128]{1,0:T(8,128)S(1)} collective-permute-done((f32[152,128]{1,0:T(8,128)S(1)}, f32[152,128]{1,0:T(8,128)S(1)}, u32[]{:S(2)}, u32[]{:S(2)}) %collective-permute-start.2) | collective-permute-done | bytes 77856 | tf_op jit(solution)/shard_map/ppermute | solution.py:435
  22.1 0.3 last_join.1
  22.4 0.4 %collective-permute-start.3 = (f32[152,128]{1,0:T(8,128)S(1)}, f32[152,128]{1,0:T(8,128)S(1)}, u32[]{:S(2)}, u32[]{:S(2)}) collective-permute-start(f32[152,128]{1,0:T(8,128)S(1)} %get-tuple-element.49), channel_id=1, source_target_pairs={{0,4},{4,0},{8,12},{12,8},{16,20},{20,16},{24,28},{28,24},{1,5},{5... | collective-permute-start | bytes 233480 | tf_op jit(solution)/shard_map/ppermute | solution.py:435
  22.7 4.1 %collective-permute-done.3.theirs = f32[152,128]{1,0:T(8,128)S(1)} collective-permute-done((f32[152,128]{1,0:T(8,128)S(1)}, f32[152,128]{1,0:T(8,128)S(1)}, u32[]{:S(2)}, u32[]{:S(2)}) %collective-permute-start.3) | collective-permute-done | bytes 77856 | tf_op jit(solution)/shard_map/ppermute | solution.py:435
  26.8 0.0 collective-permute-start.4
  26.8 1.6 %collective-permute-start.6 = (f32[16,128]{1,0:T(8,128)S(1)}, f32[16,128]{1,0:T(8,128)S(1)}, u32[]{:S(2)}, u32[]{:S(2)}) collective-permute-start(f32[16,128]{1,0:T(8,128)S(1)} %slice_add_fusion.refs_0_), channel_id=1, source_target_pairs={{0,3},{1,2},{2,1},{3,0},{4,7},{5,6},{6,5},{7,4},{8,11},{9,10},{10,... | collective-permute-start | bytes 24584 | tf_op jit(solution)/shard_map/ppermute | solution.py:435
  28.4 0.5 %collective-permute-start.5 = (f32[16,128]{1,0:T(8,128)S(1)}, f32[16,128]{1,0:T(8,128)S(1)}, u32[]{:S(2)}, u32[]{:S(2)}) collective-permute-start(f32[16,128]{1,0:T(8,128)S(1)} %slice_add_fusion.refs_0_), channel_id=1, source_target_pairs={{0,2},{1,3},{2,0},{3,1},{4,6},{5,7},{6,4},{7,5},{8,10},{9,11},{10,... | collective-permute-start | bytes 24584 | tf_op jit(solution)/shard_map/ppermute | solution.py:435
  29.0 1.8 %grads.1 = (bf16[128,1024]{1,0:T(8,128)(2,1)}, bf16[128,1024]{1,0:T(8,128)(2,1)}, bf16[128,1024]{1,0:T(8,128)(2,1)}, f32[8,128]{1,0:T(8,128)}) custom-call(f32[152,128]{1,0:T(8,128)S(1)} %get-tuple-element.48.mine, f32[152,128]{1,0:T(8,128)S(1)} %collective-permute-done.3.theirs, f32[8,16,128]{2,1,0:T(8,128)S(1)} %get-tuple-element.40.rate_ref, ...), custom_call_target="tpu_custom_call" | custom-call | flops 8388608 | bytes 2621440 | tf_op jit(solution)/shard_map/grads/pallas_call | solution.py:552
  30.7 0.0 collective-permute-done.4.refs_1_
  30.7 0.0 collective-permute-done.6.refs_3_
  30.7 1.3 %collective-permute-done.5.refs_2_ = f32[16,128]{1,0:T(8,128)S(1)} collective-permute-done((f32[16,128]{1,0:T(8,128)S(1)}, f32[16,128]{1,0:T(8,128)S(1)}, u32[]{:S(2)}, u32[]{:S(2)}) %collective-permute-start.5) | collective-permute-done | bytes 8224 | tf_op jit(solution)/shard_map/ppermute | solution.py:435
  32.1 0.7 %final.1 = (f32[16,256]{1,0:T(8,128)}, f32[16,256]{1,0:T(8,128)}) custom-call(f32[16,256]{1,0:T(8,128)S(1)} %bitcast.8, f32[16,256]{1,0:T(8,128)S(1)} %bitcast.10, f32[16,128]{1,0:T(8,128)S(1)} %slice_add_fusion.refs_0_, f32[16,128]{1,0:T(8,128)S(1)} %collective-permute-done.4.refs_1_, f32[16,128]{1,0:T(8,128)S(1)} %collective-permute-done.5.refs_2_, ...), custom_call_target="tpu_custom_call" | custom-call | tf_op jit(solution)/shard_map/final/pallas_call | solution.py:461
  (12 shorter events, 0.0 us)
Async XLA Ops:
  3.0 8.0 %collective-permute-start = (f32[256,128]{1,0:T(8,128)S(1)}, f32[256,128]{1,0:T(8,128)S(1)}, u32[]{:S(2)}, u32[]{:S(2)}) collective-permute-start(f32[256,128]{1,0:T(8,128)S(1)} %constant_dynamic-slice_fusion), channel_id=1, source_target_pairs={{0,4},{4,0},{8,12},{12,8},{16,20},{20,16},{24,28},{28,24},{1,5},{5... | collective-permute-start | bytes 393224 | tf_op jit(solution)/shard_map/ppermute | solution.py:435
  11.0 1.9 %copy-start.3 = (f32[256,16]{0,1:T(8,128)S(1)}, f32[256,16]{0,1:T(8,128)}, u32[]{:S(2)}) copy-start(f32[256,16]{0,1:T(8,128)} %param.13) | copy-start | bytes 49156
  11.0 1.9 %copy-start.4 = (f32[256,16]{0,1:T(8,128)S(1)}, f32[256,16]{0,1:T(8,128)}, u32[]{:S(2)}) copy-start(f32[256,16]{0,1:T(8,128)} %param.12) | copy-start | bytes 49156
  11.3 1.6 %copy-start.5 = (f32[1024]{0:T(1024)S(1)}, f32[1024]{0:T(1024)}, u32[]{:S(2)}) copy-start(f32[1024]{0:T(1024)} %param.11) | copy-start | bytes 12292
  11.3 5.2 %collective-permute-start.1 = (f32[280,128]{1,0:T(8,128)S(1)}, f32[280,128]{1,0:T(8,128)S(1)}, u32[]{:S(2)}, u32[]{:S(2)}) collective-permute-start(f32[280,128]{1,0:T(8,128)S(1)} %get-tuple-element.39.own_ref), channel_id=1, source_target_pairs={{0,8},{4,12},{8,0},{12,4},{16,24},{20,28},{24,16},{28,20},{1,9},{5... | collective-permute-start | bytes 430088 | tf_op jit(solution)/shard_map/ppermute | solution.py:435
  16.5 12.4 %copy-start.2 = (bf16[128,1024]{1,0:T(8,128)(2,1)S(1)}, bf16[128,1024]{1,0:T(8,128)(2,1)}, u32[]{:S(2)}) copy-start(bf16[128,1024]{1,0:T(8,128)(2,1)} %upstream.1) | copy-start | bytes 786436
  16.8 5.3 %collective-permute-start.2 = (f32[152,128]{1,0:T(8,128)S(1)}, f32[152,128]{1,0:T(8,128)S(1)}, u32[]{:S(2)}, u32[]{:S(2)}) collective-permute-start(f32[152,128]{1,0:T(8,128)S(1)} %get-tuple-element.46), channel_id=1, source_target_pairs={{0,16},{4,20},{8,24},{12,28},{16,0},{20,4},{24,8},{28,12},{1,17},{... | collective-permute-start | bytes 233480 | tf_op jit(solution)/shard_map/ppermute | solution.py:435
  22.1 6.8 %copy-start = (bf16[128,1024]{1,0:T(8,128)(2,1)S(1)}, bf16[128,1024]{1,0:T(8,128)(2,1)}, u32[]{:S(2)}) copy-start(bf16[128,1024]{1,0:T(8,128)(2,1)} %key.1) | copy-start | bytes 786436
  22.1 6.8 %copy-start.1 = (bf16[128,1024]{1,0:T(8,128)(2,1)S(1)}, bf16[128,1024]{1,0:T(8,128)(2,1)}, u32[]{:S(2)}) copy-start(bf16[128,1024]{1,0:T(8,128)(2,1)} %values.1) | copy-start | bytes 786436
  22.4 4.4 %collective-permute-start.3 = (f32[152,128]{1,0:T(8,128)S(1)}, f32[152,128]{1,0:T(8,128)S(1)}, u32[]{:S(2)}, u32[]{:S(2)}) collective-permute-start(f32[152,128]{1,0:T(8,128)S(1)} %get-tuple-element.49), channel_id=1, source_target_pairs={{0,4},{4,0},{8,12},{12,8},{16,20},{20,16},{24,28},{28,24},{1,5},{5... | collective-permute-start | bytes 233480 | tf_op jit(solution)/shard_map/ppermute | solution.py:435
  26.8 3.9 %collective-permute-start.4 = (f32[16,128]{1,0:T(8,128)S(1)}, f32[16,128]{1,0:T(8,128)S(1)}, u32[]{:S(2)}, u32[]{:S(2)}) collective-permute-start(f32[16,128]{1,0:T(8,128)S(1)} %slice_add_fusion.refs_0_), channel_id=1, source_target_pairs={{0,1},{1,0},{2,3},{3,2},{4,5},{5,4},{6,7},{7,6},{8,9},{9,8},{10,11... | collective-permute-start | bytes 24584 | tf_op jit(solution)/shard_map/ppermute | solution.py:435
  26.8 3.9 %collective-permute-start.6 = (f32[16,128]{1,0:T(8,128)S(1)}, f32[16,128]{1,0:T(8,128)S(1)}, u32[]{:S(2)}, u32[]{:S(2)}) collective-permute-start(f32[16,128]{1,0:T(8,128)S(1)} %slice_add_fusion.refs_0_), channel_id=1, source_target_pairs={{0,3},{1,2},{2,1},{3,0},{4,7},{5,6},{6,5},{7,4},{8,11},{9,10},{10,... | collective-permute-start | bytes 24584 | tf_op jit(solution)/shard_map/ppermute | solution.py:435
  28.4 3.7 %collective-permute-start.5 = (f32[16,128]{1,0:T(8,128)S(1)}, f32[16,128]{1,0:T(8,128)S(1)}, u32[]{:S(2)}, u32[]{:S(2)}) collective-permute-start(f32[16,128]{1,0:T(8,128)S(1)} %slice_add_fusion.refs_0_), channel_id=1, source_target_pairs={{0,2},{1,3},{2,0},{3,1},{4,6},{5,7},{6,4},{7,5},{8,10},{9,11},{10,... | collective-permute-start | bytes 24584 | tf_op jit(solution)/shard_map/ppermute | solution.py:435

commit v3 on v2

--- a/solution.py
+++ b/solution.py
@@ -38,33 +38,24 @@
 
 
 def wide_dot(a_high, a_low, b_high, b_low):
-    dot = functools.partial(jnp.dot, preferred_element_type=F32)
-    return dot(a_high, b_high) + (dot(a_high, b_low) + dot(a_low, b_high))
+    return jnp.dot(
+        jnp.concatenate([a_high, a_low, a_high], axis=1),
+        jnp.concatenate([b_high, b_high, b_low], axis=0),
+        preferred_element_type=F32,
+    )
 
 
 def spread(row):
     return jnp.broadcast_to(row, (SUB, LANES))
 
 
-def sub_ends(x_ref, ct, decay, steps, reverse):
-    order = range(steps - 1, -1, -1) if reverse else range(steps)
-    state = None
-    for i in order:
-        x = x_ref[ct, pl.ds(i, SUB, stride=steps), :]
-        state = [x] * len(decay) if state is None else [d * s + x for d, s in zip(decay, state)]
-    return state
-
-
-def sub_starts(ends, jumps, reverse):
-    index = lax.broadcasted_iota(jnp.int32, (SUB, LANES), 0)
-    if reverse:
-        index = SUB - 1 - index
-    shift = lambda v, n: pltpu.roll(v, SUB - n if reverse else n, 0)
+def sub_starts_back(ends, jumps):
+    index = SUB - 1 - lax.broadcasted_iota(jnp.int32, (SUB, LANES), 0)
     out = []
     for end, jump in zip(ends, jumps):
-        x = jnp.where(index == 0, 0.0, shift(end, 1))
+        x = jnp.where(index == 0, 0.0, pltpu.roll(end, SUB - 1, 0))
         for n in (1, 2, 4):
-            x = x + jnp.where(index >= n, jump, 0.0) * shift(x, n)
+            x = x + jnp.where(index >= n, jump, 0.0) * pltpu.roll(x, SUB - n, 0)
             jump = jump * jump
         out.append(x)
     return out
@@ -173,42 +164,79 @@
     return jnp.concatenate([summed[:modes], summed[modes:]], axis=1)
 
 
-def within_kernel(rate_ref, mixed_ref, carried_ref, skip, sums, starts, after_s, first_s, second_s):
+def sub_spans(x_ref, ct, decay, steps, reverse):
+    order = range(steps - 1, -1, -1) if reverse else range(steps)
+    state = slope = None
+    for i in order:
+        x = x_ref[ct, pl.ds(i, SUB, stride=steps), :]
+        if state is None:
+            state = [x] * len(decay)
+            continue
+        moved = [d * s for d, s in zip(decay, state)]
+        slope = moved if slope is None else [d * t + a for d, t, a in zip(decay, slope, moved)]
+        state = [a + x for a in moved]
+    return state, slope
+
+
+def sub_starts_both(ends, slopes, jumps, span):
+    index = lax.broadcasted_iota(jnp.int32, (SUB, LANES), 0)
+    starts, start_slopes = [], []
+    for end, slope, jump in zip(ends, slopes, jumps):
+        x = jnp.where(index == 0, 0.0, pltpu.roll(end, 1, 0))
+        y = jnp.where(index == 0, 0.0, pltpu.roll(slope, 1, 0))
+        for n in (1, 2, 4):
+            hop = jnp.where(index >= n, jump, 0.0)
+            x_far = pltpu.roll(x, n, 0)
+            y = y + hop * (pltpu.roll(y, n, 0) + float(n * span) * x_far)
+            x = x + hop * x_far
+            jump = jump * jump
+        starts.append(x)
+        start_slopes.append(y)
+    return starts, start_slopes
+
+
+def within_kernel(rate_ref, mixed_ref, carried_ref, skip, sums, starts, first_s, second_s):
     tiles, rows, _ = mixed_ref.shape
     modes = rate_ref.shape[1]
     steps = rows // SUB
     half = modes // 2
+    total = lambda v: jnp.sum(v, axis=0, keepdims=True)
 
     def tile(ct, _):
         rate = rate_ref[ct]
+        firsts, seconds = [], []
         for lo in range(0, modes, half):
             rate_rows = [spread(rate[m : m + 1, :]) for m in range(lo, lo + half)]
             decay = [jnp.exp(-r) for r in rate_rows]
             jumps = [jnp.exp(-r * float(steps)) for r in rate_rows]
-            state = sub_starts(sub_ends(carried_ref, ct, decay, steps, True), jumps, True)
+            ends, end_slopes = sub_spans(mixed_ref, ct, decay, steps, False)
+            before, before_slopes = sub_starts_both(ends, end_slopes, jumps, steps)
+            behind, behind_slopes = sub_spans(carried_ref, ct, decay, steps, True)
             for m in range(half):
-                starts[ct, 1, lo + m] = state[m]
-            for i in range(steps - 1, -1, -1):
-                c = carried_ref[ct, pl.ds(i, SUB, stride=steps), :]
-                state = [d * s for d, s in zip(decay, state)]
-                for m in range(half):
-                    after_s[i, m] = state[m]
-                state = [a + c for a in state]
-            state = sub_starts(sub_ends(mixed_ref, ct, decay, steps, False), jumps, False)
-            for m in range(half):
-                starts[ct, 0, lo + m] = state[m]
-            first = [jnp.zeros((SUB, LANES), F32)] * half
-            second = [jnp.zeros((SUB, LANES), F32)] * half
-            for i in range(steps):
-                x = mixed_ref[ct, pl.ds(i, SUB, stride=steps), :]
-                c = carried_ref[ct, pl.ds(i, SUB, stride=steps), :]
-                state = [d * s + x for d, s in zip(decay, state)]
-                first = [f + c * s for f, s in zip(first, state)]
-                second = [f + after_s[i, m] * state[m] for m, f in enumerate(second)]
-            for ref, values in ((first_s, first), (second_s, second)):
-                ref[ct, lo : lo + half, :] = jnp.concatenate(
-                    [jnp.sum(v, axis=0, keepdims=True) for v in values], axis=0
+                starts[ct, 0, lo + m] = before[m]
+                starts[ct, 1, lo + m] = behind[m]
+                reached = decay[m] * before[m]
+                firsts.append(total(reached * behind[m]))
+                seconds.append(
+                    total(
+                        (decay[m] * before_slopes[m]) * behind[m]
+                        + reached * (behind[m] + behind_slopes[m])
+                    )
                 )
+        x = [mixed_ref[ct, pl.ds(i, SUB, stride=steps), :] for i in range(steps)]
+        c = [carried_ref[ct, pl.ds(i, SUB, stride=steps), :] for i in range(steps)]
+        decay = jnp.exp(-rate)
+        first = second = jnp.zeros((modes, LANES), F32)
+        for lag in range(steps - 1, -1, -1):
+            terms = [c[i + lag] * x[i] for i in range(steps - lag)]
+            while len(terms) > 1:
+                odd = terms[len(terms) // 2 * 2 :]
+                terms = [a + b for a, b in zip(terms[::2], terms[1::2])] + odd
+            moved = decay * first
+            second = decay * second + moved
+            first = moved + total(terms[0])
+        first_s[ct] = first + jnp.concatenate(firsts, axis=0)
+        second_s[ct] = second + jnp.concatenate(seconds, axis=0)
         return 0
 
     lax.fori_loop(0, tiles, tile, 0)
@@ -299,7 +327,7 @@
 
 
 def last_join_kernel(
-    rows, step, rate_ref, own_ref, other_ref, borders_ref, states_ref, partner_ref, mine_ref, back_ref
+    rows, step, rate_ref, own_ref, other_ref, borders_ref, states_ref, partner_ref, mine_ref, back_ref, modal_ref
 ):
     tiles, modes, _ = rate_ref.shape
     part = tiles // 2 * modes
@@ -309,7 +337,11 @@
     own = [own_ref[q * part : (q + 1) * part, :] for q in range(4)]
     other = [other_ref[q * part : (q + 1) * part, :] for q in range(2)]
     _, first, second = spans_join(own, other + other, rate, upper, rows * step)
-    packet = border_sums(first, second, tiles, modes)
+    sums = own_ref[4 * part :, :] + other_ref[2 * part :, :]
+    modal = sums[:modes] + border_sums(first, second, tiles, modes)
+    modal_ref[...] = modal
+    back_ref[2 * part : 2 * part + modes, :] = modal
+    back_ref[2 * part + modes :, :] = sums[modes:]
     borders = add_borders(
         rows, step, rate, [borders_ref[:part, :], borders_ref[part:, :]], other[0], other[0]
     )
@@ -326,9 +358,6 @@
     ):
         ref[:part, :] = jnp.where(is_second, through + forward, incoming)
         ref[part : 2 * part, :] = jnp.where(is_second, outgoing, across + backward)
-        sums = own_ref[4 * part :, :] + other_ref[2 * part :, :]
-        ref[2 * part : 2 * part + modes, :] = sums[:modes] + packet
-        ref[2 * part + modes :, :] = sums[modes:]
 
 
 def block_kernel(
@@ -351,10 +380,13 @@
         scale = scales[ct]
         weight = spread(skip_weight[pl.ds(ct, 1), :])
         for lo in range(0, modes, half):
-            decay = [jnp.exp(-spread(rate[m : m + 1, :])) for m in range(lo, lo + half)]
+            rate_rows = [spread(rate[m : m + 1, :]) for m in range(lo, lo + half)]
+            decay = [jnp.exp(-r) for r in rate_rows]
             gains = [spread(scale[m : m + 1, :]) for m in range(lo, lo + half)]
             for way, x_ref in enumerate((mixed_ref, carried_ref)):
                 state = [starts[ct, way, lo + m] for m in range(half)]
+                if way:
+                    state = sub_starts_back(state, [jnp.exp(-r * float(steps)) for r in rate_rows])
                 for i in range(steps - 1, -1, -1) if way else range(steps):
                     at = pl.ds(i, SUB, stride=steps)
                     x = x_ref[ct, at, :]
@@ -370,14 +402,12 @@
     lax.fori_loop(0, tiles, tile, 0)
 
 
-def grads_kernel(full, mine, theirs, rate_ref, scale_ref, results, key, values, upstream, *refs):
-    query_grad, key_grad, value_grad, skip_grad = refs
+def grads_kernel(mine, theirs, rate_ref, scale_ref, results, key, values, upstream, *refs):
+    query_grad, key_grad, value_grad = refs
     tiles, modes, _ = scale_ref.shape
     rows = key.shape[0]
     share = tiles // 2
     part = share * modes
-    skip_rows = slice(2 * part + modes, 2 * part + modes + tiles)
-    skip_grad[...] = (mine[skip_rows, :] + theirs[skip_rows, :]) / jnp.sqrt(jnp.float32(full))
     second_half = (lax.axis_index("ctx") & 1) != 0
     lane = lax.broadcasted_iota(jnp.int32, (modes, LANES), 1)
     own_mode = lax.broadcasted_iota(jnp.int32, (modes, LANES), 0) == lax.rem(lane, modes)
@@ -410,12 +440,15 @@
         pl.when(pl.program_id(0) == p)(functools.partial(piece, p))
 
 
-def final_kernel(full, log_rates, residues, *refs):
-    *by_distance, residue_grad, log_rate_grad = refs
-    total_filters = log_rates.shape[1]
-    filters = by_distance[0].shape[1] // 2
+def final_kernel(
+    full, log_rates, residues, back, theirs, here, there, residue_grad, log_rate_grad, skip_grad
+):
+    modes, total_filters = log_rates.shape
+    filters = here.shape[1] // 2
     group = lax.axis_index("grp")
-    by_distance = [ref[...] for ref in by_distance]
+    skip_rows = slice(back.shape[0] - skip_grad.shape[0], back.shape[0])
+    skip_grad[...] = (back[skip_rows, :] + theirs[skip_rows, :]) / jnp.sqrt(jnp.float32(full))
+    by_distance = [here[:modes, :], there[:modes, :], here[modes:, :], there[modes:, :]]
     totals = []
     for g in range(total_filters // filters):
         total = by_distance[0]
@@ -450,7 +483,7 @@
     full = rows * context
     part = tiles // 2 * modes
     tail = modes + tiles
-    assert context >= 4 and context & (context - 1) == 0 and groups & (groups - 1) == 0
+    assert context >= 4 and context & (context - 1) == 0 and groups == 4
     vmem = pl.BlockSpec(memory_space=pltpu.VMEM)
     in_hbm = pl.BlockSpec(memory_space=pltpu.HBM)
     shape = lambda *dims: jax.ShapeDtypeStruct(dims, F32)
@@ -502,7 +535,7 @@
         within_kernel,
         (shape(tail, LANES), shape(tiles, 2, modes, SUB, LANES)),
         (rate, mixed, carried, skip),
-        ((rows // SUB, modes // 2, SUB, LANES), (tiles, modes, LANES), (tiles, modes, LANES)),
+        ((tiles, modes, LANES), (tiles, modes, LANES)),
         12 * work,
     )
     scale = results = None
@@ -538,36 +571,38 @@
             other = after(other, results)
         extra = (borders,)
         step *= 2
-    mine, back = call(
+    mine, back, modal = call(
         "last_join",
         functools.partial(last_join_kernel, rows, step),
-        (shape(2 * part + tail, LANES),) * 2,
+        (shape(2 * part, LANES), shape(2 * part + tail, LANES), shape(modes, LANES)),
         (rate, own, other, borders, states, partner),
     )
+
+    everyone = ("ctx", "grp")
     theirs = flip(back, 1)
-
-    packed = mine[2 * part : 2 * part + modes] + theirs[2 * part : 2 * part + modes]
-    gathered = [flip(packed, k, "grp") for k in range(1, groups)]
+    across, level = flip(modal, groups + 2, everyone), flip(modal, 2, everyone)
     columns = pl.BlockSpec((rows, channels // 2), lambda i: (0, i))
     outputs = pl.pallas_call(
-        functools.partial(grads_kernel, full),
+        grads_kernel,
         grid=(2,),
-        out_shape=(jax.ShapeDtypeStruct((rows, channels), BF16),) * 3 + (shape(tiles, LANES),),
+        out_shape=(jax.ShapeDtypeStruct((rows, channels), BF16),) * 3,
         in_specs=[vmem] * 5 + [columns] * 3,
-        out_specs=(columns,) * 3 + (pl.BlockSpec((tiles, LANES), lambda i: (0, 0)),),
+        out_specs=(columns,) * 3,
         compiler_params=params,
         cost_estimate=pl.CostEstimate(
             flops=4 * work, transcendentals=0, bytes_accessed=20 * rows * channels
         ),
         name="grads",
     )(mine, theirs, rate, scale, results, key_gate, values, upstream)
-    query_grad, key_grad, value_grad, skip_grad = outputs
-    gathered[0] = after(gathered[0], *outputs)
-    residue_grad, log_rate_grad = call(
+    query_grad, key_grad, value_grad = outputs
+    across, level = (after(x, *outputs) for x in (across, level))
+    here = jnp.concatenate([modal + theirs[2 * part : 2 * part + modes], level + across], axis=0)
+    there = flip(here, 1, "grp")
+    residue_grad, log_rate_grad, skip_grad = call(
         "final",
         functools.partial(final_kernel, full),
-        (shape(modes, total_filters),) * 2,
-        (log_rates_t, residues_t, packed, *gathered),
+        (shape(modes, total_filters),) * 2 + (shape(tiles, LANES),),
+        (log_rates_t, residues_t, back, theirs, here, there),
     )
     return (
         query_grad,

time: 33.1 us -> 30.7 us (0.927)
  waiting for transfers between devices: 8.58 us -> 5.37 us
  starting transfers between devices: 9.74 us -> 10.8 us
    ppermute x7, waiting for transfers between devices: 8.58 us -> 5.37 us  [flip(): lax.ppermute(x, axis, [(i, i ^ step) for i in range(lax.axis_size(axis))])]
    ppermute x7, starting transfers between devices: 9.74 us -> 10.8 us  [flip(): lax.ppermute(x, axis, [(i, i ^ step) for i in range(lax.axis_size(axis))])]
  transfers between devices with their start and end apart: 7 -> 7, of which waited for: 4 -> 5; matrix products, arithmetic and copies ran while one was open for 0% -> 0% of each run, Pallas kernels for 30% -> 32%
where the time goes in v3:
time: 30.7 us; the launch traced here: 30.4 us
  Pallas kernels  13.4 us (44%)
  starting transfers between devices  10.8 us (35%)
  waiting for transfers between devices  5.37 us (17%)
  between operations  0.7 us (2%)
    ppermute x7, starting transfers between devices, flip(): lax.ppermute(x, axis, [(i, i ^ step) for i in range(lax.axis_size(axis))])  10.8 us
    pallas_call x6, Pallas kernels, call(): pl.pallas_call(kernel, out_shape=out_shape, in_specs=[vmem] * len(operand...  9.36 us
    ppermute x7, waiting for transfers between devices, flip(): lax.ppermute(x, axis, [(i, i ^ step) for i in range(lax.axis_size(axis))])  5.37 us
    pallas_call x1, Pallas kernels, local(): pl.pallas_call(functools.partial(states_kernel, full), out_shape=(shape(8...  2.32 us
    pallas_call x1, Pallas kernels, local(): pl.pallas_call(grads_kernel, grid=(2,), out_shape=(jax.ShapeDtypeStruct((...  1.74 us
  transfers between devices with their start and end apart: 7, of which 5 were waited for; matrix products, arithmetic and copies ran while one was open for 0% of the time, Pallas kernels for 32%

profile of v3, /device:TPU:0, one launch (start us, length us, event | category | flops | bytes accessed | tf_op | source)
XLA Modules:
  0.0 30.4 jit_solution(2434535304247915566)
XLA Ops:
  0.6 2.3 %states.1 = (f32[512,128]{1,0:T(8,128)S(1)}, f32[8,16,128]{2,1,0:T(8,128)S(1)}, f32[8,128,128]{2,1,0:T(8,128)S(1)}, f32[8,128,128]{2,1,0:T(8,128)S(1)}, f32[8,128]{1,0:T(8,128)S(1)}) custom-call(f32[16,256]{1,0:T(8,128)} %bitcast.6, bf16[128,1024]{1,0:T(8,128)(2,1)} %key.1, bf16[128,1024]{1,0:T(8,128)(2,1)} %values.1, bf16[128,1024]{1,0:T(8,128)(2,1)} %upstream.1, ...), custom_call_target="tpu_custom_call" | custom-call | tf_op jit(solution)/shard_map/states/pallas_call | solution.py:506
  3.0 3.0 %collective-permute-start = (f32[256,128]{1,0:T(8,128)S(1)}, f32[256,128]{1,0:T(8,128)S(1)}, u32[]{:S(2)}, u32[]{:S(2)}) collective-permute-start(f32[256,128]{1,0:T(8,128)S(1)} %constant_dynamic-slice_fusion), channel_id=1, source_target_pairs={{0,4},{4,0},{8,12},{12,8},{16,20},{20,16},{24,28},{28,24},{1,5},{5... | collective-permute-start | bytes 393224 | tf_op jit(solution)/shard_map/ppermute | solution.py:468
  6.0 4.4 %within.1 = (f32[24,128]{1,0:T(8,128)S(1)}, f32[8,2,16,8,128]{4,3,2,1,0:T(8,128)S(1)}) custom-call(f32[8,16,128]{2,1,0:T(8,128)S(1)} %get-tuple-element.42.rate_ref, f32[8,128,128]{2,1,0:T(8,128)S(1)} %get-tuple-element.36.mixed_ref, f32[8,128,128]{2,1,0:T(8,128)S(1)} %get-tuple-element.37.carried_ref, f32[8,128]{1,0:T(8,128)S(1)} %get-tuple-element.38.skip), custom_call_target="tpu_custom_call" | custom-call | flops 25165824 | bytes 6291456 | tf_op jit(solution)/shard_map/within/pallas_call | solution.py:494
  10.4 0.0 collective-permute-done.other_ref.partner_ref
  10.4 0.0 copy-start.4
  10.4 0.2 join.2
  10.7 1.6 %collective-permute-start.1 = (f32[280,128]{1,0:T(8,128)S(1)}, f32[280,128]{1,0:T(8,128)S(1)}, u32[]{:S(2)}, u32[]{:S(2)}) collective-permute-start(f32[280,128]{1,0:T(8,128)S(1)} %get-tuple-element.41.own_ref), channel_id=1, source_target_pairs={{0,8},{4,12},{8,0},{12,4},{16,24},{20,28},{24,16},{28,20},{1,9},{5... | collective-permute-start | bytes 430088 | tf_op jit(solution)/shard_map/ppermute | solution.py:468
  12.3 0.0 copy-done.4
  12.3 3.5 %block.1 = (f32[8,16,128]{2,1,0:T(8,128)S(1)}, f32[8,2,128,128]{3,2,1,0:T(8,128)S(1)}) custom-call(f32[16,256]{1,0:T(8,128)S(1)} %bitcast.7, f32[16,256]{1,0:T(8,128)S(1)} %bitcast.9, f32[8,128]{1,0:T(8,128)S(1)} %bitcast.11, f32[8,16,128]{2,1,0:T(8,128)S(1)} %get-tuple-element.42.rate_ref, f32[8,128,128]{2,1,0:T(8,128)S(1)} %get-tuple-element.36.mixed_ref, ...), custom_call_target="tpu_custom_call" | custom-call | flops 16777216 | bytes 4194304 | tf_op jit(solution)/shard_map/block/pallas_call | solution.py:494
  15.8 0.1 collective-permute-done.1.other_ref
  15.9 0.3 join.3
  16.2 2.6 %collective-permute-start.2 = (f32[152,128]{1,0:T(8,128)S(1)}, f32[152,128]{1,0:T(8,128)S(1)}, u32[]{:S(2)}, u32[]{:S(2)}) collective-permute-start(f32[152,128]{1,0:T(8,128)S(1)} %get-tuple-element.48), channel_id=1, source_target_pairs={{0,16},{4,20},{8,24},{12,28},{16,0},{20,4},{24,8},{28,12},{1,17},{... | collective-permute-start | bytes 233480 | tf_op jit(solution)/shard_map/ppermute | solution.py:468
  18.8 2.7 %collective-permute-done.2.other_ref = f32[152,128]{1,0:T(8,128)S(1)} collective-permute-done((f32[152,128]{1,0:T(8,128)S(1)}, f32[152,128]{1,0:T(8,128)S(1)}, u32[]{:S(2)}, u32[]{:S(2)}) %collective-permute-start.2) | collective-permute-done | bytes 77856 | tf_op jit(solution)/shard_map/ppermute | solution.py:468
  21.5 0.3 last_join.1
  21.8 0.7 %collective-permute-start.3 = (f32[152,128]{1,0:T(8,128)S(1)}, f32[152,128]{1,0:T(8,128)S(1)}, u32[]{:S(2)}, u32[]{:S(2)}) collective-permute-start(f32[152,128]{1,0:T(8,128)S(1)} %get-tuple-element.51.back), channel_id=1, source_target_pairs={{0,4},{4,0},{8,12},{12,8},{16,20},{20,16},{24,28},{28,24},{1,5},{5... | collective-permute-start | bytes 233480 | tf_op jit(solution)/shard_map/ppermute | solution.py:468
  22.5 2.2 %collective-permute-start.5 = (f32[16,128]{1,0:T(8,128)S(1)}, f32[16,128]{1,0:T(8,128)S(1)}, u32[]{:S(2)}, u32[]{:S(2)}) collective-permute-start(f32[16,128]{1,0:T(8,128)S(1)} %get-tuple-element.56), channel_id=1, source_target_pairs={{0,6},{1,7},{2,4},{3,5},{4,2},{5,3},{6,0},{7,1},{8,14},{9,15},{10,... | collective-permute-start | bytes 24584 | tf_op jit(solution)/shard_map/ppermute | solution.py:468
  24.8 0.5 %collective-permute-start.4 = (f32[16,128]{1,0:T(8,128)S(1)}, f32[16,128]{1,0:T(8,128)S(1)}, u32[]{:S(2)}, u32[]{:S(2)}) collective-permute-start(f32[16,128]{1,0:T(8,128)S(1)} %get-tuple-element.56), channel_id=1, source_target_pairs={{0,2},{1,3},{2,0},{3,1},{4,6},{5,7},{6,4},{7,5},{8,10},{9,11},{10,... | collective-permute-start | bytes 24584 | tf_op jit(solution)/shard_map/ppermute | solution.py:468
  25.3 0.9 %collective-permute-done.3.theirs = f32[152,128]{1,0:T(8,128)S(1)} collective-permute-done((f32[152,128]{1,0:T(8,128)S(1)}, f32[152,128]{1,0:T(8,128)S(1)}, u32[]{:S(2)}, u32[]{:S(2)}) %collective-permute-start.3) | collective-permute-done | bytes 77856 | tf_op jit(solution)/shard_map/ppermute | solution.py:468
  26.2 1.7 %grads.1 = (bf16[128,1024]{1,0:T(8,128)(2,1)}, bf16[128,1024]{1,0:T(8,128)(2,1)}, bf16[128,1024]{1,0:T(8,128)(2,1)}) custom-call(f32[128,128]{1,0:T(8,128)S(1)} %get-tuple-element.50.mine, f32[152,128]{1,0:T(8,128)S(1)} %collective-permute-done.3.theirs, f32[8,16,128]{2,1,0:T(8,128)S(1)} %get-tuple-element.42.rate_ref, ...), custom_call_target="tpu_custom_call" | custom-call | flops 8388608 | bytes 2621440 | tf_op jit(solution)/shard_map/grads/pallas_call | solution.py:585
  28.0 0.0 collective-permute-done.5
  28.0 0.5 %collective-permute-done.4 = f32[16,128]{1,0:T(8,128)S(1)} collective-permute-done((f32[16,128]{1,0:T(8,128)S(1)}, f32[16,128]{1,0:T(8,128)S(1)}, u32[]{:S(2)}, u32[]{:S(2)}) %collective-permute-start.4) | collective-permute-done | bytes 8224 | tf_op jit(solution)/shard_map/ppermute | solution.py:468
  28.4 0.1 collective-permute-start.6
  28.5 1.2 %collective-permute-done.6.there = f32[32,128]{1,0:T(8,128)S(1)} collective-permute-done((f32[32,128]{1,0:T(8,128)S(1)}, f32[32,128]{1,0:T(8,128)S(1)}, u32[]{:S(2)}, u32[]{:S(2)}) %collective-permute-start.6) | collective-permute-done | bytes 16416 | tf_op jit(solution)/shard_map/ppermute | solution.py:468
  29.7 0.7 %final.1 = (f32[16,256]{1,0:T(8,128)}, f32[16,256]{1,0:T(8,128)}, f32[8,128]{1,0:T(8,128)}) custom-call(f32[16,256]{1,0:T(8,128)S(1)} %bitcast.8, f32[16,256]{1,0:T(8,128)S(1)} %bitcast.10, f32[152,128]{1,0:T(8,128)S(1)} %get-tuple-element.51.back, f32[152,128]{1,0:T(8,128)S(1)} %collective-permute-done.3.theirs, f32[32,128]{1,0:T(8,128)S(1)} %pad_maximum_fusion.here, ...), custom_call_target="tpu_custom_call" | custom-call | tf_op jit(solution)/shard_map/final/pallas_call | solution.py:494
  (14 shorter events, 0.0 us)
Async XLA Ops:
  3.0 7.4 %collective-permute-start = (f32[256,128]{1,0:T(8,128)S(1)}, f32[256,128]{1,0:T(8,128)S(1)}, u32[]{:S(2)}, u32[]{:S(2)}) collective-permute-start(f32[256,128]{1,0:T(8,128)S(1)} %constant_dynamic-slice_fusion), channel_id=1, source_target_pairs={{0,4},{4,0},{8,12},{12,8},{16,20},{20,16},{24,28},{28,24},{1,5},{5... | collective-permute-start | bytes 393224 | tf_op jit(solution)/shard_map/ppermute | solution.py:468
  10.4 1.9 %copy-start.3 = (f32[256,16]{0,1:T(8,128)S(1)}, f32[256,16]{0,1:T(8,128)}, u32[]{:S(2)}) copy-start(f32[256,16]{0,1:T(8,128)} %param.13) | copy-start | bytes 49156
  10.4 1.9 %copy-start.4 = (f32[256,16]{0,1:T(8,128)S(1)}, f32[256,16]{0,1:T(8,128)}, u32[]{:S(2)}) copy-start(f32[256,16]{0,1:T(8,128)} %param.12) | copy-start | bytes 49156
  10.7 1.6 %copy-start.5 = (f32[1024]{0:T(1024)S(1)}, f32[1024]{0:T(1024)}, u32[]{:S(2)}) copy-start(f32[1024]{0:T(1024)} %param.11) | copy-start | bytes 12292
  10.7 5.2 %collective-permute-start.1 = (f32[280,128]{1,0:T(8,128)S(1)}, f32[280,128]{1,0:T(8,128)S(1)}, u32[]{:S(2)}, u32[]{:S(2)}) collective-permute-start(f32[280,128]{1,0:T(8,128)S(1)} %get-tuple-element.41.own_ref), channel_id=1, source_target_pairs={{0,8},{4,12},{8,0},{12,4},{16,24},{20,28},{24,16},{28,20},{1,9},{5... | collective-permute-start | bytes 430088 | tf_op jit(solution)/shard_map/ppermute | solution.py:468
  15.9 10.3 %copy-start.2 = (bf16[128,1024]{1,0:T(8,128)(2,1)S(1)}, bf16[128,1024]{1,0:T(8,128)(2,1)}, u32[]{:S(2)}) copy-start(bf16[128,1024]{1,0:T(8,128)(2,1)} %upstream.1) | copy-start | bytes 786436
  16.2 5.3 %collective-permute-start.2 = (f32[152,128]{1,0:T(8,128)S(1)}, f32[152,128]{1,0:T(8,128)S(1)}, u32[]{:S(2)}, u32[]{:S(2)}) collective-permute-start(f32[152,128]{1,0:T(8,128)S(1)} %get-tuple-element.48), channel_id=1, source_target_pairs={{0,16},{4,20},{8,24},{12,28},{16,0},{20,4},{24,8},{28,12},{1,17},{... | collective-permute-start | bytes 233480 | tf_op jit(solution)/shard_map/ppermute | solution.py:468
  21.5 4.7 %copy-start = (bf16[128,1024]{1,0:T(8,128)(2,1)S(1)}, bf16[128,1024]{1,0:T(8,128)(2,1)}, u32[]{:S(2)}) copy-start(bf16[128,1024]{1,0:T(8,128)(2,1)} %key.1) | copy-start | bytes 786436
  21.5 4.7 %copy-start.1 = (bf16[128,1024]{1,0:T(8,128)(2,1)S(1)}, bf16[128,1024]{1,0:T(8,128)(2,1)}, u32[]{:S(2)}) copy-start(bf16[128,1024]{1,0:T(8,128)(2,1)} %values.1) | copy-start | bytes 786436
  21.8 4.4 %collective-permute-start.3 = (f32[152,128]{1,0:T(8,128)S(1)}, f32[152,128]{1,0:T(8,128)S(1)}, u32[]{:S(2)}, u32[]{:S(2)}) collective-permute-start(f32[152,128]{1,0:T(8,128)S(1)} %get-tuple-element.51.back), channel_id=1, source_target_pairs={{0,4},{4,0},{8,12},{12,8},{16,20},{20,16},{24,28},{28,24},{1,5},{5... | collective-permute-start | bytes 233480 | tf_op jit(solution)/shard_map/ppermute | solution.py:468
  22.5 5.4 %collective-permute-start.5 = (f32[16,128]{1,0:T(8,128)S(1)}, f32[16,128]{1,0:T(8,128)S(1)}, u32[]{:S(2)}, u32[]{:S(2)}) collective-permute-start(f32[16,128]{1,0:T(8,128)S(1)} %get-tuple-element.56), channel_id=1, source_target_pairs={{0,6},{1,7},{2,4},{3,5},{4,2},{5,3},{6,0},{7,1},{8,14},{9,15},{10,... | collective-permute-start | bytes 24584 | tf_op jit(solution)/shard_map/ppermute | solution.py:468
  24.8 3.7 %collective-permute-start.4 = (f32[16,128]{1,0:T(8,128)S(1)}, f32[16,128]{1,0:T(8,128)S(1)}, u32[]{:S(2)}, u32[]{:S(2)}) collective-permute-start(f32[16,128]{1,0:T(8,128)S(1)} %get-tuple-element.56), channel_id=1, source_target_pairs={{0,2},{1,3},{2,0},{3,1},{4,6},{5,7},{6,4},{7,5},{8,10},{9,11},{10,... | collective-permute-start | bytes 24584 | tf_op jit(solution)/shard_map/ppermute | solution.py:468
  28.4 1.2 %collective-permute-start.6 = (f32[32,128]{1,0:T(8,128)S(1)}, f32[32,128]{1,0:T(8,128)S(1)}, u32[]{:S(2)}, u32[]{:S(2)}) collective-permute-start(f32[32,128]{1,0:T(8,128)S(1)} %pad_maximum_fusion.here), channel_id=1, source_target_pairs={{0,1},{1,0},{2,3},{3,2},{4,5},{5,4},{6,7},{7,6},{8,9},{9,8},{10,11... | collective-permute-start | bytes 49160 | tf_op jit(solution)/shard_map/ppermute | solution.py:468

commit v4 on v3

--- a/solution.py
+++ b/solution.py
@@ -97,7 +97,6 @@
     filters = channels // GROUP_CH
     modes = log_rates_h.shape[0]
     part = tiles // 2 * modes
-    wide = TILE_FILTERS * modes
     copies = [
         pltpu.make_async_copy(src, dst, sems.at[n])
         for n, (src, dst) in enumerate(
@@ -121,13 +120,13 @@
         rate = jnp.broadcast_to(step_rates[:, f : f + 1], (modes, rows))
         ct, row = f // TILE_FILTERS, (f % TILE_FILTERS) * modes
         for way, away in enumerate((back_time, time)):
-            weight = jnp.exp(-rate * away)
-            for n, high_low in enumerate((split(weight), split(weight * away))):
-                at = slice(n * wide + row, n * wide + row + modes)
-                weight_s[ct, 2 * way, at, :] = high_low[0]
-                weight_s[ct, 2 * way + 1, at, :] = high_low[1]
+            high, low = split(jnp.exp(-rate * away))
+            weight_s[ct, 2 * way, row : row + modes, :] = high
+            weight_s[ct, 2 * way + 1, row : row + modes, :] = low
     for ct in range(tiles):
         rate_out[ct] = channel_rates[:, ct * LANES : (ct + 1) * LANES]
+    forward = lax.broadcasted_iota(jnp.int32, (rows, LANES), 0).astype(F32)
+    backward = float(rows - 1) - forward
     for copy in copies[1:]:
         copy.wait()
     for ct in range(tiles):
@@ -137,11 +136,12 @@
         mixed_out[ct] = mixed
         carried_out[ct] = carried
         base = ct // (tiles // 2) * 4 * part + ct % (tiles // 2) * modes
-        for way, x in enumerate((mixed, carried)):
-            products = wide_dot(weight_s[ct, 2 * way], weight_s[ct, 2 * way + 1], *split(x))
+        for way, (x, away) in enumerate(((mixed, backward), (carried, forward))):
+            both = jnp.concatenate([x, x * away], axis=1)
+            products = wide_dot(weight_s[ct, 2 * way], weight_s[ct, 2 * way + 1], *split(both))
             for n in range(2):
                 at = base + (2 * way + n) * part
-                states[at : at + modes, :] = fold_modes(products[n * wide : (n + 1) * wide], modes)
+                states[at : at + modes, :] = fold_modes(products[:, n * LANES : (n + 1) * LANES], modes)
         skip_out[ct : ct + 1, :] = jnp.sum(mixed * carried, axis=0, keepdims=True)
 
 
@@ -164,11 +164,11 @@
     return jnp.concatenate([summed[:modes], summed[modes:]], axis=1)
 
 
-def sub_spans(x_ref, ct, decay, steps, reverse):
-    order = range(steps - 1, -1, -1) if reverse else range(steps)
+def sub_spans(x_ref, decay, reverse):
+    steps = x_ref.shape[0]
     state = slope = None
-    for i in order:
-        x = x_ref[ct, pl.ds(i, SUB, stride=steps), :]
+    for i in range(steps - 1, -1, -1) if reverse else range(steps):
+        x = x_ref[i]
         if state is None:
             state = [x] * len(decay)
             continue
@@ -195,7 +195,7 @@
     return starts, start_slopes
 
 
-def within_kernel(rate_ref, mixed_ref, carried_ref, skip, sums, starts, first_s, second_s):
+def within_kernel(rate_ref, mixed_ref, carried_ref, skip, sums, starts, dealt, first_s, second_s):
     tiles, rows, _ = mixed_ref.shape
     modes = rate_ref.shape[1]
     steps = rows // SUB
@@ -204,14 +204,18 @@
 
     def tile(ct, _):
         rate = rate_ref[ct]
+        step_decay = jnp.exp(-rate)
+        sub_decay = jnp.exp(-rate * float(steps))
         firsts, seconds = [], []
+        for i in range(steps):
+            for way, ref in enumerate((mixed_ref, carried_ref)):
+                dealt[ct, way, i] = ref[ct, pl.ds(i, SUB, stride=steps), :]
         for lo in range(0, modes, half):
-            rate_rows = [spread(rate[m : m + 1, :]) for m in range(lo, lo + half)]
-            decay = [jnp.exp(-r) for r in rate_rows]
-            jumps = [jnp.exp(-r * float(steps)) for r in rate_rows]
-            ends, end_slopes = sub_spans(mixed_ref, ct, decay, steps, False)
+            decay = [spread(step_decay[m : m + 1, :]) for m in range(lo, lo + half)]
+            jumps = [spread(sub_decay[m : m + 1, :]) for m in range(lo, lo + half)]
+            ends, end_slopes = sub_spans(dealt.at[ct, 0], decay, False)
             before, before_slopes = sub_starts_both(ends, end_slopes, jumps, steps)
-            behind, behind_slopes = sub_spans(carried_ref, ct, decay, steps, True)
+            behind, behind_slopes = sub_spans(dealt.at[ct, 1], decay, True)
             for m in range(half):
                 starts[ct, 0, lo + m] = before[m]
                 starts[ct, 1, lo + m] = behind[m]
@@ -223,17 +227,16 @@
                         + reached * (behind[m] + behind_slopes[m])
                     )
                 )
-        x = [mixed_ref[ct, pl.ds(i, SUB, stride=steps), :] for i in range(steps)]
-        c = [carried_ref[ct, pl.ds(i, SUB, stride=steps), :] for i in range(steps)]
-        decay = jnp.exp(-rate)
+        x = [dealt[ct, 0, i] for i in range(steps)]
+        c = [dealt[ct, 1, i] for i in range(steps)]
         first = second = jnp.zeros((modes, LANES), F32)
         for lag in range(steps - 1, -1, -1):
             terms = [c[i + lag] * x[i] for i in range(steps - lag)]
             while len(terms) > 1:
                 odd = terms[len(terms) // 2 * 2 :]
                 terms = [a + b for a, b in zip(terms[::2], terms[1::2])] + odd
-            moved = decay * first
-            second = decay * second + moved
+            moved = step_decay * first
+            second = step_decay * second + moved
             first = moved + total(terms[0])
         first_s[ct] = first + jnp.concatenate(firsts, axis=0)
         second_s[ct] = second + jnp.concatenate(seconds, axis=0)
@@ -361,12 +364,11 @@
 
 
 def block_kernel(
-    full, log_rates, residues, skip_weight, rate_ref, mixed_ref, carried_ref, starts, scales, results
+    full, log_rates, residues, skip_weight, rate_ref, dealt, starts, scales, results, result_s
 ):
-    tiles, rows, _ = mixed_ref.shape
-    modes = rate_ref.shape[1]
+    tiles, modes, _ = rate_ref.shape
     filters = tiles * TILE_FILTERS
-    steps = rows // SUB
+    steps = dealt.shape[2]
     half = modes // 2
     scaled = own_columns(residues[...], filters) * jnp.sqrt(
         jnp.exp(own_columns(log_rates[...], filters)) / full
@@ -376,27 +378,31 @@
         scales[n] = scaled[:, n * LANES : (n + 1) * LANES]
 
     def tile(ct, _):
-        rate = rate_ref[ct]
+        step_decay = jnp.exp(-rate_ref[ct])
+        sub_decay = jnp.exp(-rate_ref[ct] * float(steps))
         scale = scales[ct]
         weight = spread(skip_weight[pl.ds(ct, 1), :])
         for lo in range(0, modes, half):
-            rate_rows = [spread(rate[m : m + 1, :]) for m in range(lo, lo + half)]
-            decay = [jnp.exp(-r) for r in rate_rows]
+            decay = [spread(step_decay[m : m + 1, :]) for m in range(lo, lo + half)]
             gains = [spread(scale[m : m + 1, :]) for m in range(lo, lo + half)]
-            for way, x_ref in enumerate((mixed_ref, carried_ref)):
+            for way in range(2):
                 state = [starts[ct, way, lo + m] for m in range(half)]
                 if way:
-                    state = sub_starts_back(state, [jnp.exp(-r * float(steps)) for r in rate_rows])
+                    state = sub_starts_back(
+                        state, [spread(sub_decay[m : m + 1, :]) for m in range(lo, lo + half)]
+                    )
                 for i in range(steps - 1, -1, -1) if way else range(steps):
-                    at = pl.ds(i, SUB, stride=steps)
-                    x = x_ref[ct, at, :]
+                    x = dealt[ct, way, i]
                     state = [d * s + x for d, s in zip(decay, state)]
                     terms = [g * s for g, s in zip(gains, state)]
-                    terms.append(results[ct, way, at, :] if lo > 0 else weight * x)
+                    terms.append(result_s[way, i] if lo > 0 else weight * x)
                     while len(terms) > 1:
                         odd = terms[len(terms) // 2 * 2 :]
                         terms = [a + b for a, b in zip(terms[::2], terms[1::2])] + odd
-                    results[ct, way, at, :] = terms[0]
+                    if lo > 0:
+                        results[ct, way, pl.ds(i, SUB, stride=steps), :] = terms[0]
+                    else:
+                        result_s[way, i] = terms[0]
         return 0
 
     lax.fori_loop(0, tiles, tile, 0)
@@ -520,7 +526,7 @@
             pltpu.VMEM((rows, channels), BF16),
             pltpu.VMEM((rows, channels), BF16),
             pltpu.VMEM((rows, channels), BF16),
-            pltpu.VMEM((tiles, 4, 2 * TILE_FILTERS * modes, rows), BF16),
+            pltpu.VMEM((tiles, 4, TILE_FILTERS * modes, rows), BF16),
             pltpu.SemaphoreType.DMA((5,)),
         ],
         compiler_params=params,
@@ -530,10 +536,14 @@
 
     other_half = lax.dynamic_slice_in_dim(states, (1 - (position & 1)) * (4 * part), 4 * part, 0)
     partner = flip(other_half, 1)
-    sums, starts = call(
+    sums, starts, dealt = call(
         "within",
         within_kernel,
-        (shape(tail, LANES), shape(tiles, 2, modes, SUB, LANES)),
+        (
+            shape(tail, LANES),
+            shape(tiles, 2, modes, SUB, LANES),
+            shape(tiles, 2, rows // SUB, SUB, LANES),
+        ),
         (rate, mixed, carried, skip),
         ((tiles, modes, LANES), (tiles, modes, LANES)),
         12 * work,
@@ -561,11 +571,10 @@
                     residues_t,
                     skip_weight.reshape(tiles, LANES),
                     after(rate, own),
-                    mixed,
-                    carried,
+                    dealt,
                     starts,
                 ),
-                (),
+                ((2, rows // SUB, SUB, LANES),),
                 8 * work,
             )
             other = after(other, results)

time: 30.7 us -> 30.1 us (0.980)
  Pallas kernels: 13.4 us -> 12.3 us
  waiting for transfers between devices: 5.37 us -> 5.84 us
    pallas_call x6, Pallas kernels: 9.36 us -> 8.49 us  [call(): pl.pallas_call(kernel, out_shape=out_shape, in_specs=[vmem] * len(operand...]
    ppermute x7, waiting for transfers between devices: 5.37 us -> 5.84 us  [flip(): lax.ppermute(x, axis, [(i, i ^ step) for i in range(lax.axis_size(axis))])]
  transfers between devices with their start and end apart: 7 -> 7, of which waited for: 5 -> 5; matrix products, arithmetic and copies ran while one was open for 0% -> 0% of each run, Pallas kernels for 32% -> 29%
where the time goes in v4:
time: 30.1 us; the launch traced here: 29.8 us
  Pallas kernels  12.3 us (41%)
  starting transfers between devices  10.8 us (36%)
  waiting for transfers between devices  5.84 us (19%)
  between operations  0.7 us (2%)
    ppermute x7, starting transfers between devices, flip(): lax.ppermute(x, axis, [(i, i ^ step) for i in range(lax.axis_size(axis))])  10.8 us
    pallas_call x6, Pallas kernels, call(): pl.pallas_call(kernel, out_shape=out_shape, in_specs=[vmem] * len(operand...  8.49 us
    ppermute x7, waiting for transfers between devices, flip(): lax.ppermute(x, axis, [(i, i ^ step) for i in range(lax.axis_size(axis))])  5.84 us
    pallas_call x1, Pallas kernels, local(): pl.pallas_call(functools.partial(states_kernel, full), out_shape=(shape(8...  2.12 us
    pallas_call x1, Pallas kernels, local(): pl.pallas_call(grads_kernel, grid=(2,), out_shape=(jax.ShapeDtypeStruct((...  1.74 us
  transfers between devices with their start and end apart: 7, of which 5 were waited for; matrix products, arithmetic and copies ran while one was open for 0% of the time, Pallas kernels for 29%

profile of v4, /device:TPU:0, one launch (start us, length us, event | category | flops | bytes accessed | tf_op | source)
XLA Modules:
  0.0 29.8 jit_solution(502824321006518835)
XLA Ops:
  0.6 2.1 %states.1 = (f32[512,128]{1,0:T(8,128)S(1)}, f32[8,16,128]{2,1,0:T(8,128)S(1)}, f32[8,128,128]{2,1,0:T(8,128)S(1)}, f32[8,128,128]{2,1,0:T(8,128)S(1)}, f32[8,128]{1,0:T(8,128)S(1)}) custom-call(f32[16,256]{1,0:T(8,128)} %bitcast.6, bf16[128,1024]{1,0:T(8,128)(2,1)} %key.1, bf16[128,1024]{1,0:T(8,128)(2,1)} %values.1, bf16[128,1024]{1,0:T(8,128)(2,1)} %upstream.1, ...), custom_call_target="tpu_custom_call" | custom-call | tf_op jit(solution)/shard_map/states/pallas_call | solution.py:512
  2.8 3.0 %collective-permute-start = (f32[256,128]{1,0:T(8,128)S(1)}, f32[256,128]{1,0:T(8,128)S(1)}, u32[]{:S(2)}, u32[]{:S(2)}) collective-permute-start(f32[256,128]{1,0:T(8,128)S(1)} %constant_dynamic-slice_fusion), channel_id=1, source_target_pairs={{0,4},{4,0},{8,12},{12,8},{16,20},{20,16},{24,28},{28,24},{1,5},{5... | collective-permute-start | bytes 393224 | tf_op jit(solution)/shard_map/ppermute | solution.py:474
  5.8 4.0 %within.1 = (f32[24,128]{1,0:T(8,128)S(1)}, f32[8,2,16,8,128]{4,3,2,1,0:T(8,128)S(1)}, f32[8,2,16,8,128]{4,3,2,1,0:T(8,128)S(1)}) custom-call(f32[8,16,128]{2,1,0:T(8,128)S(1)} %get-tuple-element.43.rate_ref, f32[8,128,128]{2,1,0:T(8,128)S(1)} %get-tuple-element.37.mixed_ref, f32[8,128,128]{2,1,0:T(8,128)S(1)} %get-tuple-element.38.carried_ref, ...), custom_call_target="tpu_custom_call" | custom-call | flops 25165824 | bytes 6291456 | tf_op jit(solution)/shard_map/within/pallas_call | solution.py:500
  9.8 0.0 collective-permute-done.other_ref.partner_ref
  9.8 0.0 copy-start.4
  9.9 0.2 join.2
  10.1 1.6 %collective-permute-start.1 = (f32[280,128]{1,0:T(8,128)S(1)}, f32[280,128]{1,0:T(8,128)S(1)}, u32[]{:S(2)}, u32[]{:S(2)}) collective-permute-start(f32[280,128]{1,0:T(8,128)S(1)} %get-tuple-element.42.own_ref), channel_id=1, source_target_pairs={{0,8},{4,12},{8,0},{12,4},{16,24},{20,28},{24,16},{28,20},{1,9},{5... | collective-permute-start | bytes 430088 | tf_op jit(solution)/shard_map/ppermute | solution.py:474
  11.7 3.0 %block.1 = (f32[8,16,128]{2,1,0:T(8,128)S(1)}, f32[8,2,128,128]{3,2,1,0:T(8,128)S(1)}) custom-call(f32[16,256]{1,0:T(8,128)S(1)} %bitcast.7, f32[16,256]{1,0:T(8,128)S(1)} %bitcast.9, f32[8,128]{1,0:T(8,128)S(1)} %bitcast.11, f32[8,16,128]{2,1,0:T(8,128)S(1)} %get-tuple-element.43.rate_ref, f32[8,2,16,8,128]{4,3,2,1,0:T(8,128)S(1)} %get-tuple-element.44.dealt, ...), custom_call_target="tpu_custom_call" | custom-call | flops 16777216 | bytes 4194304 | tf_op jit(solution)/shard_map/block/pallas_call | solution.py:500
  14.8 0.6 %collective-permute-done.1.other_ref = f32[280,128]{1,0:T(8,128)S(1)} collective-permute-done((f32[280,128]{1,0:T(8,128)S(1)}, f32[280,128]{1,0:T(8,128)S(1)}, u32[]{:S(2)}, u32[]{:S(2)}) %collective-permute-start.1) | collective-permute-done | bytes 143392 | tf_op jit(solution)/shard_map/ppermute | solution.py:474
  15.4 0.3 join.3
  15.6 2.6 %collective-permute-start.2 = (f32[152,128]{1,0:T(8,128)S(1)}, f32[152,128]{1,0:T(8,128)S(1)}, u32[]{:S(2)}, u32[]{:S(2)}) collective-permute-start(f32[152,128]{1,0:T(8,128)S(1)} %get-tuple-element.50), channel_id=1, source_target_pairs={{0,16},{4,20},{8,24},{12,28},{16,0},{20,4},{24,8},{28,12},{1,17},{... | collective-permute-start | bytes 233480 | tf_op jit(solution)/shard_map/ppermute | solution.py:474
  18.2 2.7 %collective-permute-done.2.other_ref = f32[152,128]{1,0:T(8,128)S(1)} collective-permute-done((f32[152,128]{1,0:T(8,128)S(1)}, f32[152,128]{1,0:T(8,128)S(1)}, u32[]{:S(2)}, u32[]{:S(2)}) %collective-permute-start.2) | collective-permute-done | bytes 77856 | tf_op jit(solution)/shard_map/ppermute | solution.py:474
  20.9 0.3 last_join.1
  21.2 1.1 %collective-permute-start.3 = (f32[152,128]{1,0:T(8,128)S(1)}, f32[152,128]{1,0:T(8,128)S(1)}, u32[]{:S(2)}, u32[]{:S(2)}) collective-permute-start(f32[152,128]{1,0:T(8,128)S(1)} %get-tuple-element.53.back), channel_id=1, source_target_pairs={{0,4},{4,0},{8,12},{12,8},{16,20},{20,16},{24,28},{28,24},{1,5},{5... | collective-permute-start | bytes 233480 | tf_op jit(solution)/shard_map/ppermute | solution.py:474
  22.3 1.9 %collective-permute-start.5 = (f32[16,128]{1,0:T(8,128)S(1)}, f32[16,128]{1,0:T(8,128)S(1)}, u32[]{:S(2)}, u32[]{:S(2)}) collective-permute-start(f32[16,128]{1,0:T(8,128)S(1)} %get-tuple-element.58), channel_id=1, source_target_pairs={{0,6},{1,7},{2,4},{3,5},{4,2},{5,3},{6,0},{7,1},{8,14},{9,15},{10,... | collective-permute-start | bytes 24584 | tf_op jit(solution)/shard_map/ppermute | solution.py:474
  24.2 0.5 %collective-permute-start.4 = (f32[16,128]{1,0:T(8,128)S(1)}, f32[16,128]{1,0:T(8,128)S(1)}, u32[]{:S(2)}, u32[]{:S(2)}) collective-permute-start(f32[16,128]{1,0:T(8,128)S(1)} %get-tuple-element.58), channel_id=1, source_target_pairs={{0,2},{1,3},{2,0},{3,1},{4,6},{5,7},{6,4},{7,5},{8,10},{9,11},{10,... | collective-permute-start | bytes 24584 | tf_op jit(solution)/shard_map/ppermute | solution.py:474
  24.7 0.9 %collective-permute-done.3.theirs = f32[152,128]{1,0:T(8,128)S(1)} collective-permute-done((f32[152,128]{1,0:T(8,128)S(1)}, f32[152,128]{1,0:T(8,128)S(1)}, u32[]{:S(2)}, u32[]{:S(2)}) %collective-permute-start.3) | collective-permute-done | bytes 77856 | tf_op jit(solution)/shard_map/ppermute | solution.py:474
  25.6 0.0 copy-done
  25.6 1.7 %grads.1 = (bf16[128,1024]{1,0:T(8,128)(2,1)}, bf16[128,1024]{1,0:T(8,128)(2,1)}, bf16[128,1024]{1,0:T(8,128)(2,1)}) custom-call(f32[128,128]{1,0:T(8,128)S(1)} %get-tuple-element.52.mine, f32[152,128]{1,0:T(8,128)S(1)} %collective-permute-done.3.theirs, f32[8,16,128]{2,1,0:T(8,128)S(1)} %get-tuple-element.43.rate_ref, ...), custom_call_target="tpu_custom_call" | custom-call | flops 8388608 | bytes 2621440 | tf_op jit(solution)/shard_map/grads/pallas_call | solution.py:594
  27.4 0.0 collective-permute-done.5
  27.4 0.5 %collective-permute-done.4 = f32[16,128]{1,0:T(8,128)S(1)} collective-permute-done((f32[16,128]{1,0:T(8,128)S(1)}, f32[16,128]{1,0:T(8,128)S(1)}, u32[]{:S(2)}, u32[]{:S(2)}) %collective-permute-start.4) | collective-permute-done | bytes 8224 | tf_op jit(solution)/shard_map/ppermute | solution.py:474
  27.8 0.1 collective-permute-start.6
  27.9 1.2 %collective-permute-done.6.there = f32[32,128]{1,0:T(8,128)S(1)} collective-permute-done((f32[32,128]{1,0:T(8,128)S(1)}, f32[32,128]{1,0:T(8,128)S(1)}, u32[]{:S(2)}, u32[]{:S(2)}) %collective-permute-start.6) | collective-permute-done | bytes 16416 | tf_op jit(solution)/shard_map/ppermute | solution.py:474
  29.1 0.7 %final.1 = (f32[16,256]{1,0:T(8,128)}, f32[16,256]{1,0:T(8,128)}, f32[8,128]{1,0:T(8,128)}) custom-call(f32[16,256]{1,0:T(8,128)S(1)} %bitcast.8, f32[16,256]{1,0:T(8,128)S(1)} %bitcast.10, f32[152,128]{1,0:T(8,128)S(1)} %get-tuple-element.53.back, f32[152,128]{1,0:T(8,128)S(1)} %collective-permute-done.3.theirs, f32[32,128]{1,0:T(8,128)S(1)} %pad_maximum_fusion.here, ...), custom_call_target="tpu_custom_call" | custom-call | tf_op jit(solution)/shard_map/final/pallas_call | solution.py:500
  (14 shorter events, 0.0 us)
Async XLA Ops:
  2.8 7.0 %collective-permute-start = (f32[256,128]{1,0:T(8,128)S(1)}, f32[256,128]{1,0:T(8,128)S(1)}, u32[]{:S(2)}, u32[]{:S(2)}) collective-permute-start(f32[256,128]{1,0:T(8,128)S(1)} %constant_dynamic-slice_fusion), channel_id=1, source_target_pairs={{0,4},{4,0},{8,12},{12,8},{16,20},{20,16},{24,28},{28,24},{1,5},{5... | collective-permute-start | bytes 393224 | tf_op jit(solution)/shard_map/ppermute | solution.py:474
  9.8 1.9 %copy-start.3 = (f32[256,16]{0,1:T(8,128)S(1)}, f32[256,16]{0,1:T(8,128)}, u32[]{:S(2)}) copy-start(f32[256,16]{0,1:T(8,128)} %param.13) | copy-start | bytes 49156
  9.8 1.9 %copy-start.4 = (f32[256,16]{0,1:T(8,128)S(1)}, f32[256,16]{0,1:T(8,128)}, u32[]{:S(2)}) copy-start(f32[256,16]{0,1:T(8,128)} %param.12) | copy-start | bytes 49156
  10.1 1.6 %copy-start.5 = (f32[1024]{0:T(1024)S(1)}, f32[1024]{0:T(1024)}, u32[]{:S(2)}) copy-start(f32[1024]{0:T(1024)} %param.11) | copy-start | bytes 12292
  10.1 5.2 %collective-permute-start.1 = (f32[280,128]{1,0:T(8,128)S(1)}, f32[280,128]{1,0:T(8,128)S(1)}, u32[]{:S(2)}, u32[]{:S(2)}) collective-permute-start(f32[280,128]{1,0:T(8,128)S(1)} %get-tuple-element.42.own_ref), channel_id=1, source_target_pairs={{0,8},{4,12},{8,0},{12,4},{16,24},{20,28},{24,16},{28,20},{1,9},{5... | collective-permute-start | bytes 430088 | tf_op jit(solution)/shard_map/ppermute | solution.py:474
  15.4 10.3 %copy-start.2 = (bf16[128,1024]{1,0:T(8,128)(2,1)S(1)}, bf16[128,1024]{1,0:T(8,128)(2,1)}, u32[]{:S(2)}) copy-start(bf16[128,1024]{1,0:T(8,128)(2,1)} %upstream.1) | copy-start | bytes 786436
  15.6 5.3 %collective-permute-start.2 = (f32[152,128]{1,0:T(8,128)S(1)}, f32[152,128]{1,0:T(8,128)S(1)}, u32[]{:S(2)}, u32[]{:S(2)}) collective-permute-start(f32[152,128]{1,0:T(8,128)S(1)} %get-tuple-element.50), channel_id=1, source_target_pairs={{0,16},{4,20},{8,24},{12,28},{16,0},{20,4},{24,8},{28,12},{1,17},{... | collective-permute-start | bytes 233480 | tf_op jit(solution)/shard_map/ppermute | solution.py:474
  20.9 4.7 %copy-start = (bf16[128,1024]{1,0:T(8,128)(2,1)S(1)}, bf16[128,1024]{1,0:T(8,128)(2,1)}, u32[]{:S(2)}) copy-start(bf16[128,1024]{1,0:T(8,128)(2,1)} %key.1) | copy-start | bytes 786436
  20.9 4.7 %copy-start.1 = (bf16[128,1024]{1,0:T(8,128)(2,1)S(1)}, bf16[128,1024]{1,0:T(8,128)(2,1)}, u32[]{:S(2)}) copy-start(bf16[128,1024]{1,0:T(8,128)(2,1)} %values.1) | copy-start | bytes 786436
  21.2 4.4 %collective-permute-start.3 = (f32[152,128]{1,0:T(8,128)S(1)}, f32[152,128]{1,0:T(8,128)S(1)}, u32[]{:S(2)}, u32[]{:S(2)}) collective-permute-start(f32[152,128]{1,0:T(8,128)S(1)} %get-tuple-element.53.back), channel_id=1, source_target_pairs={{0,4},{4,0},{8,12},{12,8},{16,20},{20,16},{24,28},{28,24},{1,5},{5... | collective-permute-start | bytes 233480 | tf_op jit(solution)/shard_map/ppermute | solution.py:474
  22.3 5.1 %collective-permute-start.5 = (f32[16,128]{1,0:T(8,128)S(1)}, f32[16,128]{1,0:T(8,128)S(1)}, u32[]{:S(2)}, u32[]{:S(2)}) collective-permute-start(f32[16,128]{1,0:T(8,128)S(1)} %get-tuple-element.58), channel_id=1, source_target_pairs={{0,6},{1,7},{2,4},{3,5},{4,2},{5,3},{6,0},{7,1},{8,14},{9,15},{10,... | collective-permute-start | bytes 24584 | tf_op jit(solution)/shard_map/ppermute | solution.py:474
  24.2 3.7 %collective-permute-start.4 = (f32[16,128]{1,0:T(8,128)S(1)}, f32[16,128]{1,0:T(8,128)S(1)}, u32[]{:S(2)}, u32[]{:S(2)}) collective-permute-start(f32[16,128]{1,0:T(8,128)S(1)} %get-tuple-element.58), channel_id=1, source_target_pairs={{0,2},{1,3},{2,0},{3,1},{4,6},{5,7},{6,4},{7,5},{8,10},{9,11},{10,... | collective-permute-start | bytes 24584 | tf_op jit(solution)/shard_map/ppermute | solution.py:474
  27.8 1.2 %collective-permute-start.6 = (f32[32,128]{1,0:T(8,128)S(1)}, f32[32,128]{1,0:T(8,128)S(1)}, u32[]{:S(2)}, u32[]{:S(2)}) collective-permute-start(f32[32,128]{1,0:T(8,128)S(1)} %pad_maximum_fusion.here), channel_id=1, source_target_pairs={{0,1},{1,0},{2,3},{3,2},{4,5},{5,4},{6,7},{7,6},{8,9},{9,8},{10,11... | collective-permute-start | bytes 49160 | tf_op jit(solution)/shard_map/ppermute | solution.py:474

commit v5 on v4

--- a/solution.py
+++ b/solution.py
@@ -408,42 +408,53 @@
     lax.fori_loop(0, tiles, tile, 0)
 
 
-def grads_kernel(mine, theirs, rate_ref, scale_ref, results, key, values, upstream, *refs):
-    query_grad, key_grad, value_grad = refs
+def reach_kernel(rate_ref, reach):
+    tiles, modes, _ = rate_ref.shape
+    rows = reach.shape[3]
+    lane = lax.broadcasted_iota(jnp.int32, (modes, LANES), 1)
+    own_mode = lax.broadcasted_iota(jnp.int32, (modes, LANES), 0) == lax.rem(lane, modes)
+    time = lax.broadcasted_iota(jnp.int32, (rows, LANES), 0).astype(F32)
+    for ct in range(tiles):
+        rate_row = jnp.sum(jnp.where(own_mode, rate_ref[ct], 0.0), axis=0, keepdims=True)
+        for way, away in enumerate((time + 1.0, float(rows) - time)):
+            high, low = split(jnp.exp(-rate_row * away))
+            reach[ct, way, 0] = high
+            reach[ct, way, 1] = low
+
+
+def grads_kernel(mine, theirs, reach, scale_ref, results, key, values, upstream, *refs):
+    outs, made, sems = refs[:3], refs[3:6], refs[6]
     tiles, modes, _ = scale_ref.shape
-    rows = key.shape[0]
     share = tiles // 2
     part = share * modes
     second_half = (lax.axis_index("ctx") & 1) != 0
-    lane = lax.broadcasted_iota(jnp.int32, (modes, LANES), 1)
-    own_mode = lax.broadcasted_iota(jnp.int32, (modes, LANES), 0) == lax.rem(lane, modes)
-    lane_filter = lax.div(lane, GROUP_CH)
-    time = lax.broadcasted_iota(jnp.int32, (rows, LANES), 0).astype(F32)
-
-    def piece(p):
-        is_mine = second_half if p else jnp.logical_not(second_half)
-        for n in range(share):
-            ct = p * share + n
-            rate = rate_ref[ct]
-            rate_row = jnp.sum(jnp.where(own_mode, rate, 0.0), axis=0, keepdims=True)
-            parts = []
-            for offset, away in ((0, time + 1.0), (part, float(rows) - time)):
-                at = slice(offset + n * modes, offset + (n + 1) * modes)
-                edge = scale_ref[ct] * jnp.where(is_mine, mine[at, :], theirs[at, :])
-                spaced = jnp.concatenate(
-                    [jnp.where(lane_filter == f, edge, 0.0) for f in range(TILE_FILTERS)], axis=0
+    lane_filter = lax.div(lax.broadcasted_iota(jnp.int32, (modes, LANES), 1), GROUP_CH)
+    copies = []
+    for ct in range(tiles):
+        is_mine = second_half if ct >= share else jnp.logical_not(second_half)
+        parts = []
+        for way in range(2):
+            at = slice(way * part + ct % share * modes, way * part + (ct % share + 1) * modes)
+            edge = scale_ref[ct] * jnp.where(is_mine, mine[at, :], theirs[at, :])
+            spaced = jnp.concatenate(
+                [jnp.where(lane_filter == f, edge, 0.0) for f in range(TILE_FILTERS)], axis=0
+            )
+            parts.append(wide_dot(reach[ct, way, 0], reach[ct, way, 1], *split(spaced)))
+        lanes = slice(ct * LANES, (ct + 1) * LANES)
+        mixed_grad = results[ct, 1] + parts[1]
+        for made_ref, factor, grad in zip(
+            made, (upstream, values, key), (results[ct, 0] + parts[0], mixed_grad, mixed_grad)
+        ):
+            made_ref[:, lanes] = (factor[:, lanes].astype(F32) * grad).astype(made_ref.dtype)
+        if ct % 2 == 1:
+            lanes = slice((ct - 1) * LANES, (ct + 1) * LANES)
+            for n, (made_ref, out) in enumerate(zip(made, outs)):
+                copies.append(
+                    pltpu.make_async_copy(made_ref.at[:, lanes], out.at[:, lanes], sems.at[ct // 2, n])
                 )
-                parts.append(wide_dot(*split(jnp.exp(-rate_row * away)), *split(spaced)))
-            lanes = slice(n * LANES, (n + 1) * LANES)
-            query_grad[:, lanes] = (
-                upstream[:, lanes].astype(F32) * (results[ct, 0] + parts[0])
-            ).astype(query_grad.dtype)
-            mixed_grad = results[ct, 1] + parts[1]
-            key_grad[:, lanes] = (mixed_grad * values[:, lanes].astype(F32)).astype(key_grad.dtype)
-            value_grad[:, lanes] = (mixed_grad * key[:, lanes].astype(F32)).astype(value_grad.dtype)
-
-    for p in range(2):
-        pl.when(pl.program_id(0) == p)(functools.partial(piece, p))
+                copies[-1].start()
+    for copy in copies:
+        copy.wait()
 
 
 def final_kernel(
@@ -454,7 +465,13 @@
     group = lax.axis_index("grp")
     skip_rows = slice(back.shape[0] - skip_grad.shape[0], back.shape[0])
     skip_grad[...] = (back[skip_rows, :] + theirs[skip_rows, :]) / jnp.sqrt(jnp.float32(full))
-    by_distance = [here[:modes, :], there[:modes, :], here[modes:, :], there[modes:, :]]
+    rows = [slice(n * modes, (n + 1) * modes) for n in range(3)]
+    by_distance = [
+        here[rows[0], :],
+        there[rows[0], :],
+        here[rows[1], :] + there[rows[2], :],
+        here[rows[2], :] + there[rows[1], :],
+    ]
     totals = []
     for g in range(total_filters // filters):
         total = by_distance[0]
@@ -548,7 +565,7 @@
         ((tiles, modes, LANES), (tiles, modes, LANES)),
         12 * work,
     )
-    scale = results = None
+    scale = results = reach = None
     step = 1
     own, other, extra = states, after(partner, sums), (sums,)
     while 2 * step < context:
@@ -578,6 +595,16 @@
                 8 * work,
             )
             other = after(other, results)
+        if is_last_next:
+            reach = pl.pallas_call(
+                reach_kernel,
+                out_shape=jax.ShapeDtypeStruct((tiles, 2, 2, rows, LANES), BF16),
+                in_specs=[vmem],
+                out_specs=vmem,
+                compiler_params=params,
+                name="reach",
+            )(after(rate, own))
+            other = after(other, reach)
         extra = (borders,)
         step *= 2
     mine, back, modal = call(
@@ -587,26 +614,30 @@
         (rate, own, other, borders, states, partner),
     )
 
-    everyone = ("ctx", "grp")
+    duo = jnp.concatenate([modal, flip(modal, 1, "grp")], axis=0)
     theirs = flip(back, 1)
-    across, level = flip(modal, groups + 2, everyone), flip(modal, 2, everyone)
-    columns = pl.BlockSpec((rows, channels // 2), lambda i: (0, i))
+    far = lax.ppermute(
+        duo,
+        ("ctx", "grp"),
+        [(i, i ^ (groups + 2 if i & 1 else 2)) for i in range(context * groups)],
+    )
+    grad = jax.ShapeDtypeStruct((rows, channels), BF16)
     outputs = pl.pallas_call(
         grads_kernel,
-        grid=(2,),
-        out_shape=(jax.ShapeDtypeStruct((rows, channels), BF16),) * 3,
-        in_specs=[vmem] * 5 + [columns] * 3,
-        out_specs=(columns,) * 3,
+        out_shape=(grad,) * 3,
+        in_specs=[vmem] * 8,
+        out_specs=(in_hbm,) * 3,
+        scratch_shapes=[pltpu.VMEM((rows, channels), BF16)] * 3
+        + [pltpu.SemaphoreType.DMA((tiles // 2, 3))],
         compiler_params=params,
         cost_estimate=pl.CostEstimate(
             flops=4 * work, transcendentals=0, bytes_accessed=20 * rows * channels
         ),
         name="grads",
-    )(mine, theirs, rate, scale, results, key_gate, values, upstream)
+    )(mine, theirs, reach, scale, results, key_gate, values, upstream)
     query_grad, key_grad, value_grad = outputs
-    across, level = (after(x, *outputs) for x in (across, level))
-    here = jnp.concatenate([modal + theirs[2 * part : 2 * part + modes], level + across], axis=0)
-    there = flip(here, 1, "grp")
+    here = jnp.concatenate([modal + theirs[2 * part : 2 * part + modes], far], axis=0)
+    there = after(flip(here, 1, "grp"), *outputs)
     residue_grad, log_rate_grad, skip_grad = call(
         "final",
         functools.partial(final_kernel, full),

time: 30.1 us -> 28.6 us (0.950)
  starting transfers between devices: 10.8 us -> 9.84 us
  waiting for transfers between devices: 5.84 us -> 5.37 us
    ppermute x7 -> x6, starting transfers between devices: 10.8 us -> 8.35 us  [flip(): lax.ppermute(x, axis, [(i, i ^ step) for i in range(lax.axis_size(axis))])]
    ppermute x0 -> x1, starting transfers between devices: none -> 1.49 us  [local(): lax.ppermute(duo, ('ctx', 'grp'), [(i, i ^ (groups + 2 if i & 1 else 2))...]
    ppermute x7 -> x6, waiting for transfers between devices: 5.84 us -> 5.24 us  [flip(): lax.ppermute(x, axis, [(i, i ^ step) for i in range(lax.axis_size(axis))])]
    pallas_call x1 -> x2, Pallas kernels: 1.74 us -> 1.64 us  [the longest x1 1.4 us: local(): pl.pallas_call(grads_kernel, out_shape=(grad,) * 3, in_specs=[vmem] * 8,...]
  transfers between devices with their start and end apart: 7 -> 7, of which waited for: 5 -> 5; matrix products, arithmetic and copies ran while one was open for 0% -> 0% of each run, Pallas kernels for 29% -> 31%
where the time goes in v5:
time: 28.6 us; the launch traced here: 28.3 us
  Pallas kernels  12.3 us (43%)
  starting transfers between devices  9.84 us (34%)
  waiting for transfers between devices  5.37 us (19%)
  between operations  0.72 us (3%)
    pallas_call x6, Pallas kernels, call(): pl.pallas_call(kernel, out_shape=out_shape, in_specs=[vmem] * len(operand...  8.51 us
    ppermute x6, starting transfers between devices, flip(): lax.ppermute(x, axis, [(i, i ^ step) for i in range(lax.axis_size(axis))])  8.35 us
    ppermute x6, waiting for transfers between devices, flip(): lax.ppermute(x, axis, [(i, i ^ step) for i in range(lax.axis_size(axis))])  5.24 us
    pallas_call x1, Pallas kernels, local(): pl.pallas_call(functools.partial(states_kernel, full), out_shape=(shape(8...  2.12 us
    ppermute x1, starting transfers between devices, local(): lax.ppermute(duo, ('ctx', 'grp'), [(i, i ^ (groups + 2 if i & 1 else 2))...  1.49 us
    pallas_call x1, Pallas kernels, local(): pl.pallas_call(grads_kernel, out_shape=(grad,) * 3, in_specs=[vmem] * 8,...  1.4 us
  transfers between devices with their start and end apart: 7, of which 5 were waited for; matrix products, arithmetic and copies ran while one was open for 0% of the time, Pallas kernels for 31%

profile of v5, /device:TPU:0, one launch (start us, length us, event | category | flops | bytes accessed | tf_op | source)
XLA Modules:
  0.0 28.3 jit_solution(16116628729436496432)
XLA Ops:
  0.6 2.1 %states.1 = (f32[512,128]{1,0:T(8,128)S(1)}, f32[8,16,128]{2,1,0:T(8,128)S(1)}, f32[8,128,128]{2,1,0:T(8,128)S(1)}, f32[8,128,128]{2,1,0:T(8,128)S(1)}, f32[8,128]{1,0:T(8,128)S(1)}) custom-call(f32[16,256]{1,0:T(8,128)} %bitcast.6, bf16[128,1024]{1,0:T(8,128)(2,1)} %key.1, bf16[128,1024]{1,0:T(8,128)(2,1)} %values.1, bf16[128,1024]{1,0:T(8,128)(2,1)} %upstream.1, ...), custom_call_target="tpu_custom_call" | custom-call | tf_op jit(solution)/shard_map/states/pallas_call | solution.py:529
  2.8 3.0 %collective-permute-start = (f32[256,128]{1,0:T(8,128)S(1)}, f32[256,128]{1,0:T(8,128)S(1)}, u32[]{:S(2)}, u32[]{:S(2)}) collective-permute-start(f32[256,128]{1,0:T(8,128)S(1)} %constant_dynamic-slice_fusion), channel_id=1, source_target_pairs={{0,4},{4,0},{8,12},{12,8},{16,20},{20,16},{24,28},{28,24},{1,5},{5... | collective-permute-start | bytes 393224 | tf_op jit(solution)/shard_map/ppermute | solution.py:491
  5.8 4.0 %within.1 = (f32[24,128]{1,0:T(8,128)S(1)}, f32[8,2,16,8,128]{4,3,2,1,0:T(8,128)S(1)}, f32[8,2,16,8,128]{4,3,2,1,0:T(8,128)S(1)}) custom-call(f32[8,16,128]{2,1,0:T(8,128)S(1)} %get-tuple-element.52.rate_ref, f32[8,128,128]{2,1,0:T(8,128)S(1)} %get-tuple-element.38.mixed_ref, f32[8,128,128]{2,1,0:T(8,128)S(1)} %get-tuple-element.39.carried_ref, ...), custom_call_target="tpu_custom_call" | custom-call | flops 25165824 | bytes 6291456 | tf_op jit(solution)/shard_map/within/pallas_call | solution.py:517
  9.8 0.0 collective-permute-done.other_ref.partner_ref
  9.8 0.0 copy-start.4
  9.9 0.2 join.2
  10.1 1.6 %collective-permute-start.1 = (f32[280,128]{1,0:T(8,128)S(1)}, f32[280,128]{1,0:T(8,128)S(1)}, u32[]{:S(2)}, u32[]{:S(2)}) collective-permute-start(f32[280,128]{1,0:T(8,128)S(1)} %get-tuple-element.43.own_ref), channel_id=1, source_target_pairs={{0,8},{4,12},{8,0},{12,4},{16,24},{20,28},{24,16},{28,20},{1,9},{5... | collective-permute-start | bytes 430088 | tf_op jit(solution)/shard_map/ppermute | solution.py:491
  11.7 3.0 %block.1 = (f32[8,16,128]{2,1,0:T(8,128)S(1)}, f32[8,2,128,128]{3,2,1,0:T(8,128)S(1)}) custom-call(f32[16,256]{1,0:T(8,128)S(1)} %bitcast.7, f32[16,256]{1,0:T(8,128)S(1)} %bitcast.9, f32[8,128]{1,0:T(8,128)S(1)} %bitcast.11, f32[8,16,128]{2,1,0:T(8,128)S(1)} %get-tuple-element.52.rate_ref, f32[8,2,16,8,128]{4,3,2,1,0:T(8,128)S(1)} %get-tuple-element.45.dealt, ...), custom_call_target="tpu_custom_call" | custom-call | flops 16777216 | bytes 4194304 | tf_op jit(solution)/shard_map/block/pallas_call | solution.py:517
  14.8 0.6 %collective-permute-done.1.other_ref = f32[280,128]{1,0:T(8,128)S(1)} collective-permute-done((f32[280,128]{1,0:T(8,128)S(1)}, f32[280,128]{1,0:T(8,128)S(1)}, u32[]{:S(2)}, u32[]{:S(2)}) %collective-permute-start.1) | collective-permute-done | bytes 143392 | tf_op jit(solution)/shard_map/ppermute | solution.py:491
  15.4 0.3 join.3
  15.6 2.6 %collective-permute-start.2 = (f32[152,128]{1,0:T(8,128)S(1)}, f32[152,128]{1,0:T(8,128)S(1)}, u32[]{:S(2)}, u32[]{:S(2)}) collective-permute-start(f32[152,128]{1,0:T(8,128)S(1)} %get-tuple-element.51), channel_id=1, source_target_pairs={{0,16},{4,20},{8,24},{12,28},{16,0},{20,4},{24,8},{28,12},{1,17},{... | collective-permute-start | bytes 233480 | tf_op jit(solution)/shard_map/ppermute | solution.py:491
  18.2 0.2 reach.1
  18.5 2.5 %collective-permute-done.2.other_ref = f32[152,128]{1,0:T(8,128)S(1)} collective-permute-done((f32[152,128]{1,0:T(8,128)S(1)}, f32[152,128]{1,0:T(8,128)S(1)}, u32[]{:S(2)}, u32[]{:S(2)}) %collective-permute-start.2) | collective-permute-done | bytes 77856 | tf_op jit(solution)/shard_map/ppermute | solution.py:491
  20.9 0.3 last_join.1
  21.2 0.0 collective-permute-start.4
  21.2 1.1 %collective-permute-start.3 = (f32[152,128]{1,0:T(8,128)S(1)}, f32[152,128]{1,0:T(8,128)S(1)}, u32[]{:S(2)}, u32[]{:S(2)}) collective-permute-start(f32[152,128]{1,0:T(8,128)S(1)} %get-tuple-element.56.back), channel_id=1, source_target_pairs={{0,4},{4,0},{8,12},{12,8},{16,20},{20,16},{24,28},{28,24},{1,5},{5... | collective-permute-start | bytes 233480 | tf_op jit(solution)/shard_map/ppermute | solution.py:491
  22.3 0.1 collective-permute-done.4
  22.4 1.5 %collective-permute-start.5 = (f32[32,128]{1,0:T(8,128)S(1)}, f32[32,128]{1,0:T(8,128)S(1)}, u32[]{:S(2)}, u32[]{:S(2)}) collective-permute-start(f32[32,128]{1,0:T(8,128)S(1)} %pad_maximum_fusion.1), channel_id=1, source_target_pairs={{0,2},{1,7},{2,0},{3,5},{4,6},{5,3},{6,4},{7,1},{8,10},{9,15},{10,... | collective-permute-start | bytes 49160 | tf_op jit(solution)/shard_map/ppermute | solution.py:619
  23.9 2.1 %collective-permute-done.3.theirs = f32[152,128]{1,0:T(8,128)S(1)} collective-permute-done((f32[152,128]{1,0:T(8,128)S(1)}, f32[152,128]{1,0:T(8,128)S(1)}, u32[]{:S(2)}, u32[]{:S(2)}) %collective-permute-start.3) | collective-permute-done | bytes 77856 | tf_op jit(solution)/shard_map/ppermute | solution.py:491
  26.0 0.1 collective-permute-done.5
  26.1 0.0 collective-permute-start.6
  26.2 1.4 %grads.1 = (bf16[128,1024]{1,0:T(8,128)(2,1)}, bf16[128,1024]{1,0:T(8,128)(2,1)}, bf16[128,1024]{1,0:T(8,128)(2,1)}) custom-call(f32[128,128]{1,0:T(8,128)S(1)} %get-tuple-element.55.mine, f32[152,128]{1,0:T(8,128)S(1)} %collective-permute-done.3.theirs, bf16[8,2,2,128,128]{4,3,2,1,0:T(8,128)(2,1)S(1)} %reach.1, ...), custom_call_target="tpu_custom_call" | custom-call | flops 8388608 | bytes 2621440 | tf_op jit(solution)/shard_map/grads/pallas_call | solution.py:625
  27.6 0.0 collective-permute-done.6.there
  27.6 0.7 %final.1 = (f32[16,256]{1,0:T(8,128)}, f32[16,256]{1,0:T(8,128)}, f32[8,128]{1,0:T(8,128)}) custom-call(f32[16,256]{1,0:T(8,128)S(1)} %bitcast.8, f32[16,256]{1,0:T(8,128)S(1)} %bitcast.10, f32[152,128]{1,0:T(8,128)S(1)} %get-tuple-element.56.back, f32[152,128]{1,0:T(8,128)S(1)} %collective-permute-done.3.theirs, f32[48,128]{1,0:T(8,128)S(1)} %pad_maximum_fusion.here, ...), custom_call_target="tpu_custom_call" | custom-call | tf_op jit(solution)/shard_map/final/pallas_call | solution.py:517
  (15 shorter events, 0.0 us)
Async XLA Ops:
  2.8 7.0 %collective-permute-start = (f32[256,128]{1,0:T(8,128)S(1)}, f32[256,128]{1,0:T(8,128)S(1)}, u32[]{:S(2)}, u32[]{:S(2)}) collective-permute-start(f32[256,128]{1,0:T(8,128)S(1)} %constant_dynamic-slice_fusion), channel_id=1, source_target_pairs={{0,4},{4,0},{8,12},{12,8},{16,20},{20,16},{24,28},{28,24},{1,5},{5... | collective-permute-start | bytes 393224 | tf_op jit(solution)/shard_map/ppermute | solution.py:491
  9.8 1.9 %copy-start.3 = (f32[256,16]{0,1:T(8,128)S(1)}, f32[256,16]{0,1:T(8,128)}, u32[]{:S(2)}) copy-start(f32[256,16]{0,1:T(8,128)} %param.13) | copy-start | bytes 49156
  9.8 1.9 %copy-start.4 = (f32[256,16]{0,1:T(8,128)S(1)}, f32[256,16]{0,1:T(8,128)}, u32[]{:S(2)}) copy-start(f32[256,16]{0,1:T(8,128)} %param.12) | copy-start | bytes 49156
  10.1 1.6 %copy-start.5 = (f32[1024]{0:T(1024)S(1)}, f32[1024]{0:T(1024)}, u32[]{:S(2)}) copy-start(f32[1024]{0:T(1024)} %param.11) | copy-start | bytes 12292
  10.1 5.2 %collective-permute-start.1 = (f32[280,128]{1,0:T(8,128)S(1)}, f32[280,128]{1,0:T(8,128)S(1)}, u32[]{:S(2)}, u32[]{:S(2)}) collective-permute-start(f32[280,128]{1,0:T(8,128)S(1)} %get-tuple-element.43.own_ref), channel_id=1, source_target_pairs={{0,8},{4,12},{8,0},{12,4},{16,24},{20,28},{24,16},{28,20},{1,9},{5... | collective-permute-start | bytes 430088 | tf_op jit(solution)/shard_map/ppermute | solution.py:491
  15.6 5.3 %collective-permute-start.2 = (f32[152,128]{1,0:T(8,128)S(1)}, f32[152,128]{1,0:T(8,128)S(1)}, u32[]{:S(2)}, u32[]{:S(2)}) collective-permute-start(f32[152,128]{1,0:T(8,128)S(1)} %get-tuple-element.51), channel_id=1, source_target_pairs={{0,16},{4,20},{8,24},{12,28},{16,0},{20,4},{24,8},{28,12},{1,17},{... | collective-permute-start | bytes 233480 | tf_op jit(solution)/shard_map/ppermute | solution.py:491
  20.9 5.2 %copy-start = (bf16[128,1024]{1,0:T(8,128)(2,1)S(1)}, bf16[128,1024]{1,0:T(8,128)(2,1)}, u32[]{:S(2)}) copy-start(bf16[128,1024]{1,0:T(8,128)(2,1)} %key.1) | copy-start | bytes 786436
  20.9 5.2 %copy-start.1 = (bf16[128,1024]{1,0:T(8,128)(2,1)S(1)}, bf16[128,1024]{1,0:T(8,128)(2,1)}, u32[]{:S(2)}) copy-start(bf16[128,1024]{1,0:T(8,128)(2,1)} %values.1) | copy-start | bytes 786436
  20.9 5.2 %copy-start.2 = (bf16[128,1024]{1,0:T(8,128)(2,1)S(1)}, bf16[128,1024]{1,0:T(8,128)(2,1)}, u32[]{:S(2)}) copy-start(bf16[128,1024]{1,0:T(8,128)(2,1)} %upstream.1) | copy-start | bytes 786436
  21.2 1.2 %collective-permute-start.4 = (f32[16,128]{1,0:T(8,128)S(1)}, f32[16,128]{1,0:T(8,128)S(1)}, u32[]{:S(2)}, u32[]{:S(2)}) collective-permute-start(f32[16,128]{1,0:T(8,128)S(1)} %get-tuple-element.61), channel_id=1, source_target_pairs={{0,1},{1,0},{2,3},{3,2},{4,5},{5,4},{6,7},{7,6},{8,9},{9,8},{10,11... | collective-permute-start | bytes 24584 | tf_op jit(solution)/shard_map/ppermute | solution.py:491
  21.2 4.8 %collective-permute-start.3 = (f32[152,128]{1,0:T(8,128)S(1)}, f32[152,128]{1,0:T(8,128)S(1)}, u32[]{:S(2)}, u32[]{:S(2)}) collective-permute-start(f32[152,128]{1,0:T(8,128)S(1)} %get-tuple-element.56.back), channel_id=1, source_target_pairs={{0,4},{4,0},{8,12},{12,8},{16,20},{20,16},{24,28},{28,24},{1,5},{5... | collective-permute-start | bytes 233480 | tf_op jit(solution)/shard_map/ppermute | solution.py:491
  22.4 3.7 %collective-permute-start.5 = (f32[32,128]{1,0:T(8,128)S(1)}, f32[32,128]{1,0:T(8,128)S(1)}, u32[]{:S(2)}, u32[]{:S(2)}) collective-permute-start(f32[32,128]{1,0:T(8,128)S(1)} %pad_maximum_fusion.1), channel_id=1, source_target_pairs={{0,2},{1,7},{2,0},{3,5},{4,6},{5,3},{6,4},{7,1},{8,10},{9,15},{10,... | collective-permute-start | bytes 49160 | tf_op jit(solution)/shard_map/ppermute | solution.py:619
  26.1 1.4 %collective-permute-start.6 = (f32[48,128]{1,0:T(8,128)S(1)}, f32[48,128]{1,0:T(8,128)S(1)}, u32[]{:S(2)}, u32[]{:S(2)}) collective-permute-start(f32[48,128]{1,0:T(8,128)S(1)} %pad_maximum_fusion.here), channel_id=1, source_target_pairs={{0,1},{1,0},{2,3},{3,2},{4,5},{5,4},{6,7},{7,6},{8,9},{9,8},{10,11... | collective-permute-start | bytes 73736 | tf_op jit(solution)/shard_map/ppermute | solution.py:491

commit v6 on v5

--- a/solution.py
+++ b/solution.py
@@ -408,7 +408,13 @@
     lax.fori_loop(0, tiles, tile, 0)
 
 
-def reach_kernel(rate_ref, reach):
+def reach_kernel(full, rate_ref, log_rates, residues, reach, factors):
+    rates = jnp.exp(log_rates[...])
+    scale_root = jnp.sqrt(jnp.float32(full))
+    factor = jnp.sqrt(rates / full) / scale_root
+    factors[0] = factor
+    factors[1] = residues[...] * factor * 0.5
+    factors[2] = residues[...] * factor * (rates / full)
     tiles, modes, _ = rate_ref.shape
     rows = reach.shape[3]
     lane = lax.broadcasted_iota(jnp.int32, (modes, LANES), 1)
@@ -422,35 +428,38 @@
             reach[ct, way, 1] = low
 
 
-def grads_kernel(mine, theirs, reach, scale_ref, results, key, values, upstream, *refs):
-    outs, made, sems = refs[:3], refs[3:6], refs[6]
+def grads_kernel(is_own, edges, reach, scale_ref, results, key, values, upstream, *refs):
+    outs, made, sems = refs[-7:-4], refs[-4:-1], refs[-1]
     tiles, modes, _ = scale_ref.shape
     share = tiles // 2
     part = share * modes
-    second_half = (lax.axis_index("ctx") & 1) != 0
+    second_half = lax.axis_index("ctx") & 1
+    begin = (second_half if is_own else 1 - second_half) * share
     lane_filter = lax.div(lax.broadcasted_iota(jnp.int32, (modes, LANES), 1), GROUP_CH)
     copies = []
-    for ct in range(tiles):
-        is_mine = second_half if ct >= share else jnp.logical_not(second_half)
+    for n in range(share):
+        ct = begin + n
         parts = []
         for way in range(2):
-            at = slice(way * part + ct % share * modes, way * part + (ct % share + 1) * modes)
-            edge = scale_ref[ct] * jnp.where(is_mine, mine[at, :], theirs[at, :])
+            at = slice(way * part + n * modes, way * part + (n + 1) * modes)
+            edge = scale_ref[ct] * edges[at, :]
             spaced = jnp.concatenate(
                 [jnp.where(lane_filter == f, edge, 0.0) for f in range(TILE_FILTERS)], axis=0
             )
             parts.append(wide_dot(reach[ct, way, 0], reach[ct, way, 1], *split(spaced)))
-        lanes = slice(ct * LANES, (ct + 1) * LANES)
+        there = pl.ds(pl.multiple_of(ct * LANES, LANES), LANES)
+        here = slice(n * LANES, (n + 1) * LANES)
         mixed_grad = results[ct, 1] + parts[1]
         for made_ref, factor, grad in zip(
             made, (upstream, values, key), (results[ct, 0] + parts[0], mixed_grad, mixed_grad)
         ):
-            made_ref[:, lanes] = (factor[:, lanes].astype(F32) * grad).astype(made_ref.dtype)
-        if ct % 2 == 1:
-            lanes = slice((ct - 1) * LANES, (ct + 1) * LANES)
-            for n, (made_ref, out) in enumerate(zip(made, outs)):
+            made_ref[:, here] = (factor[:, there].astype(F32) * grad).astype(made_ref.dtype)
+        if n % 2 == 1:
+            here = slice((n - 1) * LANES, (n + 1) * LANES)
+            there = pl.ds(pl.multiple_of((ct - 1) * LANES, LANES), 2 * LANES)
+            for k, (made_ref, out) in enumerate(zip(made, outs)):
                 copies.append(
-                    pltpu.make_async_copy(made_ref.at[:, lanes], out.at[:, lanes], sems.at[ct // 2, n])
+                    pltpu.make_async_copy(made_ref.at[:, here], out.at[:, there], sems.at[n // 2, k])
                 )
                 copies[-1].start()
     for copy in copies:
@@ -458,9 +467,9 @@
 
 
 def final_kernel(
-    full, log_rates, residues, back, theirs, here, there, residue_grad, log_rate_grad, skip_grad
+    full, factors, back, theirs, here, there, residue_grad, log_rate_grad, skip_grad
 ):
-    modes, total_filters = log_rates.shape
+    _, modes, total_filters = factors.shape
     filters = here.shape[1] // 2
     group = lax.axis_index("grp")
     skip_rows = slice(back.shape[0] - skip_grad.shape[0], back.shape[0])
@@ -479,12 +488,9 @@
             total = jnp.where((group ^ k) == g, by_distance[k], total)
         totals.append(total)
     first_sum = jnp.concatenate([t[:, :filters] for t in totals], axis=1)
-    second_sum = jnp.concatenate([t[:, filters:] for t in totals], axis=1) * (1.0 / full)
-    rates = jnp.exp(log_rates[...])
-    root = jnp.sqrt(rates / full)
-    scale_root = jnp.sqrt(jnp.float32(full))
-    residue_grad[...] = root * first_sum / scale_root
-    log_rate_grad[...] = residues[...] * root * (0.5 * first_sum - rates * second_sum) / scale_root
+    second_sum = jnp.concatenate([t[:, filters:] for t in totals], axis=1)
+    residue_grad[...] = factors[0] * first_sum
+    log_rate_grad[...] = factors[1] * first_sum - factors[2] * second_sum
 
 
 def flip(x, step, axis="ctx"):
@@ -565,7 +571,7 @@
         ((tiles, modes, LANES), (tiles, modes, LANES)),
         12 * work,
     )
-    scale = results = reach = None
+    scale = results = reach = factors = None
     step = 1
     own, other, extra = states, after(partner, sums), (sums,)
     while 2 * step < context:
@@ -596,14 +602,17 @@
             )
             other = after(other, results)
         if is_last_next:
-            reach = pl.pallas_call(
-                reach_kernel,
-                out_shape=jax.ShapeDtypeStruct((tiles, 2, 2, rows, LANES), BF16),
-                in_specs=[vmem],
-                out_specs=vmem,
+            reach, factors = pl.pallas_call(
+                functools.partial(reach_kernel, full),
+                out_shape=(
+                    jax.ShapeDtypeStruct((tiles, 2, 2, rows, LANES), BF16),
+                    shape(3, modes, total_filters),
+                ),
+                in_specs=[vmem] * 3,
+                out_specs=(vmem,) * 2,
                 compiler_params=params,
                 name="reach",
-            )(after(rate, own))
+            )(after(rate, own), log_rates_t, residues_t)
             other = after(other, reach)
         extra = (borders,)
         step *= 2
@@ -622,19 +631,27 @@
         [(i, i ^ (groups + 2 if i & 1 else 2)) for i in range(context * groups)],
     )
     grad = jax.ShapeDtypeStruct((rows, channels), BF16)
-    outputs = pl.pallas_call(
-        grads_kernel,
-        out_shape=(grad,) * 3,
-        in_specs=[vmem] * 8,
-        out_specs=(in_hbm,) * 3,
-        scratch_shapes=[pltpu.VMEM((rows, channels), BF16)] * 3
-        + [pltpu.SemaphoreType.DMA((tiles // 2, 3))],
-        compiler_params=params,
-        cost_estimate=pl.CostEstimate(
-            flops=4 * work, transcendentals=0, bytes_accessed=20 * rows * channels
-        ),
-        name="grads",
-    )(mine, theirs, reach, scale, results, key_gate, values, upstream)
+
+    def grads(name, is_own, edges, before):
+        operands = (edges, reach, scale, results, key_gate, values, upstream)
+        return pl.pallas_call(
+            functools.partial(grads_kernel, is_own),
+            out_shape=(grad,) * 3,
+            in_specs=[vmem] * len(operands) + [in_hbm] * len(before),
+            out_specs=(in_hbm,) * 3,
+            scratch_shapes=[pltpu.VMEM((rows, channels // 2), BF16)] * 3
+            + [pltpu.SemaphoreType.DMA((tiles // 4, 3))],
+            input_output_aliases={len(operands) + k: k for k in range(len(before))},
+            compiler_params=params,
+            cost_estimate=pl.CostEstimate(
+                flops=2 * work, transcendentals=0, bytes_accessed=10 * rows * channels
+            ),
+            name=name,
+        )(*operands, *before)
+
+    outputs = grads("grads_own", True, after(mine, duo), ())
+    theirs = after(theirs, *outputs)
+    outputs = grads("grads_other", False, theirs[: 2 * part], outputs)
     query_grad, key_grad, value_grad = outputs
     here = jnp.concatenate([modal + theirs[2 * part : 2 * part + modes], far], axis=0)
     there = after(flip(here, 1, "grp"), *outputs)
@@ -642,7 +659,7 @@
         "final",
         functools.partial(final_kernel, full),
         (shape(modes, total_filters),) * 2 + (shape(tiles, LANES),),
-        (log_rates_t, residues_t, back, theirs, here, there),
+        (factors, back, theirs, here, there),
     )
     return (
         query_grad,

time: 28.6 us -> 28.3 us (0.990)
  waiting for transfers between devices: 5.37 us -> 4.3 us
  Pallas kernels: 12.3 us -> 13.1 us
    ppermute x6, waiting for transfers between devices: 5.24 us -> 4.16 us  [flip(): lax.ppermute(x, axis, [(i, i ^ step) for i in range(lax.axis_size(axis))])]
    pallas_call x2 -> x3, Pallas kernels: 1.64 us -> 2.47 us  [the longest x2 2.22 us: grads(): pl.pallas_call(functools.partial(grads_kernel, is_own), out_shape=(grad,)...]
  transfers between devices with their start and end apart: 7 -> 7, of which waited for: 5 -> 5; matrix products, arithmetic and copies ran while one was open for 0% -> 0% of each run, Pallas kernels for 31% -> 34%
where the time goes in v6:
time: 28.3 us; the launch traced here: 28 us
  Pallas kernels  13.1 us (46%)
  starting transfers between devices  9.87 us (35%)
  waiting for transfers between devices  4.3 us (15%)
  between operations  0.71 us (3%)
    pallas_call x6, Pallas kernels, call(): pl.pallas_call(kernel, out_shape=out_shape, in_specs=[vmem] * len(operand...  8.48 us
    ppermute x6, starting transfers between devices, flip(): lax.ppermute(x, axis, [(i, i ^ step) for i in range(lax.axis_size(axis))])  8.38 us
    ppermute x6, waiting for transfers between devices, flip(): lax.ppermute(x, axis, [(i, i ^ step) for i in range(lax.axis_size(axis))])  4.16 us
    pallas_call x2, Pallas kernels, grads(): pl.pallas_call(functools.partial(grads_kernel, is_own), out_shape=(grad,)...  2.22 us
    pallas_call x1, Pallas kernels, local(): pl.pallas_call(functools.partial(states_kernel, full), out_shape=(shape(8...  2.12 us
    ppermute x1, starting transfers between devices, local(): lax.ppermute(duo, ('ctx', 'grp'), [(i, i ^ (groups + 2 if i & 1 else 2))...  1.49 us
  transfers between devices with their start and end apart: 7, of which 5 were waited for; matrix products, arithmetic and copies ran while one was open for 0% of the time, Pallas kernels for 34%

profile of v6, /device:TPU:0, one launch (start us, length us, event | category | flops | bytes accessed | tf_op | source)
XLA Modules:
  0.0 28.0 jit_solution(12388436678663847546)
XLA Ops:
  0.6 2.1 %states.1 = (f32[512,128]{1,0:T(8,128)S(1)}, f32[8,16,128]{2,1,0:T(8,128)S(1)}, f32[8,128,128]{2,1,0:T(8,128)S(1)}, f32[8,128,128]{2,1,0:T(8,128)S(1)}, f32[8,128]{1,0:T(8,128)S(1)}) custom-call(f32[16,256]{1,0:T(8,128)} %bitcast.6, bf16[128,1024]{1,0:T(8,128)(2,1)} %key.3, bf16[128,1024]{1,0:T(8,128)(2,1)} %values.3, bf16[128,1024]{1,0:T(8,128)(2,1)} %upstream.3, ...), custom_call_target="tpu_custom_call" | custom-call | tf_op jit(solution)/shard_map/states/pallas_call | solution.py:535
  2.8 3.0 %collective-permute-start = (f32[256,128]{1,0:T(8,128)S(1)}, f32[256,128]{1,0:T(8,128)S(1)}, u32[]{:S(2)}, u32[]{:S(2)}) collective-permute-start(f32[256,128]{1,0:T(8,128)S(1)} %constant_dynamic-slice_fusion), channel_id=1, source_target_pairs={{0,4},{4,0},{8,12},{12,8},{16,20},{20,16},{24,28},{28,24},{1,5},{5... | collective-permute-start | bytes 393224 | tf_op jit(solution)/shard_map/ppermute | solution.py:497
  5.8 4.0 %within.1 = (f32[24,128]{1,0:T(8,128)S(1)}, f32[8,2,16,8,128]{4,3,2,1,0:T(8,128)S(1)}, f32[8,2,16,8,128]{4,3,2,1,0:T(8,128)S(1)}) custom-call(f32[8,16,128]{2,1,0:T(8,128)S(1)} %get-tuple-element.59.rate_ref, f32[8,128,128]{2,1,0:T(8,128)S(1)} %get-tuple-element.45.mixed_ref, f32[8,128,128]{2,1,0:T(8,128)S(1)} %get-tuple-element.46.carried_ref, ...), custom_call_target="tpu_custom_call" | custom-call | flops 25165824 | bytes 6291456 | tf_op jit(solution)/shard_map/within/pallas_call | solution.py:523
  9.8 0.0 collective-permute-done.other_ref.partner_ref
  9.8 0.0 copy-start.4
  9.9 0.3 join.2
  10.1 1.6 %collective-permute-start.1 = (f32[280,128]{1,0:T(8,128)S(1)}, f32[280,128]{1,0:T(8,128)S(1)}, u32[]{:S(2)}, u32[]{:S(2)}) collective-permute-start(f32[280,128]{1,0:T(8,128)S(1)} %get-tuple-element.50.own_ref), channel_id=1, source_target_pairs={{0,8},{4,12},{8,0},{12,4},{16,24},{20,28},{24,16},{28,20},{1,9},{5... | collective-permute-start | bytes 430088 | tf_op jit(solution)/shard_map/ppermute | solution.py:497
  11.7 3.0 %block.1 = (f32[8,16,128]{2,1,0:T(8,128)S(1)}, f32[8,2,128,128]{3,2,1,0:T(8,128)S(1)}) custom-call(f32[16,256]{1,0:T(8,128)S(1)} %bitcast.7, f32[16,256]{1,0:T(8,128)S(1)} %bitcast.9, f32[8,128]{1,0:T(8,128)S(1)} %bitcast.11, f32[8,16,128]{2,1,0:T(8,128)S(1)} %get-tuple-element.59.rate_ref, f32[8,2,16,8,128]{4,3,2,1,0:T(8,128)S(1)} %get-tuple-element.52.dealt, ...), custom_call_target="tpu_custom_call" | custom-call | flops 16777216 | bytes 4194304 | tf_op jit(solution)/shard_map/block/pallas_call | solution.py:523
  14.8 0.6 %collective-permute-done.1.other_ref = f32[280,128]{1,0:T(8,128)S(1)} collective-permute-done((f32[280,128]{1,0:T(8,128)S(1)}, f32[280,128]{1,0:T(8,128)S(1)}, u32[]{:S(2)}, u32[]{:S(2)}) %collective-permute-start.1) | collective-permute-done | bytes 143392 | tf_op jit(solution)/shard_map/ppermute | solution.py:497
  15.4 0.3 join.3
  15.6 2.6 %collective-permute-start.2 = (f32[152,128]{1,0:T(8,128)S(1)}, f32[152,128]{1,0:T(8,128)S(1)}, u32[]{:S(2)}, u32[]{:S(2)}) collective-permute-start(f32[152,128]{1,0:T(8,128)S(1)} %get-tuple-element.58), channel_id=1, source_target_pairs={{0,16},{4,20},{8,24},{12,28},{16,0},{20,4},{24,8},{28,12},{1,17},{... | collective-permute-start | bytes 233480 | tf_op jit(solution)/shard_map/ppermute | solution.py:497
  18.2 0.3 reach.1
  18.5 2.5 %collective-permute-done.2.other_ref = f32[152,128]{1,0:T(8,128)S(1)} collective-permute-done((f32[152,128]{1,0:T(8,128)S(1)}, f32[152,128]{1,0:T(8,128)S(1)}, u32[]{:S(2)}, u32[]{:S(2)}) %collective-permute-start.2) | collective-permute-done | bytes 77856 | tf_op jit(solution)/shard_map/ppermute | solution.py:497
  20.9 0.3 last_join.1
  21.2 0.0 collective-permute-start.4
  21.2 1.1 %collective-permute-start.3 = (f32[152,128]{1,0:T(8,128)S(1)}, f32[152,128]{1,0:T(8,128)S(1)}, u32[]{:S(2)}, u32[]{:S(2)}) collective-permute-start(f32[152,128]{1,0:T(8,128)S(1)} %get-tuple-element.63.back), channel_id=1, source_target_pairs={{0,4},{4,0},{8,12},{12,8},{16,20},{20,16},{24,28},{28,24},{1,5},{5... | collective-permute-start | bytes 233480 | tf_op jit(solution)/shard_map/ppermute | solution.py:497
  22.3 0.0 collective-permute-done.4
  22.4 1.5 %collective-permute-start.5 = (f32[32,128]{1,0:T(8,128)S(1)}, f32[32,128]{1,0:T(8,128)S(1)}, u32[]{:S(2)}, u32[]{:S(2)}) collective-permute-start(f32[32,128]{1,0:T(8,128)S(1)} %constant_dynamic-update-slice_fusion), channel_id=1, source_target_pairs={{0,2},{1,7},{2,0},{3,5},{4,6},{5,3},{6,4},{7,1},{8,10},{9,15},{10,... | collective-permute-start | bytes 49160 | tf_op jit(solution)/shard_map/ppermute | solution.py:628
  23.9 1.1 %grads_own.1 = (bf16[128,1024]{1,0:T(8,128)(2,1)}, bf16[128,1024]{1,0:T(8,128)(2,1)}, bf16[128,1024]{1,0:T(8,128)(2,1)}) custom-call(f32[128,128]{1,0:T(8,128)S(1)} %get-tuple-element.66.edges, bf16[8,2,2,128,128]{4,3,2,1,0:T(8,128)(2,1)S(1)} %get-tuple-element.60.reach, f32[8,16,128]{2,1,0:T(8,128)S(1)} %get-tuple-element.67.scale_ref, ...), custom_call_target="tpu_custom_call" | custom-call | flops 4194304 | bytes 1310720 | tf_op jit(solution)/shard_map/grads_own/pallas_call | solution.py:637
  25.0 1.0 %collective-permute-done.3.theirs = f32[152,128]{1,0:T(8,128)S(1)} collective-permute-done((f32[152,128]{1,0:T(8,128)S(1)}, f32[152,128]{1,0:T(8,128)S(1)}, u32[]{:S(2)}, u32[]{:S(2)}) %collective-permute-start.3) | collective-permute-done | bytes 77856 | tf_op jit(solution)/shard_map/ppermute | solution.py:497
  26.0 0.1 collective-permute-done.5
  26.2 1.1 %grads_other.1 = (bf16[128,1024]{1,0:T(8,128)(2,1)}, bf16[128,1024]{1,0:T(8,128)(2,1)}, bf16[128,1024]{1,0:T(8,128)(2,1)}) custom-call(f32[128,128]{1,0:T(8,128)S(1)} %slice.6.edges, bf16[8,2,2,128,128]{4,3,2,1,0:T(8,128)(2,1)S(1)} %get-tuple-element.60.reach, ...), custom_call_target="tpu_custom_call", output_to_operand_aliasing={{0}: (7, {}), {1}: (8, {}), {2}: (9, {})} | custom-call | flops 4194304 | bytes 1310720 | tf_op jit(solution)/shard_map/grads_other/pallas_call | solution.py:637
  27.3 0.1 collective-permute-done.6.there
  27.3 0.7 %final.1 = (f32[16,256]{1,0:T(8,128)}, f32[16,256]{1,0:T(8,128)}, f32[8,128]{1,0:T(8,128)}) custom-call(f32[3,16,256]{2,1,0:T(8,128)S(1)} %get-tuple-element.75.factors, f32[152,128]{1,0:T(8,128)S(1)} %get-tuple-element.63.back, f32[152,128]{1,0:T(8,128)S(1)} %collective-permute-done.3.theirs, f32[48,128]{1,0:T(8,128)S(1)} %pad_maximum_fusion.here, ...), custom_call_target="tpu_custom_call" | custom-call | tf_op jit(solution)/shard_map/final/pallas_call | solution.py:523
  (18 shorter events, 0.1 us)
Async XLA Ops:
  2.8 7.0 %collective-permute-start = (f32[256,128]{1,0:T(8,128)S(1)}, f32[256,128]{1,0:T(8,128)S(1)}, u32[]{:S(2)}, u32[]{:S(2)}) collective-permute-start(f32[256,128]{1,0:T(8,128)S(1)} %constant_dynamic-slice_fusion), channel_id=1, source_target_pairs={{0,4},{4,0},{8,12},{12,8},{16,20},{20,16},{24,28},{28,24},{1,5},{5... | collective-permute-start | bytes 393224 | tf_op jit(solution)/shard_map/ppermute | solution.py:497
  9.8 1.9 %copy-start.3 = (f32[256,16]{0,1:T(8,128)S(1)}, f32[256,16]{0,1:T(8,128)}, u32[]{:S(2)}) copy-start(f32[256,16]{0,1:T(8,128)} %param.13) | copy-start | bytes 49156
  9.8 1.9 %copy-start.4 = (f32[256,16]{0,1:T(8,128)S(1)}, f32[256,16]{0,1:T(8,128)}, u32[]{:S(2)}) copy-start(f32[256,16]{0,1:T(8,128)} %param.12) | copy-start | bytes 49156
  10.1 1.6 %copy-start.5 = (f32[1024]{0:T(1024)S(1)}, f32[1024]{0:T(1024)}, u32[]{:S(2)}) copy-start(f32[1024]{0:T(1024)} %param.11) | copy-start | bytes 12292
  10.1 5.2 %collective-permute-start.1 = (f32[280,128]{1,0:T(8,128)S(1)}, f32[280,128]{1,0:T(8,128)S(1)}, u32[]{:S(2)}, u32[]{:S(2)}) collective-permute-start(f32[280,128]{1,0:T(8,128)S(1)} %get-tuple-element.50.own_ref), channel_id=1, source_target_pairs={{0,8},{4,12},{8,0},{12,4},{16,24},{20,28},{24,16},{28,20},{1,9},{5... | collective-permute-start | bytes 430088 | tf_op jit(solution)/shard_map/ppermute | solution.py:497
  15.6 5.3 %collective-permute-start.2 = (f32[152,128]{1,0:T(8,128)S(1)}, f32[152,128]{1,0:T(8,128)S(1)}, u32[]{:S(2)}, u32[]{:S(2)}) collective-permute-start(f32[152,128]{1,0:T(8,128)S(1)} %get-tuple-element.58), channel_id=1, source_target_pairs={{0,16},{4,20},{8,24},{12,28},{16,0},{20,4},{24,8},{28,12},{1,17},{... | collective-permute-start | bytes 233480 | tf_op jit(solution)/shard_map/ppermute | solution.py:497
  18.2 5.7 %copy-start.2 = (bf16[128,1024]{1,0:T(8,128)(2,1)S(1)}, bf16[128,1024]{1,0:T(8,128)(2,1)}, u32[]{:S(2)}) copy-start(bf16[128,1024]{1,0:T(8,128)(2,1)} %upstream.3) | copy-start | bytes 786436
  20.9 3.0 %copy-start = (bf16[128,1024]{1,0:T(8,128)(2,1)S(1)}, bf16[128,1024]{1,0:T(8,128)(2,1)}, u32[]{:S(2)}) copy-start(bf16[128,1024]{1,0:T(8,128)(2,1)} %key.3) | copy-start | bytes 786436
  20.9 3.0 %copy-start.1 = (bf16[128,1024]{1,0:T(8,128)(2,1)S(1)}, bf16[128,1024]{1,0:T(8,128)(2,1)}, u32[]{:S(2)}) copy-start(bf16[128,1024]{1,0:T(8,128)(2,1)} %values.3) | copy-start | bytes 786436
  21.2 1.2 %collective-permute-start.4 = (f32[16,128]{1,0:T(8,128)S(1)}, f32[16,128]{1,0:T(8,128)S(1)}, u32[]{:S(2)}, u32[]{:S(2)}) collective-permute-start(f32[16,128]{1,0:T(8,128)S(1)} %get-tuple-element.65), channel_id=1, source_target_pairs={{0,1},{1,0},{2,3},{3,2},{4,5},{5,4},{6,7},{7,6},{8,9},{9,8},{10,11... | collective-permute-start | bytes 24584 | tf_op jit(solution)/shard_map/ppermute | solution.py:497
  21.2 4.8 %collective-permute-start.3 = (f32[152,128]{1,0:T(8,128)S(1)}, f32[152,128]{1,0:T(8,128)S(1)}, u32[]{:S(2)}, u32[]{:S(2)}) collective-permute-start(f32[152,128]{1,0:T(8,128)S(1)} %get-tuple-element.63.back), channel_id=1, source_target_pairs={{0,4},{4,0},{8,12},{12,8},{16,20},{20,16},{24,28},{28,24},{1,5},{5... | collective-permute-start | bytes 233480 | tf_op jit(solution)/shard_map/ppermute | solution.py:497
  22.4 3.7 %collective-permute-start.5 = (f32[32,128]{1,0:T(8,128)S(1)}, f32[32,128]{1,0:T(8,128)S(1)}, u32[]{:S(2)}, u32[]{:S(2)}) collective-permute-start(f32[32,128]{1,0:T(8,128)S(1)} %constant_dynamic-update-slice_fusion), channel_id=1, source_target_pairs={{0,2},{1,7},{2,0},{3,5},{4,6},{5,3},{6,4},{7,1},{8,10},{9,15},{10,... | collective-permute-start | bytes 49160 | tf_op jit(solution)/shard_map/ppermute | solution.py:628
  26.1 1.2 %collective-permute-start.6 = (f32[48,128]{1,0:T(8,128)S(1)}, f32[48,128]{1,0:T(8,128)S(1)}, u32[]{:S(2)}, u32[]{:S(2)}) collective-permute-start(f32[48,128]{1,0:T(8,128)S(1)} %pad_maximum_fusion.here), channel_id=1, source_target_pairs={{0,1},{1,0},{2,3},{3,2},{4,5},{5,4},{6,7},{7,6},{8,9},{9,8},{10,11... | collective-permute-start | bytes 73736 | tf_op jit(solution)/shard_map/ppermute | solution.py:497

commit v7 on v6

--- a/solution.py
+++ b/solution.py
@@ -11,7 +11,6 @@
 LANES = 128
 SUB = 8
 TILE_FILTERS = LANES // GROUP_CH
-HIGHEST = lax.Precision.HIGHEST
 F32 = jnp.float32
 BF16 = jnp.bfloat16
 
@@ -29,7 +28,13 @@
 
 
 def per_channel(table, mask):
-    return jnp.dot(table, mask, precision=HIGHEST, preferred_element_type=F32)
+    modes = table.shape[0]
+    high, _ = split(table)
+    middle, low = split(table - high.astype(F32))
+    terms = jnp.dot(
+        jnp.concatenate([high, middle, low], axis=0), mask.astype(BF16), preferred_element_type=F32
+    )
+    return terms[:modes] + (terms[modes : 2 * modes] + terms[2 * modes :])
 
 
 def split(x):

time: 28.3 us -> 28.3 us (level)
  no operation moved by 1% of the time
where the time goes in v7:
time: 28.3 us; the launch traced here: 28 us
  Pallas kernels  13 us (46%)
  starting transfers between devices  9.87 us (35%)
  waiting for transfers between devices  4.36 us (15%)
  between operations  0.71 us (3%)
    pallas_call x6, Pallas kernels, call(): pl.pallas_call(kernel, out_shape=out_shape, in_specs=[vmem] * len(operand...  8.41 us
    ppermute x6, starting transfers between devices, flip(): lax.ppermute(x, axis, [(i, i ^ step) for i in range(lax.axis_size(axis))])  8.37 us
    ppermute x6, waiting for transfers between devices, flip(): lax.ppermute(x, axis, [(i, i ^ step) for i in range(lax.axis_size(axis))])  4.22 us
    pallas_call x2, Pallas kernels, grads(): pl.pallas_call(functools.partial(grads_kernel, is_own), out_shape=(grad,)...  2.21 us
    pallas_call x1, Pallas kernels, local(): pl.pallas_call(functools.partial(states_kernel, full), out_shape=(shape(8...  2.11 us
    ppermute x1, starting transfers between devices, local(): lax.ppermute(duo, ('ctx', 'grp'), [(i, i ^ (groups + 2 if i & 1 else 2))...  1.5 us
  transfers between devices with their start and end apart: 7, of which 5 were waited for; matrix products, arithmetic and copies ran while one was open for 0% of the time, Pallas kernels for 34%

profile of v7, /device:TPU:0, one launch (start us, length us, event | category | flops | bytes accessed | tf_op | source)
XLA Modules:
  0.0 28.0 jit_solution(12693533669444741490)
XLA Ops:
  0.6 2.1 %states.1 = (f32[512,128]{1,0:T(8,128)S(1)}, f32[8,16,128]{2,1,0:T(8,128)S(1)}, f32[8,128,128]{2,1,0:T(8,128)S(1)}, f32[8,128,128]{2,1,0:T(8,128)S(1)}, f32[8,128]{1,0:T(8,128)S(1)}) custom-call(f32[16,256]{1,0:T(8,128)} %bitcast.6, bf16[128,1024]{1,0:T(8,128)(2,1)} %key.3, bf16[128,1024]{1,0:T(8,128)(2,1)} %values.3, bf16[128,1024]{1,0:T(8,128)(2,1)} %upstream.3, ...), custom_call_target="tpu_custom_call" | custom-call | tf_op jit(solution)/shard_map/states/pallas_call | solution.py:540
  2.8 3.0 %collective-permute-start = (f32[256,128]{1,0:T(8,128)S(1)}, f32[256,128]{1,0:T(8,128)S(1)}, u32[]{:S(2)}, u32[]{:S(2)}) collective-permute-start(f32[256,128]{1,0:T(8,128)S(1)} %constant_dynamic-slice_fusion), channel_id=1, source_target_pairs={{0,4},{4,0},{8,12},{12,8},{16,20},{20,16},{24,28},{28,24},{1,5},{5... | collective-permute-start | bytes 393224 | tf_op jit(solution)/shard_map/ppermute | solution.py:502
  5.8 4.0 %within.1 = (f32[24,128]{1,0:T(8,128)S(1)}, f32[8,2,16,8,128]{4,3,2,1,0:T(8,128)S(1)}, f32[8,2,16,8,128]{4,3,2,1,0:T(8,128)S(1)}) custom-call(f32[8,16,128]{2,1,0:T(8,128)S(1)} %get-tuple-element.59.rate_ref, f32[8,128,128]{2,1,0:T(8,128)S(1)} %get-tuple-element.45.mixed_ref, f32[8,128,128]{2,1,0:T(8,128)S(1)} %get-tuple-element.46.carried_ref, ...), custom_call_target="tpu_custom_call" | custom-call | flops 25165824 | bytes 6291456 | tf_op jit(solution)/shard_map/within/pallas_call | solution.py:528
  9.8 0.0 copy-start.4
  9.9 0.2 join.2
  10.1 1.6 %collective-permute-start.1 = (f32[280,128]{1,0:T(8,128)S(1)}, f32[280,128]{1,0:T(8,128)S(1)}, u32[]{:S(2)}, u32[]{:S(2)}) collective-permute-start(f32[280,128]{1,0:T(8,128)S(1)} %get-tuple-element.50.own_ref), channel_id=1, source_target_pairs={{0,8},{4,12},{8,0},{12,4},{16,24},{20,28},{24,16},{28,20},{1,9},{5... | collective-permute-start | bytes 430088 | tf_op jit(solution)/shard_map/ppermute | solution.py:502
  11.7 3.0 %block.1 = (f32[8,16,128]{2,1,0:T(8,128)S(1)}, f32[8,2,128,128]{3,2,1,0:T(8,128)S(1)}) custom-call(f32[16,256]{1,0:T(8,128)S(1)} %bitcast.7, f32[16,256]{1,0:T(8,128)S(1)} %bitcast.9, f32[8,128]{1,0:T(8,128)S(1)} %bitcast.11, f32[8,16,128]{2,1,0:T(8,128)S(1)} %get-tuple-element.59.rate_ref, f32[8,2,16,8,128]{4,3,2,1,0:T(8,128)S(1)} %get-tuple-element.52.dealt, ...), custom_call_target="tpu_custom_call" | custom-call | flops 16777216 | bytes 4194304 | tf_op jit(solution)/shard_map/block/pallas_call | solution.py:528
  14.7 0.7 %collective-permute-done.1.other_ref = f32[280,128]{1,0:T(8,128)S(1)} collective-permute-done((f32[280,128]{1,0:T(8,128)S(1)}, f32[280,128]{1,0:T(8,128)S(1)}, u32[]{:S(2)}, u32[]{:S(2)}) %collective-permute-start.1) | collective-permute-done | bytes 143392 | tf_op jit(solution)/shard_map/ppermute | solution.py:502
  15.3 0.3 join.3
  15.6 2.6 %collective-permute-start.2 = (f32[152,128]{1,0:T(8,128)S(1)}, f32[152,128]{1,0:T(8,128)S(1)}, u32[]{:S(2)}, u32[]{:S(2)}) collective-permute-start(f32[152,128]{1,0:T(8,128)S(1)} %get-tuple-element.58), channel_id=1, source_target_pairs={{0,16},{4,20},{8,24},{12,28},{16,0},{20,4},{24,8},{28,12},{1,17},{... | collective-permute-start | bytes 233480 | tf_op jit(solution)/shard_map/ppermute | solution.py:502
  18.2 0.3 reach.1
  18.5 2.5 %collective-permute-done.2.other_ref = f32[152,128]{1,0:T(8,128)S(1)} collective-permute-done((f32[152,128]{1,0:T(8,128)S(1)}, f32[152,128]{1,0:T(8,128)S(1)}, u32[]{:S(2)}, u32[]{:S(2)}) %collective-permute-start.2) | collective-permute-done | bytes 77856 | tf_op jit(solution)/shard_map/ppermute | solution.py:502
  20.9 0.3 last_join.1
  21.2 0.0 collective-permute-start.4
  21.2 1.1 %collective-permute-start.3 = (f32[152,128]{1,0:T(8,128)S(1)}, f32[152,128]{1,0:T(8,128)S(1)}, u32[]{:S(2)}, u32[]{:S(2)}) collective-permute-start(f32[152,128]{1,0:T(8,128)S(1)} %get-tuple-element.63.back), channel_id=1, source_target_pairs={{0,4},{4,0},{8,12},{12,8},{16,20},{20,16},{24,28},{28,24},{1,5},{5... | collective-permute-start | bytes 233480 | tf_op jit(solution)/shard_map/ppermute | solution.py:502
  22.3 0.0 collective-permute-done.4
  22.4 1.5 %collective-permute-start.5 = (f32[32,128]{1,0:T(8,128)S(1)}, f32[32,128]{1,0:T(8,128)S(1)}, u32[]{:S(2)}, u32[]{:S(2)}) collective-permute-start(f32[32,128]{1,0:T(8,128)S(1)} %constant_dynamic-update-slice_fusion), channel_id=1, source_target_pairs={{0,2},{1,7},{2,0},{3,5},{4,6},{5,3},{6,4},{7,1},{8,10},{9,15},{10,... | collective-permute-start | bytes 49160 | tf_op jit(solution)/shard_map/ppermute | solution.py:633
  23.9 1.1 %grads_own.1 = (bf16[128,1024]{1,0:T(8,128)(2,1)}, bf16[128,1024]{1,0:T(8,128)(2,1)}, bf16[128,1024]{1,0:T(8,128)(2,1)}) custom-call(f32[128,128]{1,0:T(8,128)S(1)} %get-tuple-element.66.edges, bf16[8,2,2,128,128]{4,3,2,1,0:T(8,128)(2,1)S(1)} %get-tuple-element.60.reach, f32[8,16,128]{2,1,0:T(8,128)S(1)} %get-tuple-element.67.scale_ref, ...), custom_call_target="tpu_custom_call" | custom-call | flops 4194304 | bytes 1310720 | tf_op jit(solution)/shard_map/grads_own/pallas_call | solution.py:642
  25.0 1.0 %collective-permute-done.3.theirs = f32[152,128]{1,0:T(8,128)S(1)} collective-permute-done((f32[152,128]{1,0:T(8,128)S(1)}, f32[152,128]{1,0:T(8,128)S(1)}, u32[]{:S(2)}, u32[]{:S(2)}) %collective-permute-start.3) | collective-permute-done | bytes 77856 | tf_op jit(solution)/shard_map/ppermute | solution.py:502
  26.0 0.1 collective-permute-done.5
  26.1 0.0 collective-permute-start.6
  26.1 1.1 %grads_other.1 = (bf16[128,1024]{1,0:T(8,128)(2,1)}, bf16[128,1024]{1,0:T(8,128)(2,1)}, bf16[128,1024]{1,0:T(8,128)(2,1)}) custom-call(f32[128,128]{1,0:T(8,128)S(1)} %slice.6.edges, bf16[8,2,2,128,128]{4,3,2,1,0:T(8,128)(2,1)S(1)} %get-tuple-element.60.reach, ...), custom_call_target="tpu_custom_call", output_to_operand_aliasing={{0}: (7, {}), {1}: (8, {}), {2}: (9, {})} | custom-call | flops 4194304 | bytes 1310720 | tf_op jit(solution)/shard_map/grads_other/pallas_call | solution.py:642
  27.3 0.1 collective-permute-done.6.there
  27.3 0.7 %final.1 = (f32[16,256]{1,0:T(8,128)}, f32[16,256]{1,0:T(8,128)}, f32[8,128]{1,0:T(8,128)}) custom-call(f32[3,16,256]{2,1,0:T(8,128)S(1)} %get-tuple-element.75.factors, f32[152,128]{1,0:T(8,128)S(1)} %get-tuple-element.63.back, f32[152,128]{1,0:T(8,128)S(1)} %collective-permute-done.3.theirs, f32[48,128]{1,0:T(8,128)S(1)} %pad_maximum_fusion.here, ...), custom_call_target="tpu_custom_call" | custom-call | tf_op jit(solution)/shard_map/final/pallas_call | solution.py:528
  (18 shorter events, 0.1 us)
Async XLA Ops:
  2.8 7.0 %collective-permute-start = (f32[256,128]{1,0:T(8,128)S(1)}, f32[256,128]{1,0:T(8,128)S(1)}, u32[]{:S(2)}, u32[]{:S(2)}) collective-permute-start(f32[256,128]{1,0:T(8,128)S(1)} %constant_dynamic-slice_fusion), channel_id=1, source_target_pairs={{0,4},{4,0},{8,12},{12,8},{16,20},{20,16},{24,28},{28,24},{1,5},{5... | collective-permute-start | bytes 393224 | tf_op jit(solution)/shard_map/ppermute | solution.py:502
  9.8 1.9 %copy-start.3 = (f32[256,16]{0,1:T(8,128)S(1)}, f32[256,16]{0,1:T(8,128)}, u32[]{:S(2)}) copy-start(f32[256,16]{0,1:T(8,128)} %param.13) | copy-start | bytes 49156
  9.8 1.9 %copy-start.4 = (f32[256,16]{0,1:T(8,128)S(1)}, f32[256,16]{0,1:T(8,128)}, u32[]{:S(2)}) copy-start(f32[256,16]{0,1:T(8,128)} %param.12) | copy-start | bytes 49156
  10.1 1.6 %copy-start.5 = (f32[1024]{0:T(1024)S(1)}, f32[1024]{0:T(1024)}, u32[]{:S(2)}) copy-start(f32[1024]{0:T(1024)} %param.11) | copy-start | bytes 12292
  10.1 5.2 %collective-permute-start.1 = (f32[280,128]{1,0:T(8,128)S(1)}, f32[280,128]{1,0:T(8,128)S(1)}, u32[]{:S(2)}, u32[]{:S(2)}) collective-permute-start(f32[280,128]{1,0:T(8,128)S(1)} %get-tuple-element.50.own_ref), channel_id=1, source_target_pairs={{0,8},{4,12},{8,0},{12,4},{16,24},{20,28},{24,16},{28,20},{1,9},{5... | collective-permute-start | bytes 430088 | tf_op jit(solution)/shard_map/ppermute | solution.py:502
  15.6 5.3 %collective-permute-start.2 = (f32[152,128]{1,0:T(8,128)S(1)}, f32[152,128]{1,0:T(8,128)S(1)}, u32[]{:S(2)}, u32[]{:S(2)}) collective-permute-start(f32[152,128]{1,0:T(8,128)S(1)} %get-tuple-element.58), channel_id=1, source_target_pairs={{0,16},{4,20},{8,24},{12,28},{16,0},{20,4},{24,8},{28,12},{1,17},{... | collective-permute-start | bytes 233480 | tf_op jit(solution)/shard_map/ppermute | solution.py:502
  18.2 5.7 %copy-start.2 = (bf16[128,1024]{1,0:T(8,128)(2,1)S(1)}, bf16[128,1024]{1,0:T(8,128)(2,1)}, u32[]{:S(2)}) copy-start(bf16[128,1024]{1,0:T(8,128)(2,1)} %upstream.3) | copy-start | bytes 786436
  20.9 3.0 %copy-start = (bf16[128,1024]{1,0:T(8,128)(2,1)S(1)}, bf16[128,1024]{1,0:T(8,128)(2,1)}, u32[]{:S(2)}) copy-start(bf16[128,1024]{1,0:T(8,128)(2,1)} %key.3) | copy-start | bytes 786436
  20.9 3.0 %copy-start.1 = (bf16[128,1024]{1,0:T(8,128)(2,1)S(1)}, bf16[128,1024]{1,0:T(8,128)(2,1)}, u32[]{:S(2)}) copy-start(bf16[128,1024]{1,0:T(8,128)(2,1)} %values.3) | copy-start | bytes 786436
  21.2 1.2 %collective-permute-start.4 = (f32[16,128]{1,0:T(8,128)S(1)}, f32[16,128]{1,0:T(8,128)S(1)}, u32[]{:S(2)}, u32[]{:S(2)}) collective-permute-start(f32[16,128]{1,0:T(8,128)S(1)} %get-tuple-element.65), channel_id=1, source_target_pairs={{0,1},{1,0},{2,3},{3,2},{4,5},{5,4},{6,7},{7,6},{8,9},{9,8},{10,11... | collective-permute-start | bytes 24584 | tf_op jit(solution)/shard_map/ppermute | solution.py:502
  21.2 4.8 %collective-permute-start.3 = (f32[152,128]{1,0:T(8,128)S(1)}, f32[152,128]{1,0:T(8,128)S(1)}, u32[]{:S(2)}, u32[]{:S(2)}) collective-permute-start(f32[152,128]{1,0:T(8,128)S(1)} %get-tuple-element.63.back), channel_id=1, source_target_pairs={{0,4},{4,0},{8,12},{12,8},{16,20},{20,16},{24,28},{28,24},{1,5},{5... | collective-permute-start | bytes 233480 | tf_op jit(solution)/shard_map/ppermute | solution.py:502
  22.4 3.7 %collective-permute-start.5 = (f32[32,128]{1,0:T(8,128)S(1)}, f32[32,128]{1,0:T(8,128)S(1)}, u32[]{:S(2)}, u32[]{:S(2)}) collective-permute-start(f32[32,128]{1,0:T(8,128)S(1)} %constant_dynamic-update-slice_fusion), channel_id=1, source_target_pairs={{0,2},{1,7},{2,0},{3,5},{4,6},{5,3},{6,4},{7,1},{8,10},{9,15},{10,... | collective-permute-start | bytes 49160 | tf_op jit(solution)/shard_map/ppermute | solution.py:633
  26.1 1.2 %collective-permute-start.6 = (f32[48,128]{1,0:T(8,128)S(1)}, f32[48,128]{1,0:T(8,128)S(1)}, u32[]{:S(2)}, u32[]{:S(2)}) collective-permute-start(f32[48,128]{1,0:T(8,128)S(1)} %pad_maximum_fusion.here), channel_id=1, source_target_pairs={{0,1},{1,0},{2,3},{3,2},{4,5},{5,4},{6,7},{7,6},{8,9},{9,8},{10,11... | collective-permute-start | bytes 73736 | tf_op jit(solution)/shard_map/ppermute | solution.py:502
